TPU v7x, 32 devices: a whole 2x2x4 slice. The times are simulated.
32 devices in a mesh: fsdp: 2 (over core), context: 4 (over y, x), tensor: 4 (over z).
Axes of the slice: x: 2, y: 2, z: 4, core: 2. Of those that a mesh axis runs over, the one named last changes fastest.
Arguments:
- inputs: bfloat16 [2, 2, 4096, 768], P(None, 'fsdp', 'context'), may hold values from -6 to 6
- cotangent: bfloat16 [2, 2, 4096, 768], P(None, 'fsdp', 'context'), may hold values from -6 to 6
- picture_starts: int32 [2, 2, 4], P(None, 'fsdp'), may hold values from 0 to 3840, as said below
- qkv_weight: bfloat16 [3, 768, 768], P(None, 'fsdp', 'tensor'), may hold values from -0.21875 to 0.21875
- out_weight: bfloat16 [768, 768], P('tensor', 'fsdp'), may hold values from -1.75 to 1.75
- up_weight: bfloat16 [768, 3072], P('fsdp', 'tensor'), may hold values from -0.21875 to 0.21875
- down_weight: bfloat16 [3072, 768], P('tensor', 'fsdp'), may hold values from -0.109375 to 0.109375
- query_map: bfloat16 [12, 64, 64], P('tensor', 'fsdp'), may hold values from -1.5 to 1.5
- key_map: bfloat16 [12, 64, 64], P('tensor', 'fsdp'), may hold values from -1.5 to 1.5
- first_gain: bfloat16 [768], P('fsdp'), may hold values from 0.5 to 1.5
- first_bias: bfloat16 [768], P('fsdp'), may hold values from -3 to 3
- second_gain: bfloat16 [768], P('fsdp'), may hold values from 0.5 to 1.5
- second_bias: bfloat16 [768], P('fsdp'), may hold values from -3 to 3
Outputs:
- output: bfloat16 [2, 2, 4096, 768], P(None, 'fsdp', 'context')
- input_grad: float32 [2, 2, 4096, 768], P(None, 'fsdp', 'context')
- qkv_grad: float32 [3, 768, 768], P(None, 'fsdp', 'tensor')
- out_grad: float32 [768, 768], P('tensor', 'fsdp')
- up_grad: float32 [768, 3072], P('fsdp', 'tensor')
- down_grad: float32 [3072, 768], P('tensor', 'fsdp')
- query_map_grad: float32 [12, 64, 64], P('tensor', 'fsdp')
- key_map_grad: float32 [12, 64, 64], P('tensor', 'fsdp')
- first_gain_grad: float32 [768], P('fsdp')
- first_bias_grad: float32 [768], P('fsdp')
- second_gain_grad: float32 [768], P('fsdp')
- second_bias_grad: float32 [768], P('fsdp')
Inputs may be any that keep to these rules, and one draw needn't show every extreme that they name: `picture_starts`: the 4 starts of a sequence are distinct multiples of 256.
All inputs are finite; a program needn't handle non-finite values.
Results may differ from a plain program's by a relative error of at most 0.025.
Values may be sent and summed in bfloat16 or wider, within the bound.
A program may use at most 192 MiB of HBM per device.

v0:
```python
import jax
import jax.numpy as jnp
from jax import lax
from jax.sharding import PartitionSpec as P

BLK = 256
MICRO = 2


epsilon = 1e-05
highest = lax.Precision.HIGHEST


def carried_in(value, axis, join, neutral, backward):
    count, mine = (lax.axis_size(axis), lax.axis_index(axis))
    pieces = jax.tree.map(lambda part: lax.all_gather(part, axis), value)
    if backward:
        pieces = jax.tree.map(lambda part: part[::-1], pieces)
        mine = count - 1 - mine
    total = jax.tree.map(
        lambda part, zero: jnp.full_like(part, 0) + jnp.asarray(zero, part.dtype), value, neutral
    )

    def hop(position, total):
        longer = join(total, jax.tree.map(lambda part: part[position], pieces))
        return jax.tree.map(lambda new, old: jnp.where(position < mine, new, old), longer, total)

    return lax.fori_loop(0, count - 1, hop, total)


def layer_norm(values, norm_gain, norm_bias):
    center = values - jnp.mean(values, -1, keepdims=True)
    spread = jnp.mean(center * center, -1, keepdims=True)
    return center * lax.rsqrt(spread + epsilon) * norm_gain + norm_bias


def features(logits):
    return jnp.concatenate([jax.nn.softmax(logits, -1), jax.nn.softmax(-logits, -1)], -1)


def gelu_tanh(values):
    return jax.nn.gelu(values, approximate=True)


def add_pair(earlier, latter):
    return (earlier[0] + latter[0], earlier[1] + latter[1])


def prefix_before(values):
    running = jnp.cumsum(values, 1)
    return jnp.concatenate([jnp.zeros_like(values[:, :1]), running[:, :-1]], 1)


def suffix_after(values):
    running = jnp.flip(jnp.cumsum(jnp.flip(values, 1), 1), 1)
    return jnp.concatenate([running[:, 1:], jnp.zeros_like(values[:, :1])], 1)


def fetch_weights(
    qkv_weight,
    out_weight,
    up_weight,
    down_weight,
    query_map,
    key_map,
    first_gain,
    first_bias,
    second_gain,
    second_bias,
):
    return (
        lax.all_gather(qkv_weight, "fsdp", axis=1, tiled=True),
        lax.all_gather(out_weight, "fsdp", axis=1, tiled=True),
        lax.all_gather(up_weight, "fsdp", axis=0, tiled=True),
        lax.all_gather(down_weight, "fsdp", axis=1, tiled=True),
        lax.all_gather(query_map, "fsdp", axis=1, tiled=True),
        lax.all_gather(key_map, "fsdp", axis=1, tiled=True),
        lax.all_gather(first_gain, "fsdp", axis=0, tiled=True),
        lax.all_gather(first_bias, "fsdp", axis=0, tiled=True),
        lax.all_gather(second_gain, "fsdp", axis=0, tiled=True),
        lax.all_gather(second_bias, "fsdp", axis=0, tiled=True),
    )


def reduce_grads(grad_list):
    shares = (
        lax.psum_scatter(grad_list[0], "fsdp", scatter_dimension=1, tiled=True),
        lax.psum_scatter(grad_list[1], "fsdp", scatter_dimension=1, tiled=True),
        lax.psum_scatter(grad_list[2], "fsdp", scatter_dimension=0, tiled=True),
        lax.psum_scatter(grad_list[3], "fsdp", scatter_dimension=1, tiled=True),
        lax.psum_scatter(grad_list[4], "fsdp", scatter_dimension=1, tiled=True),
        lax.psum_scatter(grad_list[5], "fsdp", scatter_dimension=1, tiled=True),
        lax.psum_scatter(grad_list[6], "fsdp", scatter_dimension=0, tiled=True),
        lax.psum_scatter(grad_list[7], "fsdp", scatter_dimension=0, tiled=True),
        lax.psum_scatter(grad_list[8], "fsdp", scatter_dimension=0, tiled=True),
        lax.psum_scatter(grad_list[9], "fsdp", scatter_dimension=0, tiled=True),
    )
    return lax.psum(
        (
            shares[0],
            shares[1],
            shares[2],
            shares[3],
            shares[4],
            shares[5],
            shares[6],
            shares[7],
            shares[8],
            shares[9],
        ),
        "context",
    )


def per_device(
    inputs,
    cotangent,
    picture_starts,
    qkv_weight,
    out_weight,
    up_weight,
    down_weight,
    query_map,
    key_map,
    first_gain,
    first_bias,
    second_gain,
    second_bias,
):
    seq_local = inputs.shape[1]
    seq_len = inputs.shape[2]
    model_width = inputs.shape[3]
    row_count = seq_local * seq_len
    head_size = query_map.shape[2]
    feat_size = 2 * head_size
    blocks_local = seq_len // BLK
    block_total = seq_local * blocks_local
    context_pos = lax.axis_index("context")
    block_ids = context_pos * blocks_local + jnp.arange(blocks_local, dtype=jnp.int32)
    position = jnp.arange(BLK, dtype=jnp.int32)
    causal = position[None, :] <= position[:, None]

    def gather_all():
        return fetch_weights(
            qkv_weight,
            out_weight,
            up_weight,
            down_weight,
            query_map,
            key_map,
            first_gain,
            first_bias,
            second_gain,
            second_bias,
        )

    totals = None
    outputs = []
    in_grads = []
    for batch_index in range(MICRO):
        params = gather_all()
        in_full = params[0]
        out_full = params[1]
        up_full = params[2]
        down_full = params[3]
        qmap_full = params[4]
        kmap_full = params[5]
        gain_first = params[6].astype(jnp.float32)
        bias_first = params[7].astype(jnp.float32)
        gain_second = params[8].astype(jnp.float32)
        bias_second = params[9].astype(jnp.float32)
        source = inputs[batch_index].reshape(row_count, model_width).astype(jnp.float32)
        starts_here = picture_starts[batch_index]
        block_flags = (
            jnp.sum(
                (starts_here[:, :, None] // BLK == block_ids[None, None, :]).astype(jnp.int32), 1
            )
            > 0
        )
        allowed = causal[None, None] | block_flags[:, :, None, None]
        allowed = allowed.reshape(block_total, 1, BLK, BLK)
        normed_one = layer_norm(source, gain_first, bias_first)
        normed_low = normed_one.astype(jnp.bfloat16)
        projected = jnp.einsum(
            "rd,cde->cre", normed_low, in_full, preferred_element_type=jnp.float32
        ).astype(jnp.bfloat16)
        heads_local = projected.shape[2] // head_size
        queries = projected[0].reshape(row_count, heads_local, head_size)
        key_rows = projected[1].reshape(row_count, heads_local, head_size)
        value_rows = projected[2].reshape(row_count, heads_local, head_size)
        query_logits = jnp.einsum(
            "rhi,hij->rhj", queries, qmap_full, preferred_element_type=jnp.float32
        )
        key_logits = jnp.einsum(
            "rhi,hij->rhj", key_rows, kmap_full, preferred_element_type=jnp.float32
        )
        query_blocks = (
            features(query_logits)
            .astype(jnp.bfloat16)
            .reshape(block_total, BLK, heads_local, feat_size)
        )
        key_blocks = (
            features(key_logits)
            .astype(jnp.bfloat16)
            .reshape(block_total, BLK, heads_local, feat_size)
        )
        value_blocks = value_rows.reshape(block_total, BLK, heads_local, head_size)
        scores = jnp.einsum(
            "nthf,nshf->nhts", query_blocks, key_blocks, preferred_element_type=jnp.float32
        )
        weights_low = jnp.where(allowed, scores, 0.0).astype(jnp.bfloat16)
        states = jnp.einsum(
            "nshf,nshe->nhfe", key_blocks, value_blocks, preferred_element_type=jnp.float32
        )
        states = states.reshape(seq_local, blocks_local, heads_local, feat_size, head_size)
        key_sums = jnp.sum(key_blocks.astype(jnp.float32), 1).reshape(
            seq_local, blocks_local, heads_local, feat_size
        )
        state_total = jnp.sum(states, 1)
        sums_total = jnp.sum(key_sums, 1)
        carried, carried_sums = carried_in(
            (state_total, sums_total),
            "context",
            add_pair,
            (jnp.zeros_like(state_total), jnp.zeros_like(sums_total)),
            False,
        )
        prior_states = (carried[:, None] + prefix_before(states)).astype(jnp.bfloat16)
        prior_states = prior_states.reshape(block_total, heads_local, feat_size, head_size)
        prior_sums = (carried_sums[:, None] + prefix_before(key_sums)).reshape(
            block_total, heads_local, feat_size
        )
        numerator = jnp.einsum(
            "nhts,nshe->nthe", weights_low, value_blocks, preferred_element_type=jnp.float32
        )
        numerator = numerator + jnp.einsum(
            "nthf,nhfe->nthe", query_blocks, prior_states, preferred_element_type=jnp.float32
        )
        denominator = jnp.sum(weights_low.astype(jnp.float32), -1).transpose(0, 2, 1)
        denominator = denominator + jnp.einsum(
            "nthf,nhf->nth", query_blocks.astype(jnp.float32), prior_sums, precision=highest
        )
        mixed_heads = (
            (numerator / denominator[..., None])
            .astype(jnp.bfloat16)
            .reshape(row_count, heads_local * head_size)
        )
        attended = lax.psum(
            jnp.dot(mixed_heads, out_full, preferred_element_type=jnp.float32).astype(jnp.bfloat16),
            "tensor",
        ).astype(jnp.float32)
        middle = source + attended
        normed_two = layer_norm(middle, gain_second, bias_second)
        normed_two_low = normed_two.astype(jnp.bfloat16)
        hidden_pre = jnp.dot(normed_two_low, up_full, preferred_element_type=jnp.float32)
        hidden_low = gelu_tanh(hidden_pre).astype(jnp.bfloat16)
        branch = lax.psum(
            jnp.dot(hidden_low, down_full, preferred_element_type=jnp.float32).astype(jnp.bfloat16),
            "tensor",
        ).astype(jnp.float32)
        outputs.append(
            (middle + branch).astype(jnp.bfloat16).reshape(seq_local, seq_len, model_width)
        )
        params = gather_all()
        in_full = params[0]
        out_full = params[1]
        up_full = params[2]
        down_full = params[3]
        qmap_full = params[4]
        kmap_full = params[5]
        gain_first = params[6].astype(jnp.float32)
        bias_first = params[7].astype(jnp.float32)
        gain_second = params[8].astype(jnp.float32)
        bias_second = params[9].astype(jnp.float32)
        upstream_low = cotangent[batch_index].reshape(row_count, model_width)
        upstream = upstream_low.astype(jnp.float32)
        grad_down = jnp.einsum(
            "rk,rd->kd", hidden_low, upstream_low, preferred_element_type=jnp.float32
        )
        hidden_grad = jnp.einsum(
            "rd,kd->rk", upstream_low, down_full, preferred_element_type=jnp.float32
        )
        gelu_result, gelu_pull = jax.vjp(gelu_tanh, hidden_pre)
        pre_grad = gelu_pull(hidden_grad)[0].astype(jnp.bfloat16)
        grad_up = jnp.einsum(
            "rd,rf->df", normed_two_low, pre_grad, preferred_element_type=jnp.float32
        )
        normed_two_grad = lax.psum(
            jnp.einsum("rf,df->rd", pre_grad, up_full, preferred_element_type=jnp.float32), "tensor"
        )
        norm_result, second_pull = jax.vjp(layer_norm, middle, gain_second, bias_second)
        middle_part, grad_gain_second, grad_bias_second = second_pull(normed_two_grad)
        middle_grad = upstream + middle_part
        middle_low = middle_grad.astype(jnp.bfloat16)
        grad_out = jnp.einsum(
            "rk,rd->kd", mixed_heads, middle_low, preferred_element_type=jnp.float32
        )
        mixed_grad = jnp.einsum(
            "rd,kd->rk", middle_low, out_full, preferred_element_type=jnp.float32
        )
        mixed_grad = mixed_grad.reshape(block_total, BLK, heads_local, head_size)
        numer_grad = (mixed_grad / denominator[..., None]).astype(jnp.bfloat16)
        denom_grad = -jnp.sum(mixed_grad * numerator, -1) / (denominator * denominator)
        weight_grad = jnp.einsum(
            "nthe,nshe->nhts", numer_grad, value_blocks, preferred_element_type=jnp.float32
        )
        weight_grad = weight_grad + denom_grad.transpose(0, 2, 1)[..., None]
        weight_grad_low = jnp.where(allowed, weight_grad, 0.0).astype(jnp.bfloat16)
        value_grad = jnp.einsum(
            "nhts,nthe->nshe", weights_low, numer_grad, preferred_element_type=jnp.float32
        )
        query_grad = jnp.einsum(
            "nhts,nshf->nthf", weight_grad_low, key_blocks, preferred_element_type=jnp.float32
        )
        query_grad = query_grad + jnp.einsum(
            "nthe,nhfe->nthf", numer_grad, prior_states, preferred_element_type=jnp.float32
        )
        query_grad = query_grad + denom_grad[..., None] * prior_sums[:, None]
        key_grad = jnp.einsum(
            "nhts,nthf->nshf", weight_grad_low, query_blocks, preferred_element_type=jnp.float32
        )
        prior_grad = jnp.einsum(
            "nthf,nthe->nhfe", query_blocks, numer_grad, preferred_element_type=jnp.float32
        )
        prior_grad = prior_grad.reshape(seq_local, blocks_local, heads_local, feat_size, head_size)
        prior_sums_grad = jnp.einsum(
            "nthf,nth->nhf", query_blocks.astype(jnp.float32), denom_grad, precision=highest
        )
        prior_sums_grad = prior_sums_grad.reshape(seq_local, blocks_local, heads_local, feat_size)
        grad_total = jnp.sum(prior_grad, 1)
        grad_sums_total = jnp.sum(prior_sums_grad, 1)
        later_states, later_sums = carried_in(
            (grad_total, grad_sums_total),
            "context",
            add_pair,
            (jnp.zeros_like(grad_total), jnp.zeros_like(grad_sums_total)),
            True,
        )
        state_grad = (later_states[:, None] + suffix_after(prior_grad)).astype(jnp.bfloat16)
        state_grad = state_grad.reshape(block_total, heads_local, feat_size, head_size)
        sums_grad = (later_sums[:, None] + suffix_after(prior_sums_grad)).reshape(
            block_total, heads_local, feat_size
        )
        key_grad = key_grad + jnp.einsum(
            "nshe,nhfe->nshf", value_blocks, state_grad, preferred_element_type=jnp.float32
        )
        key_grad = key_grad + sums_grad[:, None]
        value_grad = value_grad + jnp.einsum(
            "nshf,nhfe->nshe", key_blocks, state_grad, preferred_element_type=jnp.float32
        )
        query_feat_now, query_pull = jax.vjp(features, query_logits)
        query_logit_grad = query_pull(query_grad.reshape(row_count, heads_local, feat_size))[
            0
        ].astype(jnp.bfloat16)
        key_feat_now, key_pull = jax.vjp(features, key_logits)
        key_logit_grad = key_pull(key_grad.reshape(row_count, heads_local, feat_size))[0].astype(
            jnp.bfloat16
        )
        grad_qmap = jnp.einsum(
            "rhi,rhj->hij", queries, query_logit_grad, preferred_element_type=jnp.float32
        )
        grad_kmap = jnp.einsum(
            "rhi,rhj->hij", key_rows, key_logit_grad, preferred_element_type=jnp.float32
        )
        raw_query_grad = jnp.einsum(
            "rhj,hij->rhi", query_logit_grad, qmap_full, preferred_element_type=jnp.float32
        )
        raw_key_grad = jnp.einsum(
            "rhj,hij->rhi", key_logit_grad, kmap_full, preferred_element_type=jnp.float32
        )
        projected_grad = jnp.stack(
            [
                raw_query_grad.reshape(row_count, -1),
                raw_key_grad.reshape(row_count, -1),
                value_grad.reshape(row_count, -1),
            ]
        ).astype(jnp.bfloat16)
        grad_in = jnp.einsum(
            "rd,cre->cde", normed_low, projected_grad, preferred_element_type=jnp.float32
        )
        normed_one_grad = lax.psum(
            jnp.einsum("cre,cde->rd", projected_grad, in_full, preferred_element_type=jnp.float32),
            "tensor",
        )
        first_result, first_pull = jax.vjp(layer_norm, source, gain_first, bias_first)
        source_part, grad_gain_first, grad_bias_first = first_pull(normed_one_grad)
        in_grads.append((middle_grad + source_part).reshape(seq_local, seq_len, model_width))
        grad_list = (
            grad_in,
            grad_out,
            grad_up,
            grad_down,
            grad_qmap,
            grad_kmap,
            grad_gain_first,
            grad_bias_first,
            grad_gain_second,
            grad_bias_second,
        )
        reduced = reduce_grads(grad_list)
        totals = reduced if totals is None else jax.tree.map(jnp.add, totals, reduced)
    return (
        jnp.stack(outputs),
        jnp.stack(in_grads),
        totals[0],
        totals[1],
        totals[2],
        totals[3],
        totals[4],
        totals[5],
        totals[6],
        totals[7],
        totals[8],
        totals[9],
    )


def solution(mesh):
    in_specs = (
        P(None, "fsdp", "context", None),
        P(None, "fsdp", "context", None),
        P(None, "fsdp", None),
        P(None, "fsdp", "tensor"),
        P("tensor", "fsdp"),
        P("fsdp", "tensor"),
        P("tensor", "fsdp"),
        P("tensor", "fsdp", None),
        P("tensor", "fsdp", None),
        P("fsdp"),
        P("fsdp"),
        P("fsdp"),
        P("fsdp"),
    )
    out_specs = (
        P(None, "fsdp", "context", None),
        P(None, "fsdp", "context", None),
        P(None, "fsdp", "tensor"),
        P("tensor", "fsdp"),
        P("fsdp", "tensor"),
        P("tensor", "fsdp"),
        P("tensor", "fsdp", None),
        P("tensor", "fsdp", None),
        P("fsdp"),
        P("fsdp"),
        P("fsdp"),
        P("fsdp"),
    )
    return jax.shard_map(
        per_device, mesh=mesh, in_specs=in_specs, out_specs=out_specs, check_vma=False
    )
```

profile of v0, /device:TPU:0, one launch (start us, length us, event | category | flops | bytes accessed | tf_op | source)
XLA Modules:
  0.0 1212.1 jit_solution(11642279815812940089)
XLA Ops:
  14.2 3.0 convert_reduce_fusion.1
  19.9 2.4 all_gather.106
  24.9 2.7 fusion.196
  29.7 3.4 all_gather.107
  33.1 2.9 fusion.194
  36.0 2.9 fusion.195
  40.7 3.6 all_gather.113
  60.7 9.4 all-gather.10
  71.2 10.8 all-gather
  82.0 10.2 while.64
  115.8 69.3 %all-reduce.25.cloned.1.call-done = bf16[1024,768]{1,0:T(8,128)(2,1)} async-done(((bf16[1024,768]{1,0:T(8,128)(2,1)}), bf16[1024,768]{1,0:T(8,128)(2,1)}) %all-reduce.25.cloned.1.call-update) | async-done | bytes 1572880 | tf_op jit(solution)/shard_map/psum | solution.py:248
  185.1 3.1 fusion.49
  190.8 2.7 fusion.201
  195.7 2.9 fusion.199
  198.6 2.9 fusion.200
  217.8 8.7 all-gather.13
  227.5 10.5 all-gather.2
  238.1 10.9 while.65
  275.7 62.7 %all-reduce.27.cloned.1.call-done = bf16[1024,768]{1,0:T(8,128)(2,1)} async-done(((bf16[1024,768]{1,0:T(8,128)(2,1)}), bf16[1024,768]{1,0:T(8,128)(2,1)}) %all-reduce.27.cloned.1.call-update) | async-done | bytes 1572880 | tf_op jit(solution)/shard_map/psum | solution.py:248
  338.4 3.2 multiply_reduce_fusion.5
  342.3 2.6 add_convert_fusion.3
  344.9 4.9 fusion.206
  349.9 3.5 fusion.189
  353.4 5.7 fusion.47
  359.1 3.1 fusion.40
  362.2 3.1 fusion.212
  365.3 3.1 fusion.207
  368.7 5.5 convolution_convert_fusion
  374.3 3.2 convolution_convert_fusion.2
  377.6 4.4 fusion.61
  382.1 3.3 fusion.74
  390.0 4.0 fusion.218
  394.0 3.4 convolution_add_fusion
  397.7 193.0 %all-reduce.31.cloned.1.call-done = (f32[1024,768]{1,0:T(8,128)}, f32[1024,768]{1,0:T(8,128)}) async-done(((f32[1024,768]{1,0:T(8,128)}, f32[1024,768]{1,0:T(8,128)}), (f32[1024,768]{1,0:T(8,128)}, f32[1024,768]{1,0:T(8,128)})) %all-reduce.31.cloned.1.call-update) | async-done | bytes 6291472 | tf_op jit(solution)/shard_map/psum | solution.py:288
  590.7 5.9 multiply_reduce_fusion.1
  596.6 116.4 %all-reduce.35.cloned.1.call-done = (bf16[1024,768]{1,0:T(8,128)(2,1)}, bf16[1024,768]{1,0:T(8,128)(2,1)}) async-done(((bf16[1024,768]{1,0:T(8,128)(2,1)}, bf16[1024,768]{1,0:T(8,128)(2,1)}), (bf16[1024,768]{1,0:T(8,128)(2,1)}, bf16[1024,768]{1,0:T(8,128)(2,1)})) %all-reduce.35.cloned.1.call-update) | async-done | bytes 3145744 | tf_op jit(solution)/shard_map/psum | solution.py:257
  713.0 7.5 fusion.191
  721.1 2.5 fusion.53
  726.4 2.4 reshape.654
  728.8 2.3 multiply_reduce_fusion.10
  732.4 2.9 fusion.208
  735.3 2.5 reshape.650
  753.5 8.0 all-gather.15
  762.2 8.1 all-gather.14
  770.3 9.3 all-gather.4
  783.8 3.1 while.66
  791.6 2.3 fusion.205
  793.9 10.4 all-gather.6
  808.6 5.1 while.67
  851.3 2.4 add_convert_fusion.5
  864.5 2.7 fusion.56
  867.3 2.6 add_bitcast_fusion.2
  870.1 4.6 convolution_bitcast_fusion.1
  874.7 3.1 convolution_bitcast_fusion
  887.7 3.9 pad_maximum_fusion.1
  891.6 207.3 %all-reduce.29.cloned.1.call-done = (f32[1024,768]{1,0:T(8,128)}, f32[1024,768]{1,0:T(8,128)}) async-done(((f32[1024,768]{1,0:T(8,128)}, f32[1024,768]{1,0:T(8,128)}), (f32[1024,768]{1,0:T(8,128)}, f32[1024,768]{1,0:T(8,128)})) %all-reduce.29.cloned.1.call-update) | async-done | bytes 6291472 | tf_op jit(solution)/shard_map/psum | solution.py:381
  1099.0 3.8 fusion.31
  1103.7 3.3 fusion.29
  1107.0 3.3 all-reduce.16
  1110.6 22.8 %all-reduce.14 = (f32[3,32,64]{2,1,0:T(8,128)}, f32[3,32,64]{2,1,0:T(8,128)}, f32[384]{0:T(512)}, f32[384]{0:T(512)}, f32[384]{0:T(512)}, /*index=5*/f32[384]{0:T(512)}) all-reduce(f32[3,32,64]{2,1,0:T(8,128)} %reduce-scatter.15.cloned.1.call-done, ...), channel_id=1, replica_groups=mesh['fsdp'=2,'context'=4,'tensor'=4] {'context'}, use_global_device_ids=true, to_apply=%region_97.98 | all-reduce | flops 13824 | bytes 110592 | tf_op jit(solution)/shard_map/psum | solution.py:98
  1133.4 7.6 add_bitcast_fusion.1
  1141.1 3.1 pad_maximum_fusion
  1144.2 54.3 %all-reduce.33.cloned.1.call-done = (f32[3,384,192]{1,2,0:T(8,128)}, f32[192,384]{1,0:T(8,128)}, f32[384,768]{1,0:T(8,128)}, f32[768,384]{1,0:T(8,128)}) async-done(((f32[3,384,192]{1,2,0:T(8,128)}, f32[192,384]{1,0:T(8,128)}, f32[384,768]{1,0:T(8,128)}, f32[768,384]{1,0:T(8,128)}), (f32[3,384,192]{1,2,0:T(8,128)}, f32[192,384]{1,0:T(8,128)}, f32[384,768]{1,0:T(8,128)}, ...) | async-done | bytes 3538960 | tf_op jit(solution)/shard_map/psum | solution.py:98
  1198.5 2.3 copy.349
  (747 shorter events, 235.1 us)
Async XLA Ops:
  8.0 9.3 copy-start
  8.0 9.9 copy-start.200
  8.0 177.1 %all-reduce.25.cloned.1.call-start = ((), (), s32[]{:S(2)}) async-start(), calls=%async_computation.6 | async-start | bytes 3145728 | tf_op jit(solution)/shard_map/psum | solution.py:248
  11.7 12.0 copy-start.154
  14.2 9.4 copy-start.212
  17.3 6.4 copy-start.142
  24.9 19.4 %copy-start.69 = (bf16[1,1024,192]{1,2,0:T(8,128)(2,1)}, bf16[1,1024,192]{1,2,0:T(8,128)(2,1)S(1)}, u32[]{:S(2)}) copy-start(bf16[1,1024,192]{1,2,0:T(8,128)(2,1)S(1)} %get-tuple-element.719) | copy-start | bytes 1179652
  29.7 22.2 %copy-start.114 = (f32[1024,3]{0,1:T(4,128)}, f32[1024,3]{0,1:T(4,128)S(1)}, u32[]{:S(2)}) copy-start(f32[1024,3]{0,1:T(4,128)S(1)} %get-tuple-element.739) | copy-start | bytes 36868
  45.6 24.5 %copy-start.57 = (bf16[4,256,3,64]{1,0,3,2:T(4,128)(2,1)}, bf16[4,256,3,64]{1,0,3,2:T(4,128)(2,1)S(1)}, u32[]{:S(2)}) copy-start(bf16[4,256,3,64]{1,0,3,2:T(4,128)(2,1)S(1)} %reshape_reshape_squeeze.6) | copy-start | bytes 1179652
  60.0 10.1 copy-start.33
  82.0 13.7 %copy-start.131 = (f32[1024,3]{0,1:T(4,128)S(1)}, f32[1024,3]{0,1:T(4,128)}, u32[]{:S(2)}) copy-start(f32[1024,3]{0,1:T(4,128)} %get-tuple-element.733) | copy-start | bytes 36868
  92.2 7.9 copy-start.117
  115.7 72.5 %copy-start.155 = (f32[768]{0:T(1024)S(1)}, f32[768]{0:T(1024)}, u32[]{:S(2)}) copy-start(f32[768]{0:T(1024)} %copy-done.154) | copy-start | bytes 9220
  115.7 72.5 %copy-start.213 = (f32[768]{0:T(1024)S(1)}, f32[768]{0:T(1024)}, u32[]{:S(2)}) copy-start(f32[768]{0:T(1024)} %copy-done.212) | copy-start | bytes 9220
  115.7 222.7 %all-reduce.27.cloned.1.call-start = ((), (), s32[]{:S(2)}) async-start(), calls=%async_computation.9 | async-start | bytes 3145728 | tf_op jit(solution)/shard_map/psum | solution.py:248
  115.8 73.7 %copy-start.144 = (f32[1024]{0:T(1024)}, f32[1024]{0:T(1024)S(1)}, u32[]{:S(2)}) copy-start(f32[1024]{0:T(1024)S(1)} %broadcast_multiply_fusion.1) | copy-start | bytes 12292
  190.8 10.7 copy-start.73
  202.7 23.8 %copy-start.61 = (bf16[4,256,3,64]{1,0,3,2:T(4,128)(2,1)}, bf16[4,256,3,64]{1,0,3,2:T(4,128)(2,1)S(1)}, u32[]{:S(2)}) copy-start(bf16[4,256,3,64]{1,0,3,2:T(4,128)(2,1)S(1)} %reshape_reshape_squeeze.7) | copy-start | bytes 1179652
  217.2 9.3 copy-start.37
  238.1 14.3 %copy-start.126 = (f32[1024,3]{0,1:T(4,128)S(1)}, f32[1024,3]{0,1:T(4,128)}, u32[]{:S(2)}) copy-start(f32[1024,3]{0,1:T(4,128)} %get-tuple-element.747) | copy-start | bytes 36868
  267.7 6.1 copy-start.216
  267.7 8.0 copy-start.209
  270.7 74.2 %all-gather.19.cloned.1.call-start = ((), (), s32[]{:S(2)}) async-start(), calls=%async_computation.7 | async-start | bytes 1769472 | tf_op jit(solution)/shard_map/all_gather | solution.py:74
  271.3 82.1 %all-gather.21.cloned.1.call-start = ((), (), s32[]{:S(2)}) async-start(), calls=%async_computation.8 | async-start | bytes 1769472 | tf_op jit(solution)/shard_map/all_gather | solution.py:75
  271.9 318.8 %all-reduce.31.cloned.1.call-start = ((), (), s32[]{:S(2)}) async-start(), calls=%async_computation.17 | async-start | bytes 12582912 | tf_op jit(solution)/shard_map/psum | solution.py:288
  273.8 76.0 %copy-start.170 = (f32[768]{0:T(1024)}, f32[768]{0:T(1024)S(1)}, u32[]{:S(2)}) copy-start(f32[768]{0:T(1024)S(1)} %reshape.684) | copy-start | bytes 9220
  275.7 74.2 %copy-start.205 = (f32[768]{0:T(1024)}, f32[768]{0:T(1024)S(1)}, u32[]{:S(2)}) copy-start(f32[768]{0:T(1024)S(1)} %reshape.685) | copy-start | bytes 9220
  275.7 66.5 %copy-start.146 = (f32[1024]{0:T(1024)}, f32[1024]{0:T(1024)S(1)}, u32[]{:S(2)}) copy-start(f32[1024]{0:T(1024)S(1)} %broadcast_multiply_fusion.2) | copy-start | bytes 12292
  341.7 8.2 copy-start.172
  368.5 344.5 %all-reduce.35.cloned.1.call-start = ((), (), s32[]{:S(2)}) async-start(), calls=%async_computation.19 | async-start | bytes 6291456 | tf_op jit(solution)/shard_map/psum | solution.py:257
  377.5 510.0 %reduce-scatter.13.cloned.1.call-start = ((), (), s32[]{:S(2)}) async-start(), calls=%async_computation.13 | async-start | bytes 3538944 | tf_op jit(solution)/shard_map/reduce_scatter | solution.py:90
  382.0 6.7 copy-start.127
  382.0 7.3 copy-start.112
  385.4 502.2 %reduce-scatter.11.cloned.1.call-start = ((), (), s32[]{:S(2)}) async-start(), calls=%async_computation.12 | async-start | bytes 3538944 | tf_op jit(solution)/shard_map/reduce_scatter | solution.py:89
  394.0 196.7 %copy-start.147 = (f32[1024]{0:T(1024)S(1)}, f32[1024]{0:T(1024)}, u32[]{:S(2)}) copy-start(f32[1024]{0:T(1024)} %copy-done.146) | copy-start | bytes 12292
  394.0 196.7 %copy-start.175 = (f32[1024]{0:T(1024)S(1)}, f32[1024]{0:T(1024)}, u32[]{:S(2)}) copy-start(f32[1024]{0:T(1024)} %copy-done.174) | copy-start | bytes 12292
  397.4 490.2 %reduce-scatter.9.cloned.1.call-start = ((), (), s32[]{:S(2)}) async-start(), calls=%async_computation.11 | async-start | bytes 884736 | tf_op jit(solution)/shard_map/reduce_scatter | solution.py:88
  713.0 8.2 copy-start.25
  723.6 7.5 copy-start.141
  723.6 7.5 copy-start.169
  735.3 12.9 %copy-start.59 = (bf16[4,256,3,64]{1,0,3,2:T(4,128)(2,1)S(1)}, bf16[4,256,3,64]{1,0,3,2:T(4,128)(2,1)}, u32[]{:S(2)}) copy-start(bf16[4,256,3,64]{1,0,3,2:T(4,128)(2,1)} %copy-done.57) | copy-start | bytes 1179652
  737.8 8.8 copy-start.12
  737.8 10.4 copy-start.124
  739.4 9.4 copy-start.67
  748.9 13.3 %copy-start.210 = (f32[3,128]{1,0:T(4,128)S(1)}, f32[3,128]{1,0:T(4,128)}, u32[]{:S(2)}) copy-start(f32[3,128]{1,0:T(4,128)} %fusion.167) | copy-start | bytes 4612
  748.9 21.3 %copy-start.107 = (f32[3,128,64]{1,2,0:T(8,128)S(1)}, f32[3,128,64]{1,2,0:T(8,128)}, u32[]{:S(2)}) copy-start(f32[3,128,64]{1,2,0:T(8,128)} %get-tuple-element.761) | copy-start | bytes 294916
  750.7 33.0 %copy-start.50 = (f32[1,3,128,64]{3,2,1,0:T(8,128)S(1)}, f32[1,3,128,64]{3,2,1,0:T(8,128)}, u32[]{:S(2)}) copy-start(f32[1,3,128,64]{3,2,1,0:T(8,128)} %custom-call.4) | copy-start | bytes 294916
  750.7 33.0 %copy-start.151 = (f32[1,3,128]{2,1,0:T(4,128)S(1)}, f32[1,3,128]{2,1,0:T(4,128)}, u32[]{:S(2)}) copy-start(f32[1,3,128]{2,1,0:T(4,128)} %custom-call.5) | copy-start | bytes 4612
  789.1 19.5 %copy-start.49 = (f32[1,3,128,64]{3,2,1,0:T(8,128)S(1)}, f32[1,3,128,64]{3,2,1,0:T(8,128)}, u32[]{:S(2)}) copy-start(f32[1,3,128,64]{3,2,1,0:T(8,128)} %custom-call.6) | copy-start | bytes 294916
  789.1 19.5 %copy-start.148 = (f32[1,3,128]{2,1,0:T(4,128)S(1)}, f32[1,3,128]{2,1,0:T(4,128)}, u32[]{:S(2)}) copy-start(f32[1,3,128]{2,1,0:T(4,128)} %custom-call.7) | copy-start | bytes 4612
  806.4 10.8 copy-start.109
  806.4 10.8 copy-start.138
  806.4 10.8 copy-start.194
  826.8 8.5 copy-start.66
  851.0 36.7 %reduce-scatter.7.cloned.1.call-start = ((), (), s32[]{:S(2)}) async-start(), calls=%async_computation.10 | async-start | bytes 2654208 | tf_op jit(solution)/shard_map/reduce_scatter | solution.py:87
  855.3 11.9 copy-start.74
  855.3 9.2 copy-start.145
  855.3 9.2 copy-start.156
  870.0 229.0 %all-reduce.29.cloned.1.call-start = ((), (), s32[]{:S(2)}) async-start(), calls=%async_computation.16 | async-start | bytes 12582912 | tf_op jit(solution)/shard_map/psum | solution.py:381
  877.8 232.7 %reduce-scatter.15.cloned.1.call-start = ((), (), s32[]{:S(2)}) async-start(), calls=%async_computation.14 | async-start | bytes 147456 | tf_op jit(solution)/shard_map/reduce_scatter | solution.py:91
  883.5 227.1 %reduce-scatter.17.cloned.1.call-start = ((), (), s32[]{:S(2)}) async-start(), calls=%async_computation.15 | async-start | bytes 147456 | tf_op jit(solution)/shard_map/reduce_scatter | solution.py:92
  885.6 312.9 %all-reduce.33.cloned.1.call-start = ((), (), s32[]{:S(2)}) async-start(), calls=%async_computation.18 | async-start | bytes 7077888 | tf_op jit(solution)/shard_map/psum | solution.py:98
  1103.7 29.7 %copy-start.181 = (f32[1024]{0:T(1024)S(1)}, f32[1024]{0:T(1024)}, u32[]{:S(2)}) copy-start(f32[1024]{0:T(1024)} %copy-done.180) | copy-start | bytes 12292
  1103.7 29.7 %copy-start.183 = (f32[1024]{0:T(1024)S(1)}, f32[1024]{0:T(1024)}, u32[]{:S(2)}) copy-start(f32[1024]{0:T(1024)} %copy-done.182) | copy-start | bytes 12292
  (178 other events, 545.3 us)
Sparse Core Ops, SparseCore 0:
  115.9 69.2 all-reduce.24
  270.8 67.5 all-reduce.26
  368.6 222.0 all-reduce.30
  593.0 119.9 all-reduce.34
  878.0 220.9 all-reduce.28
  1102.3 96.1 all-reduce.32
Sparse Core Ops, SparseCore 1:
  272.7 7.7 all-gather.18
  281.9 10.2 all-gather.20
  385.5 9.0 reduce-scatter.12
  397.5 11.1 reduce-scatter.10
  851.0 6.0 reduce-scatter.8
  870.0 7.1 reduce-scatter.6
  883.6 5.4 reduce-scatter.14
  891.6 8.6 reduce-scatter.16
where the time goes:
time: 1220 us; the launch traced here: 1210 us
  waiting for transfers between devices  704 us (58%)
  matrix products  136 us (11%)
  other arithmetic  134 us (11%)
  blocking collectives  120 us (10%)
  local copies, waits for them, and re-layouts  96.9 us (8%)
  between operations  19.4 us (2%)
    psum x1, waiting for transfers between devices, per_device(): lax.psum(jnp.einsum('cre,cde->rd', projected_grad, in_full, preferred_ele...  207 us
    psum x1, waiting for transfers between devices, per_device(): lax.psum(jnp.einsum('rf,df->rd', pre_grad, up_full, preferred_element_typ...  193 us
    psum x2, waiting for transfers between devices, per_device(): lax.psum(jnp.dot(mixed_heads, out_full, preferred_element_type=jnp.float3...  132 us
    psum x1, waiting for transfers between devices, per_device(): lax.psum(jnp.dot(hidden_low, down_full, preferred_element_type=jnp.float3...  116 us
    all_gather x8, blocking collectives, carried_in(): pieces = jax.tree.map(lambda part: lax.all_gather(part, axis), value)  75.3 us
    psum x1, waiting for transfers between devices, reduce_grads(): lax.psum((shares[0], shares[1], shares[2], shares[3], shares[4], shares[5...  54.3 us
    concatenate x16, local copies, waits for them, and re-layouts, features(): jnp.concatenate([jax.nn.softmax(logits, -1), jax.nn.softmax(-logits, -1)]...  27 us
  transfers between devices with their start and end apart: 14, of which 6 were waited for; matrix products, arithmetic and copies ran while one was open for 17% of the time, Pallas kernels for 0%

commit v1 on v0

v1 whole, which is shorter than its diff:
```python
import jax
import jax.numpy as jnp
from jax import lax
from jax.sharding import PartitionSpec as P

BLK = 256
MICRO = 2


epsilon = 1e-05
highest = lax.Precision.HIGHEST


EVERY = ("fsdp", "context", "tensor")


def carried_in(value, backward):
    slot, mine = lax.axis_index("tensor"), lax.axis_index("context")
    near = lax.all_gather(value, "tensor")
    far = lax.all_gather(jnp.sum(near, 0).astype(value.dtype), "context")
    near_ids = jnp.arange(near.shape[0]).reshape((-1,) + (1,) * value.ndim)
    far_ids = jnp.arange(far.shape[0]).reshape((-1,) + (1,) * value.ndim)
    near_mask = near_ids > slot if backward else near_ids < slot
    far_mask = far_ids > mine if backward else far_ids < mine
    near, far = near.astype(jnp.float32), far.astype(jnp.float32)
    return jnp.sum(jnp.where(near_mask, near, 0.0), 0) + jnp.sum(jnp.where(far_mask, far, 0.0), 0)


def layer_norm(values, norm_gain, norm_bias):
    center = values - jnp.mean(values, -1, keepdims=True)
    spread = jnp.mean(center * center, -1, keepdims=True)
    return center * lax.rsqrt(spread + epsilon) * norm_gain + norm_bias


def features(logits):
    return jnp.concatenate([jax.nn.softmax(logits, -1), jax.nn.softmax(-logits, -1)], -1)


def gelu_tanh(values):
    return jax.nn.gelu(values, approximate=True)


def prefix_before(values):
    running = jnp.cumsum(values, 1)
    return jnp.concatenate([jnp.zeros_like(values[:, :1]), running[:, :-1]], 1)


def suffix_after(values):
    running = jnp.flip(jnp.cumsum(jnp.flip(values, 1), 1), 1)
    return jnp.concatenate([running[:, 1:], jnp.zeros_like(values[:, :1])], 1)


def spread(part, axis, parts):
    own = lax.axis_index("context")
    size = part.shape[axis] // parts
    mine = lax.dynamic_slice_in_dim(part, own * size, size, axis)
    return lax.all_gather(mine, EVERY)


def full_in(part):
    pieces = spread(part, 1, lax.axis_size("context"))
    fsdp, ctx, tens = (lax.axis_size(name) for name in EVERY)
    pieces = pieces.reshape((fsdp, ctx, tens) + pieces.shape[1:])
    pieces = pieces.transpose(3, 0, 1, 4, 2, 5)
    return pieces.reshape(pieces.shape[0], -1, pieces.shape[4] * pieces.shape[5])


def share_in(grad):
    fsdp, ctx, tens = (lax.axis_size(name) for name in EVERY)
    kinds, rows, cols = grad.shape
    pieces = grad.astype(jnp.bfloat16).reshape(kinds, fsdp, ctx, rows // fsdp // ctx, tens, cols // tens)
    pieces = pieces.transpose(1, 2, 4, 0, 3, 5).reshape((-1,) + (kinds, rows // fsdp // ctx, cols // tens))
    mine = lax.psum_scatter(pieces, EVERY, scatter_dimension=0)
    return lax.all_gather(mine, "context", axis=1, tiled=True).astype(jnp.float32)


def full_rows(part):
    pieces = spread(part, 0, lax.axis_size("context"))
    fsdp, ctx, tens = (lax.axis_size(name) for name in EVERY)
    pieces = pieces.reshape((fsdp, ctx, tens) + pieces.shape[1:])
    pieces = pieces.transpose(2, 1, 3, 0, 4)
    return pieces.reshape(tens * part.shape[0], -1)


def share_rows(grad):
    fsdp, ctx, tens = (lax.axis_size(name) for name in EVERY)
    rows, cols = grad.shape
    pieces = grad.astype(jnp.bfloat16).reshape(tens, ctx, rows // tens // ctx, fsdp, cols // fsdp)
    pieces = pieces.transpose(3, 1, 0, 2, 4).reshape(-1, rows // tens // ctx, cols // fsdp)
    mine = lax.psum_scatter(pieces, EVERY, scatter_dimension=0)
    return lax.all_gather(mine, "context", axis=0, tiled=True).astype(jnp.float32)


def full_maps(part):
    pieces = lax.all_gather(part, ("fsdp", "tensor"))
    fsdp, tens = lax.axis_size("fsdp"), lax.axis_size("tensor")
    pieces = pieces.reshape((fsdp, tens) + part.shape).transpose(1, 2, 0, 3, 4)
    return pieces.reshape(tens * part.shape[0], fsdp * part.shape[1], part.shape[2])


def own_maps(total):
    fsdp, tens = lax.axis_size("fsdp"), lax.axis_size("tensor")
    heads, rows, _ = total.shape
    mine = lax.dynamic_slice_in_dim(total, lax.axis_index("tensor") * (heads // tens), heads // tens, 0)
    return lax.dynamic_slice_in_dim(mine, lax.axis_index("fsdp") * (rows // fsdp), rows // fsdp, 1)


def per_device(
    inputs,
    cotangent,
    picture_starts,
    qkv_weight,
    out_weight,
    up_weight,
    down_weight,
    query_map,
    key_map,
    first_gain,
    first_bias,
    second_gain,
    second_bias,
):
    tensor_size = lax.axis_size("tensor")
    micro, seq_local, seq_len, model_width = inputs.shape
    span = seq_len // tensor_size
    slot = lax.axis_index("tensor")
    head_size = query_map.shape[2]
    feat_size = 2 * head_size
    blocks_local = span // BLK
    seq_count = micro * seq_local
    block_total = seq_count * blocks_local
    row_count = seq_count * span
    first_block = (lax.axis_index("context") * tensor_size + slot) * blocks_local
    block_ids = first_block + jnp.arange(blocks_local, dtype=jnp.int32)
    position = jnp.arange(BLK, dtype=jnp.int32)
    causal = position[None, :] <= position[:, None]

    in_full = full_in(qkv_weight)
    out_full = full_rows(out_weight)
    up_full = full_in(up_weight[None])[0]
    down_full = full_rows(down_weight)
    qmap_full, kmap_full = full_maps(query_map), full_maps(key_map)
    norms = lax.all_gather(jnp.stack([first_gain, first_bias, second_gain, second_bias]), "fsdp", axis=1, tiled=True)
    gain_first, bias_first, gain_second, bias_second = norms.astype(jnp.float32)

    def own(values):
        mine = lax.dynamic_slice_in_dim(values, slot * span, span, 2)
        return mine.reshape(row_count, model_width)

    source = own(inputs).astype(jnp.float32)
    starts_here = picture_starts.reshape(seq_count, -1)
    block_flags = (
        jnp.sum((starts_here[:, :, None] // BLK == block_ids[None, None, :]).astype(jnp.int32), 1)
        > 0
    )
    allowed = causal[None, None] | block_flags[:, :, None, None]
    allowed = allowed.reshape(block_total, 1, BLK, BLK)
    normed_one = layer_norm(source, gain_first, bias_first)
    normed_low = normed_one.astype(jnp.bfloat16)
    projected = jnp.einsum(
        "rd,cde->cre", normed_low, in_full, preferred_element_type=jnp.float32
    ).astype(jnp.bfloat16)
    heads_local = projected.shape[2] // head_size
    queries = projected[0].reshape(row_count, heads_local, head_size)
    key_rows = projected[1].reshape(row_count, heads_local, head_size)
    value_rows = projected[2].reshape(row_count, heads_local, head_size)
    query_logits = jnp.einsum(
        "rhi,hij->rhj", queries, qmap_full, preferred_element_type=jnp.float32
    )
    key_logits = jnp.einsum(
        "rhi,hij->rhj", key_rows, kmap_full, preferred_element_type=jnp.float32
    )
    query_blocks = (
        features(query_logits)
        .astype(jnp.bfloat16)
        .reshape(block_total, BLK, heads_local, feat_size)
    )
    key_blocks = (
        features(key_logits)
        .astype(jnp.bfloat16)
        .reshape(block_total, BLK, heads_local, feat_size)
    )
    value_blocks = value_rows.reshape(block_total, BLK, heads_local, head_size)
    scores = jnp.einsum(
        "nthf,nshf->nhts", query_blocks, key_blocks, preferred_element_type=jnp.float32
    )
    weights_low = jnp.where(allowed, scores, 0.0).astype(jnp.bfloat16)
    states = jnp.einsum(
        "nshf,nshe->nhfe", key_blocks, value_blocks, preferred_element_type=jnp.float32
    )
    states = states.reshape(seq_count, blocks_local, heads_local, feat_size, head_size)
    key_sums = jnp.sum(key_blocks.astype(jnp.float32), 1).reshape(
        seq_count, blocks_local, heads_local, feat_size
    )
    state_total = jnp.sum(states, 1)
    sums_total = jnp.sum(key_sums, 1)
    carried = carried_in(state_total.astype(jnp.bfloat16), False)
    carried_sums = carried_in(sums_total, False)
    prior_states = (carried[:, None] + prefix_before(states)).astype(jnp.bfloat16)
    prior_states = prior_states.reshape(block_total, heads_local, feat_size, head_size)
    prior_sums = (carried_sums[:, None] + prefix_before(key_sums)).reshape(
        block_total, heads_local, feat_size
    )
    numerator = jnp.einsum(
        "nhts,nshe->nthe", weights_low, value_blocks, preferred_element_type=jnp.float32
    )
    numerator = numerator + jnp.einsum(
        "nthf,nhfe->nthe", query_blocks, prior_states, preferred_element_type=jnp.float32
    )
    denominator = jnp.sum(weights_low.astype(jnp.float32), -1).transpose(0, 2, 1)
    denominator = denominator + jnp.einsum(
        "nthf,nhf->nth", query_blocks.astype(jnp.float32), prior_sums, precision=highest
    )
    mixed_heads = (
        (numerator / denominator[..., None])
        .astype(jnp.bfloat16)
        .reshape(row_count, heads_local * head_size)
    )
    attended = jnp.dot(mixed_heads, out_full, preferred_element_type=jnp.float32)
    middle = source + attended
    normed_two = layer_norm(middle, gain_second, bias_second)
    normed_two_low = normed_two.astype(jnp.bfloat16)
    hidden_pre = jnp.dot(normed_two_low, up_full, preferred_element_type=jnp.float32)
    hidden_low = gelu_tanh(hidden_pre).astype(jnp.bfloat16)
    branch = jnp.dot(hidden_low, down_full, preferred_element_type=jnp.float32)
    output = (middle + branch).astype(jnp.bfloat16).reshape(micro, seq_local, span, model_width)
    output = lax.all_gather(output, "tensor", axis=2, tiled=True)
    upstream_low = own(cotangent)
    upstream = upstream_low.astype(jnp.float32)
    grad_down = jnp.einsum(
        "rk,rd->kd", hidden_low, upstream_low, preferred_element_type=jnp.float32
    )
    hidden_grad = jnp.einsum(
        "rd,kd->rk", upstream_low, down_full, preferred_element_type=jnp.float32
    )
    gelu_result, gelu_pull = jax.vjp(gelu_tanh, hidden_pre)
    pre_grad = gelu_pull(hidden_grad)[0].astype(jnp.bfloat16)
    grad_up = jnp.einsum(
        "rd,rf->df", normed_two_low, pre_grad, preferred_element_type=jnp.float32
    )
    normed_two_grad = jnp.einsum(
        "rf,df->rd", pre_grad, up_full, preferred_element_type=jnp.float32
    )
    norm_result, second_pull = jax.vjp(layer_norm, middle, gain_second, bias_second)
    middle_part, grad_gain_second, grad_bias_second = second_pull(normed_two_grad)
    middle_grad = upstream + middle_part
    middle_low = middle_grad.astype(jnp.bfloat16)
    grad_out = jnp.einsum(
        "rk,rd->kd", mixed_heads, middle_low, preferred_element_type=jnp.float32
    )
    mixed_grad = jnp.einsum(
        "rd,kd->rk", middle_low, out_full, preferred_element_type=jnp.float32
    )
    mixed_grad = mixed_grad.reshape(block_total, BLK, heads_local, head_size)
    numer_grad = (mixed_grad / denominator[..., None]).astype(jnp.bfloat16)
    denom_grad = -jnp.sum(mixed_grad * numerator, -1) / (denominator * denominator)
    weight_grad = jnp.einsum(
        "nthe,nshe->nhts", numer_grad, value_blocks, preferred_element_type=jnp.float32
    )
    weight_grad = weight_grad + denom_grad.transpose(0, 2, 1)[..., None]
    weight_grad_low = jnp.where(allowed, weight_grad, 0.0).astype(jnp.bfloat16)
    value_grad = jnp.einsum(
        "nhts,nthe->nshe", weights_low, numer_grad, preferred_element_type=jnp.float32
    )
    query_grad = jnp.einsum(
        "nhts,nshf->nthf", weight_grad_low, key_blocks, preferred_element_type=jnp.float32
    )
    query_grad = query_grad + jnp.einsum(
        "nthe,nhfe->nthf", numer_grad, prior_states, preferred_element_type=jnp.float32
    )
    query_grad = query_grad + denom_grad[..., None] * prior_sums[:, None]
    key_grad = jnp.einsum(
        "nhts,nthf->nshf", weight_grad_low, query_blocks, preferred_element_type=jnp.float32
    )
    prior_grad = jnp.einsum(
        "nthf,nthe->nhfe", query_blocks, numer_grad, preferred_element_type=jnp.float32
    )
    prior_grad = prior_grad.reshape(seq_count, blocks_local, heads_local, feat_size, head_size)
    prior_sums_grad = jnp.einsum(
        "nthf,nth->nhf", query_blocks.astype(jnp.float32), denom_grad, precision=highest
    )
    prior_sums_grad = prior_sums_grad.reshape(seq_count, blocks_local, heads_local, feat_size)
    grad_total = jnp.sum(prior_grad, 1)
    grad_sums_total = jnp.sum(prior_sums_grad, 1)
    later_states = carried_in(grad_total.astype(jnp.bfloat16), True)
    later_sums = carried_in(grad_sums_total, True)
    state_grad = (later_states[:, None] + suffix_after(prior_grad)).astype(jnp.bfloat16)
    state_grad = state_grad.reshape(block_total, heads_local, feat_size, head_size)
    sums_grad = (later_sums[:, None] + suffix_after(prior_sums_grad)).reshape(
        block_total, heads_local, feat_size
    )
    key_grad = key_grad + jnp.einsum(
        "nshe,nhfe->nshf", value_blocks, state_grad, preferred_element_type=jnp.float32
    )
    key_grad = key_grad + sums_grad[:, None]
    value_grad = value_grad + jnp.einsum(
        "nshf,nhfe->nshe", key_blocks, state_grad, preferred_element_type=jnp.float32
    )
    query_feat_now, query_pull = jax.vjp(features, query_logits)
    query_logit_grad = query_pull(query_grad.reshape(row_count, heads_local, feat_size))[
        0
    ].astype(jnp.bfloat16)
    key_feat_now, key_pull = jax.vjp(features, key_logits)
    key_logit_grad = key_pull(key_grad.reshape(row_count, heads_local, feat_size))[0].astype(
        jnp.bfloat16
    )
    grad_qmap = jnp.einsum(
        "rhi,rhj->hij", queries, query_logit_grad, preferred_element_type=jnp.float32
    )
    grad_kmap = jnp.einsum(
        "rhi,rhj->hij", key_rows, key_logit_grad, preferred_element_type=jnp.float32
    )
    raw_query_grad = jnp.einsum(
        "rhj,hij->rhi", query_logit_grad, qmap_full, preferred_element_type=jnp.float32
    )
    raw_key_grad = jnp.einsum(
        "rhj,hij->rhi", key_logit_grad, kmap_full, preferred_element_type=jnp.float32
    )
    projected_grad = jnp.stack(
        [
            raw_query_grad.reshape(row_count, -1),
            raw_key_grad.reshape(row_count, -1),
            value_grad.reshape(row_count, -1),
        ]
    ).astype(jnp.bfloat16)
    grad_in = jnp.einsum(
        "rd,cre->cde", normed_low, projected_grad, preferred_element_type=jnp.float32
    )
    normed_one_grad = jnp.einsum(
        "cre,cde->rd", projected_grad, in_full, preferred_element_type=jnp.float32
    )
    first_result, first_pull = jax.vjp(layer_norm, source, gain_first, bias_first)
    source_part, grad_gain_first, grad_bias_first = first_pull(normed_one_grad)
    input_grad = (middle_grad + source_part).astype(jnp.bfloat16)
    input_grad = input_grad.reshape(micro, seq_local, span, model_width)
    input_grad = lax.all_gather(input_grad, "tensor", axis=2, tiled=True).astype(jnp.float32)
    norm_grads = jnp.stack([grad_gain_first, grad_bias_first, grad_gain_second, grad_bias_second])
    grad_qmap, grad_kmap, norm_grads = lax.psum((grad_qmap, grad_kmap, norm_grads), EVERY)
    share = first_gain.shape[0]
    norm_grads = lax.dynamic_slice_in_dim(norm_grads, lax.axis_index("fsdp") * share, share, 1)
    return (
        output,
        input_grad,
        share_in(grad_in),
        share_rows(grad_out),
        share_in(grad_up[None])[0],
        share_rows(grad_down),
        own_maps(grad_qmap),
        own_maps(grad_kmap),
        norm_grads[0],
        norm_grads[1],
        norm_grads[2],
        norm_grads[3],
    )


def solution(mesh):
    in_specs = (
        P(None, "fsdp", "context", None),
        P(None, "fsdp", "context", None),
        P(None, "fsdp", None),
        P(None, "fsdp", "tensor"),
        P("tensor", "fsdp"),
        P("fsdp", "tensor"),
        P("tensor", "fsdp"),
        P("tensor", "fsdp", None),
        P("tensor", "fsdp", None),
        P("fsdp"),
        P("fsdp"),
        P("fsdp"),
        P("fsdp"),
    )
    out_specs = (
        P(None, "fsdp", "context", None),
        P(None, "fsdp", "context", None),
        P(None, "fsdp", "tensor"),
        P("tensor", "fsdp"),
        P("fsdp", "tensor"),
        P("tensor", "fsdp"),
        P("tensor", "fsdp", None),
        P("tensor", "fsdp", None),
        P("fsdp"),
        P("fsdp"),
        P("fsdp"),
        P("fsdp"),
    )
    return jax.shard_map(
        per_device, mesh=mesh, in_specs=in_specs, out_specs=out_specs, check_vma=False
    )
```

time: 1220 us -> 1160 us (0.951)
  other arithmetic: 134 us -> 51.4 us
  local copies, waits for them, and re-layouts: 96.9 us -> 168 us
  waiting for transfers between devices: 704 us -> 637 us
  blocking collectives: 120 us -> 179 us
  matrix products: 136 us -> 93.7 us
    psum x6 -> x1, waiting for transfers between devices: 703 us -> 94.5 us  [per_device(): lax.psum((grad_qmap, grad_kmap, norm_grads), EVERY)]
    reduce_scatter x6 -> x4, waiting for transfers between devices: 0.09 us -> 309 us  [the longest x2 208 us: share_in(): mine = lax.psum_scatter(pieces, EVERY, scatter_dimension=0)]
    all_gather x2 -> x10, waiting for transfers between devices: 0.03 us -> 233 us  [the longest x4 103 us: spread(): return lax.all_gather(mine, EVERY)]
    reshape x2 -> x13, local copies, waits for them, and re-layouts: 4.81 us -> 66.5 us  [the longest x2 15.9 us: full_in(): pieces = pieces.reshape((fsdp, ctx, tens) + pieces.shape[1:])]
    all_gather x16 -> x11, blocking collectives: 94.1 us -> 140 us  [the longest x2 52.6 us: full_maps(): pieces = lax.all_gather(part, ('fsdp', 'tensor'))]
    another operation x19 -> x6, other arithmetic: 35.3 us -> 4.95 us
    select_n x25 -> x0, other arithmetic: 24.2 us -> none  [the longest x24 23 us: hop(): jnp.where(position < mine, new, old)]
    transpose x0 -> x6, local copies, waits for them, and re-layouts: none -> 23.1 us  [the longest x2 15.1 us: share_in(): pieces.transpose(1, 2, 4, 0, 3, 5)]
  transfers between devices with their start and end apart: 14 -> 15, of which waited for: 6 -> 11; matrix products, arithmetic and copies ran while one was open for 17% -> 23% of each run, Pallas kernels for 0% -> 0%
where the time goes in v1:
time: 1160 us; the launch traced here: 1150 us
  waiting for transfers between devices  637 us (55%)
  blocking collectives  179 us (15%)
  local copies, waits for them, and re-layouts  168 us (14%)
  matrix products  93.7 us (8%)
  other arithmetic  51.4 us (4%)
  between operations  15.6 us (1%)
    reduce_scatter x2, waiting for transfers between devices, share_in(): mine = lax.psum_scatter(pieces, EVERY, scatter_dimension=0)  208 us
    all_gather x4, waiting for transfers between devices, spread(): return lax.all_gather(mine, EVERY)  103 us
    reduce_scatter x2, waiting for transfers between devices, share_rows(): mine = lax.psum_scatter(pieces, EVERY, scatter_dimension=0)  101 us
    psum x1, waiting for transfers between devices, per_device(): lax.psum((grad_qmap, grad_kmap, norm_grads), EVERY)  94.5 us
    all_gather x2, blocking collectives, full_maps(): pieces = lax.all_gather(part, ('fsdp', 'tensor'))  52.6 us
    all_gather x1, waiting for transfers between devices, per_device(): lax.all_gather(input_grad, 'tensor', axis=2, tiled=True).astype(jnp.float32)  49.7 us
    psum x1, blocking collectives, per_device(): lax.psum((grad_qmap, grad_kmap, norm_grads), EVERY)  39.2 us
    all_gather x2, waiting for transfers between devices, carried_in(): near = lax.all_gather(value, 'tensor')  37.1 us
  transfers between devices with their start and end apart: 15, of which 11 were waited for; matrix products, arithmetic and copies ran while one was open for 23% of the time, Pallas kernels for 0%

profile of v1, /device:TPU:0, one launch (start us, length us, event | category | flops | bytes accessed | tf_op | source)
XLA Modules:
  0.0 1146.1 jit_solution(3411823024918991780)
XLA Ops:
  20.1 26.9 %all-gather.2 = bf16[24,32,64]{2,1,0:T(8,128)(2,1)S(1)} all-gather(bf16[3,32,64]{2,1,0:T(8,128)(2,1)S(1)} %copy-done.77), channel_id=4, replica_groups=mesh['fsdp'=2,'context'=4,'tensor'=4] {'fsdp','tensor'}, dimensions={0}, use_global_device_ids=true | all-gather | bytes 110592 | tf_op jit(solution)/shard_map/all_gather | solution.py:95
  48.6 29.3 %all-gather.33.cloned.1.call-done = bf16[96,96,192]{2,1,0:T(8,128)(2,1)} async-done(((bf16[3,96,192]{2,1,0:T(8,128)(2,1)}), bf16[96,96,192]{2,1,0:T(8,128)(2,1)}) %all-gather.33.cloned.1.call-update) | async-done | bytes 3538960 | tf_op jit(solution)/shard_map/all_gather | solution.py:57
  77.9 9.6 copy.173
  87.5 9.2 reshape.511
  96.7 4.0 convert_bitcast_fusion.1
  104.9 2.2 concatenate.22
  112.7 2.2 concatenate.21
  117.0 4.1 convert_reduce_fusion.1
  121.1 2.6 convolution_convert_fusion.6
  126.2 25.6 %all-gather.1 = bf16[24,32,64]{2,1,0:T(8,128)(2,1)S(1)} all-gather(bf16[3,32,64]{2,1,0:T(8,128)(2,1)S(1)} %copy-done.78), channel_id=3, replica_groups=mesh['fsdp'=2,'context'=4,'tensor'=4] {'fsdp','tensor'}, dimensions={0}, use_global_device_ids=true | all-gather | bytes 110592 | tf_op jit(solution)/shard_map/all_gather | solution.py:95
  152.1 2.7 constant_dynamic-slice_fusion.3
  155.0 2.5 copy.259
  163.5 2.9 concatenate.19
  166.4 3.3 copy.177
  172.8 2.9 concatenate.18
  175.7 3.3 copy.176
  179.0 13.2 %all-gather.5 = f32[8,12,128]{2,1,0:T(8,128)S(1)} all-gather(f32[2,12,128]{2,1,0:T(8,128)S(1)} %get-tuple-element.62), channel_id=7, replica_groups=mesh['fsdp'=2,'context'=4,'tensor'=4] {'tensor'}, dimensions={0}, use_global_device_ids=true | all-gather | bytes 61440 | tf_op jit(solution)/shard_map/all_gather | solution.py:19
  192.3 8.3 all-gather.6
  200.6 2.6 reduce_sum.338
  203.8 2.8 pad_maximum_fusion.1
  207.9 2.5 convert_reduce_fusion
  213.8 23.7 %all-gather.43.cloned.1.call-done = bf16[6144,384]{1,0:T(8,128)(2,1)} async-done(((bf16[192,384]{1,0:T(8,128)(2,1)}), bf16[6144,384]{1,0:T(8,128)(2,1)}) %all-gather.43.cloned.1.call-update) | async-done | bytes 4718608 | tf_op jit(solution)/shard_map/all_gather | solution.py:57
  237.5 9.4 copy.188
  246.9 5.4 copy.235
  252.3 49.8 %all-gather.41.cloned.1.call-done = bf16[3072,768]{1,0:T(8,128)(2,1)} async-done(((bf16[96,768]{1,0:T(8,128)(2,1)}), bf16[3072,768]{1,0:T(8,128)(2,1)}) %all-gather.41.cloned.1.call-update) | async-done | bytes 4718608 | tf_op jit(solution)/shard_map/all_gather | solution.py:57
  302.1 6.3 copy.187
  308.4 3.3 copy.234
  311.7 4.5 fusion.87
  317.6 15.4 %all-gather.37.cloned.1.call-done = bf16[8,12,128,64]{2,3,1,0:T(8,128)(2,1)} async-done(((bf16[2,12,128,64]{2,3,1,0:T(8,128)(2,1)}), bf16[8,12,128,64]{2,3,1,0:T(8,128)(2,1)}) %all-gather.37.cloned.1.call-update) | async-done | bytes 1572880 | tf_op jit(solution)/shard_map/all_gather | solution.py:20
  342.3 8.9 fusion.10
  351.2 3.5 multiply_reduce_fusion
  360.9 37.1 %all-gather.45.cloned.1.call-done = bf16[8,12,128,64]{2,3,1,0:T(8,128)(2,1)} async-done(((bf16[2,12,128,64]{2,3,1,0:T(8,128)(2,1)}), bf16[8,12,128,64]{2,3,1,0:T(8,128)(2,1)}) %all-gather.45.cloned.1.call-update) | async-done | bytes 1572880 | tf_op jit(solution)/shard_map/all_gather | solution.py:19
  398.0 2.5 reduce_sum.365
  409.6 3.6 reshape.529
  413.1 2.4 copy.209
  416.5 4.2 select_convert_fusion
  420.6 8.8 add_convert_fusion.4
  429.5 3.1 fusion.88
  436.7 13.1 %all-gather.12 = f32[8,12,128]{2,1,0:T(8,128)S(1)} all-gather(f32[2,12,128]{2,1,0:T(8,128)S(1)} %bitcast.341), channel_id=14, replica_groups=mesh['fsdp'=2,'context'=4,'tensor'=4] {'tensor'}, dimensions={0}, use_global_device_ids=true | all-gather | bytes 61440 | tf_op jit(solution)/shard_map/all_gather | solution.py:19
  449.9 8.3 all-gather.13
  460.7 2.9 fusion.89
  474.3 6.5 convolution_convert_fusion.1
  480.8 9.8 reshape.531
  490.6 5.4 copy.210
  497.1 8.3 convolution_convert_fusion
  505.4 10.1 reshape.533
  515.5 5.5 copy.211
  521.7 2.6 convolution_convert_fusion.4
  524.3 2.3 copy.201
  534.3 4.4 fusion.35
  544.3 6.0 reshape.527
  550.3 9.8 copy.207
  560.8 8.5 all-gather.15
  570.1 27.6 %all-gather.29.cloned.1.call-done = bf16[2,1,1024,768]{3,2,1,0:T(8,128)(2,1)} async-done(((bf16[2,1,256,768]{3,2,1,0:T(8,128)(2,1)}), bf16[2,1,1024,768]{3,2,1,0:T(8,128)(2,1)}) %all-gather.29.cloned.1.call-update) | async-done | bytes 3145744 | tf_op jit(solution)/shard_map/all_gather | solution.py:227
  597.7 39.2 %psum.23 = f32[4,768]{1,0:T(4,128)S(1)} all-reduce(f32[4,768]{1,0:T(4,128)S(1)} %pad_maximum_fusion.5), channel_id=1, replica_groups=mesh['fsdp'=2,'context'=4,'tensor'=4] {'fsdp','context','tensor'}, use_global_device_ids=true, to_apply=%region_46.47 | all-reduce | flops 3072 | bytes 24576 | tf_op jit(solution)/shard_map/psum | solution.py:338
  637.6 94.5 %all-reduce.3.cloned.1.call-done = (f32[12,64,64]{2,1,0:T(8,128)}, f32[12,64,64]{2,1,0:T(8,128)}) async-done(((f32[12,64,64]{2,1,0:T(8,128)}, f32[12,64,64]{2,1,0:T(8,128)}), (f32[12,64,64]{2,1,0:T(8,128)}, f32[12,64,64]{2,1,0:T(8,128)})) %all-reduce.3.cloned.1.call-update) | async-done | bytes 393232 | tf_op jit(solution)/shard_map/psum | solution.py:338
  735.1 108.9 %reduce-scatter.9.cloned.1.call-done = bf16[1,1,96,768]{3,2,1,0:T(8,128)(2,1)} async-done(((bf16[32,1,96,768]{3,2,1,0:T(8,128)(2,1)}), bf16[1,1,96,768]{3,2,1,0:T(8,128)(2,1)}) %reduce-scatter.9.cloned.1.call-update) | async-done | bytes 147472 | tf_op jit(solution)/shard_map/reduce_scatter | solution.py:73
  844.0 11.0 all-gather.16
  855.1 100.9 %reduce-scatter.11.cloned.1.call-done = bf16[1,192,384]{2,1,0:T(8,128)(2,1)} async-done(((bf16[32,192,384]{2,1,0:T(8,128)(2,1)}), bf16[1,192,384]{2,1,0:T(8,128)(2,1)}) %reduce-scatter.11.cloned.1.call-update) | async-done | bytes 147472 | tf_op jit(solution)/shard_map/reduce_scatter | solution.py:90
  956.0 11.0 all-gather.17
  969.2 98.6 %reduce-scatter.5.cloned.1.call-done = bf16[1,3,96,192]{3,2,1,0:T(8,128)(2,1)} async-done(((bf16[32,3,96,192]{3,2,1,0:T(8,128)(2,1)}), bf16[1,3,96,192]{3,2,1,0:T(8,128)(2,1)}) %reduce-scatter.5.cloned.1.call-update) | async-done | bytes 110608 | tf_op jit(solution)/shard_map/reduce_scatter | solution.py:73
  1068.9 12.0 %all-gather.14 = bf16[1,3,384,192]{3,1,0,2:T(4,128)(2,1)S(1)} all-gather(bf16[1,3,96,192]{3,1,0,2:T(4,128)(2,1)S(1)} %copy.208), channel_id=16, replica_groups=mesh['fsdp'=2,'context'=4,'tensor'=4] {'context'}, dimensions={2}, use_global_device_ids=true | all-gather | bytes 552960 | tf_op jit(solution)/shard_map/all_gather | solution.py:74
  1082.6 49.7 %all-gather.31.cloned.1.call-done = bf16[2,1,1024,768]{3,2,1,0:T(8,128)(2,1)} async-done(((bf16[2,1,256,768]{3,2,1,0:T(8,128)(2,1)}), bf16[2,1,1024,768]{3,2,1,0:T(8,128)(2,1)}) %all-gather.31.cloned.1.call-update) | async-done | bytes 3145744 | tf_op jit(solution)/shard_map/all_gather | solution.py:336
  1132.3 5.2 convert_element_type.196
  (368 shorter events, 113.3 us)
Async XLA Ops:
  7.2 116.6 %copy-start = (bf16[768,384]{1,0:T(8,128)(2,1)S(1)}, bf16[768,384]{1,0:T(8,128)(2,1)}, u32[]{:S(2)}) copy-start(bf16[768,384]{1,0:T(8,128)(2,1)} %param.19) | copy-start | bytes 1769476
  7.2 12.9 %copy-start.77 = (bf16[3,32,64]{2,1,0:T(8,128)(2,1)S(1)}, bf16[3,32,64]{2,1,0:T(8,128)(2,1)}, u32[]{:S(2)}) copy-start(bf16[3,32,64]{2,1,0:T(8,128)(2,1)} %param.21) | copy-start | bytes 36868
  7.2 70.7 %all-gather.33.cloned.1.call-start = ((), (), s32[]{:S(2)}) async-start(), calls=%async_computation.10 | async-start | bytes 4866048 | tf_op jit(solution)/shard_map/all_gather | solution.py:57
  9.2 145.8 %all-gather.39.cloned.1.call-start = ((), (), s32[]{:S(2)}) async-start(), calls=%async_computation.13 | async-start | bytes 1216512 | tf_op jit(solution)/shard_map/all_gather | solution.py:57
  10.7 189.9 %all-gather.35.cloned.1.call-start = ((), (), s32[]{:S(2)}) async-start(), calls=%async_computation.11 | async-start | bytes 1966080 | tf_op jit(solution)/shard_map/all_gather | solution.py:19
  20.1 67.4 %copy-start.72 = (f32[768]{0:T(1024)}, f32[768]{0:T(1024)S(1)}, u32[]{:S(2)}) copy-start(f32[768]{0:T(1024)S(1)} %get-tuple-element.57) | copy-start | bytes 9220
  20.1 67.4 %copy-start.75 = (f32[768]{0:T(1024)}, f32[768]{0:T(1024)S(1)}, u32[]{:S(2)}) copy-start(f32[768]{0:T(1024)S(1)} %get-tuple-element.56) | copy-start | bytes 9220
  47.0 62.3 %copy-start.37 = (bf16[4,3,2,32,64]{4,3,2,1,0:T(8,128)(2,1)}, bf16[4,3,2,32,64]{4,3,2,1,0:T(8,128)(2,1)S(1)}, u32[]{:S(2)}) copy-start(bf16[4,3,2,32,64]{4,3,2,1,0:T(8,128)(2,1)S(1)} %copy.178) | copy-start | bytes 294916
  103.6 3.5 copy-start.4
  103.6 3.5 copy-start.58
  117.0 4.1 copy-start.14
  121.1 5.1 copy-start.78
  123.7 28.3 %copy-start.99 = (s32[2,1,4]{2,1,0:T(1,128)S(1)}, s32[2,1,4]{2,1,0:T(1,128)}, u32[]{:S(2)}) copy-start(s32[2,1,4]{2,1,0:T(1,128)} %param.15) | copy-start | bytes 100
  123.7 113.8 %all-gather.43.cloned.1.call-start = ((), (), s32[]{:S(2)}) async-start(), calls=%async_computation.15 | async-start | bytes 4866048 | tf_op jit(solution)/shard_map/all_gather | solution.py:57
  124.5 177.6 %all-gather.41.cloned.1.call-start = ((), (), s32[]{:S(2)}) async-start(), calls=%async_computation.14 | async-start | bytes 4866048 | tf_op jit(solution)/shard_map/all_gather | solution.py:57
  126.2 206.8 %all-gather.37.cloned.1.call-start = ((), (), s32[]{:S(2)}) async-start(), calls=%async_computation.12 | async-start | bytes 1966080 | tf_op jit(solution)/shard_map/all_gather | solution.py:20
  151.9 17.8 %copy-start.39 = (bf16[4,3,2,32,64]{4,3,2,1,0:T(8,128)(2,1)}, bf16[4,3,2,32,64]{4,3,2,1,0:T(8,128)(2,1)S(1)}, u32[]{:S(2)}) copy-start(bf16[4,3,2,32,64]{4,3,2,1,0:T(8,128)(2,1)S(1)} %copy.174) | copy-start | bytes 294916
  151.9 40.3 %copy-start.96 = (pred[4]{0:T(512)(128)(4,1)}, pred[4]{0:T(512)(128)(4,1)S(1)}, u32[]{:S(2)}) copy-start(pred[4]{0:T(512)(128)(4,1)S(1)} %iota_compare_fusion.4) | copy-start | bytes 16
  151.9 51.7 %copy-start.94 = (pred[4]{0:T(512)(128)(4,1)}, pred[4]{0:T(512)(128)(4,1)S(1)}, u32[]{:S(2)}) copy-start(pred[4]{0:T(512)(128)(4,1)S(1)} %iota_compare_fusion.3) | copy-start | bytes 16
  155.0 52.9 %copy-start.69 = (pred[2,256,256]{1,2,0:T(8,128)(4,1)}, pred[2,256,256]{1,2,0:T(8,128)(4,1)S(1)}, u32[]{:S(2)}) copy-start(pred[2,256,256]{1,2,0:T(8,128)(4,1)S(1)} %broadcast_or_fusion) | copy-start | bytes 393220
  162.2 4.2 copy-start.6
  162.2 4.2 copy-start.60
  171.5 4.2 copy-start.2
  171.5 4.2 copy-start.56
  203.2 194.8 %all-gather.45.cloned.1.call-start = ((), (), s32[]{:S(2)}) async-start(), calls=%async_computation.16 | async-start | bytes 1966080 | tf_op jit(solution)/shard_map/all_gather | solution.py:19
  207.9 2.5 copy-start.64
  207.9 4.2 copy-start.15
  210.4 3.4 copy-start.71
  302.1 9.6 slice-start
  308.4 3.3 copy-start.24
  308.4 3.3 slice-start.1
  311.7 4.6 copy-start.30
  311.7 4.6 copy-start.97
  316.2 16.7 %copy-start.95 = (pred[4]{0:T(512)(128)(4,1)S(1)}, pred[4]{0:T(512)(128)(4,1)}, u32[]{:S(2)}) copy-start(pred[4]{0:T(512)(128)(4,1)} %copy-done.94) | copy-start | bytes 16
  336.4 3.8 slice-start.2
  337.1 3.1 slice-start.3
  338.0 4.4 copy-start.100
  339.9 14.9 %copy-start.32 = (f32[512,768]{1,0:T(8,128)}, f32[512,768]{1,0:T(8,128)S(1)}, u32[]{:S(2)}) copy-start(f32[512,768]{1,0:T(8,128)S(1)} %get-tuple-element.92) | copy-start | bytes 4718596
  339.9 14.8 %copy-start.79 = (f32[512]{0:T(512)}, f32[512]{0:T(512)S(1)}, u32[]{:S(2)}) copy-start(f32[512]{0:T(512)S(1)} %broadcast_multiply_fusion) | copy-start | bytes 6148
  340.2 14.5 %copy-start.85 = (f32[512]{0:T(512)}, f32[512]{0:T(512)S(1)}, u32[]{:S(2)}) copy-start(f32[512]{0:T(512)S(1)} %fusion.68) | copy-start | bytes 6148
  351.2 3.6 copy-start.101
  360.8 103.2 %all-gather.47.cloned.1.call-start = ((), (), s32[]{:S(2)}) async-start(), calls=%async_computation.17 | async-start | bytes 1966080 | tf_op jit(solution)/shard_map/all_gather | solution.py:20
  400.6 160.3 %reduce-scatter.7.cloned.1.call-start = ((), (), s32[]{:S(2)}) async-start(), calls=%async_computation.7 | async-start | bytes 1216512 | tf_op jit(solution)/shard_map/reduce_scatter | solution.py:90
  401.0 6.8 copy-start.44
  401.0 6.8 copy-start.52
  415.6 182.1 %all-gather.29.cloned.1.call-start = ((), (), s32[]{:S(2)}) async-start(), calls=%async_computation.4 | async-start | bytes 3932160 | tf_op jit(solution)/shard_map/all_gather | solution.py:227
  416.4 4.2 copy-start.33
  429.5 302.7 %all-reduce.3.cloned.1.call-start = ((), (), s32[]{:S(2)}) async-start(), calls=%async_computation.18 | async-start | bytes 1572864 | tf_op jit(solution)/shard_map/psum | solution.py:338
  429.5 3.1 copy-start.29
  429.5 3.1 copy-start.63
  435.7 14.1 %copy-start.98 = (pred[4]{0:T(512)(128)(4,1)S(1)}, pred[4]{0:T(512)(128)(4,1)}, u32[]{:S(2)}) copy-start(pred[4]{0:T(512)(128)(4,1)} %iota_compare_fusion.2) | copy-start | bytes 16
  435.7 22.5 %copy-start.93 = (pred[4]{0:T(512)(128)(4,1)S(1)}, pred[4]{0:T(512)(128)(4,1)}, u32[]{:S(2)}) copy-start(pred[4]{0:T(512)(128)(4,1)} %iota_compare_fusion.1) | copy-start | bytes 16
  435.7 22.6 %copy-start.57 = (f32[512,12]{0,1:T(8,128)S(1)}, f32[512,12]{0,1:T(8,128)}, u32[]{:S(2)}) copy-start(f32[512,12]{0,1:T(8,128)} %copy-done.56) | copy-start | bytes 73732
  435.7 22.6 %copy-start.61 = (f32[512,12]{0,1:T(8,128)S(1)}, f32[512,12]{0,1:T(8,128)}, u32[]{:S(2)}) copy-start(f32[512,12]{0,1:T(8,128)} %copy-done.60) | copy-start | bytes 73732
  459.5 4.1 copy-start.17
  460.7 2.9 copy-start.31
  473.8 370.2 %reduce-scatter.9.cloned.1.call-start = ((), (), s32[]{:S(2)}) async-start(), calls=%async_computation.8 | async-start | bytes 4866048 | tf_op jit(solution)/shard_map/reduce_scatter | solution.py:73
  496.0 460.0 %reduce-scatter.11.cloned.1.call-start = ((), (), s32[]{:S(2)}) async-start(), calls=%async_computation.9 | async-start | bytes 4866048 | tf_op jit(solution)/shard_map/reduce_scatter | solution.py:90
  521.0 546.9 %reduce-scatter.5.cloned.1.call-start = ((), (), s32[]{:S(2)}) async-start(), calls=%async_computation.6 | async-start | bytes 4866048 | tf_op jit(solution)/shard_map/reduce_scatter | solution.py:73
  521.7 4.9 copy-start.12
  533.5 5.2 copy-start.49
  534.3 4.5 copy-start.23
  560.1 572.2 %all-gather.31.cloned.1.call-start = ((), (), s32[]{:S(2)}) async-start(), calls=%async_computation.5 | async-start | bytes 3932160 | tf_op jit(solution)/shard_map/all_gather | solution.py:336
  1132.3 5.2 copy-start.35
  (57 other events, 82.4 us)
Sparse Core Ops, SparseCore 0:
  11.4 66.4 all-gather.32
  81.3 52.3 all-gather.38
  135.2 37.0 all-gather.34
  175.0 62.4 all-gather.42
  240.2 61.8 all-gather.40
  303.8 29.1 all-gather.36
  360.9 37.0 all-gather.44
  400.7 29.6 all-gather.46
  436.1 97.0 reduce-scatter.6
  535.1 62.5 all-gather.28
  603.1 129.0 all-reduce.2
  737.5 106.4 reduce-scatter.8
  849.5 106.4 reduce-scatter.10
  961.3 106.4 reduce-scatter.4
  1069.9 62.4 all-gather.30

commit v2 on v1

--- a/solution.py
+++ b/solution.py
@@ -1,6 +1,10 @@
+import functools
+
 import jax
 import jax.numpy as jnp
 from jax import lax
+from jax.experimental import pallas as pl
+from jax.experimental.pallas import tpu as pltpu
 from jax.sharding import PartitionSpec as P
 
 BLK = 256
@@ -105,7 +109,373 @@
     return lax.dynamic_slice_in_dim(mine, lax.axis_index("fsdp") * (rows // fsdp), rows // fsdp, 1)
 
 
+MESH = pl.DeviceIdType.MESH
+bf16 = jnp.bfloat16
+f32 = jnp.float32
+
+
+def whereabouts():
+    return tuple(lax.axis_index(name) for name in EVERY)
+
+
+def neighbours(f, c, t):
+    n = c * 4 + t
+    peers = [(1 - f, c, t)]
+    for k in range(1, 16):
+        other = lax.rem(n + k, 16)
+        peers.append((f, other // 4, lax.rem(other, 4)))
+    return peers
+
+
+def meet(f, c, t):
+    barrier = pltpu.get_barrier_semaphore()
+    peers = neighbours(f, c, t)
+    for peer in peers:
+        pl.semaphore_signal(barrier, inc=1, device_id=peer, device_id_type=MESH)
+    pl.semaphore_wait(barrier, len(peers))
+
+
+def send(src, dst, send_sem, recv_sem, peer):
+    copy = pltpu.make_async_remote_copy(
+        src_ref=src, dst_ref=dst, send_sem=send_sem, recv_sem=recv_sem,
+        device_id=peer, device_id_type=MESH,
+    )
+    copy.start()
+    return copy
+
+
+def arrived(ref, sem):
+    pltpu.make_async_copy(ref, ref, sem).wait()
+
+
+def at(start, size, unit):
+    return pl.ds(pl.multiple_of(start, unit), size)
+
+
+def half(ref, m, f):
+    if len(ref.shape) == 4:
+        w = ref.shape[3] // 2
+        return ref.at[:, :, :, at(f * w, w, 128)]
+    if len(ref.shape) == 3 and m == 1:
+        w = ref.shape[2] // 2
+        return ref.at[:, :, at(f * w, w, 128)]
+    if m == 0:
+        w = ref.shape[2] // 2
+        return ref.at[:, :, at(f * w, w, 128)]
+    if m == 1:
+        w = ref.shape[1] // 2
+        return ref.at[:, at(f * w, w, 128)]
+    w = ref.shape[0] // 2
+    return ref.at[at(f * w, w, 16), :]
+
+
+def shard(ref, m, f, t):
+    if m == 0:
+        w, h = ref.shape[2] // 2, ref.shape[1] // 4
+        return ref.at[:, at(t * h, h, 16), at(f * w, w, 128)]
+    if m == 1:
+        w, h = ref.shape[1] // 2, ref.shape[0] // 4
+        return ref.at[at(t * h, h, 16), at(f * w, w, 128)]
+    h, w = ref.shape[0] // 2, ref.shape[1] // 4
+    return ref.at[at(f * h, h, 16), at(t * w, w, 128)]
+
+
+def piece(ref, m, f, c, t):
+    if m == 0:
+        w, h = ref.shape[2] // 2, ref.shape[1] // 16
+        return ref.at[:, at(t * 4 * h + c * h, h, 16), at(f * w, w, 128)]
+    if m == 1:
+        w, h = ref.shape[1] // 2, ref.shape[0] // 16
+        return ref.at[at(t * 4 * h + c * h, h, 16), at(f * w, w, 128)]
+    h, w = ref.shape[0] // 8, ref.shape[1] // 4
+    return ref.at[at(f * 4 * h + c * h, h, 16), at(t * w, w, 128)]
+
+
+def quarter(ref, m, c):
+    if m == 0:
+        h = ref.shape[1] // 4
+        return ref.at[:, at(c * h, h, 16), :]
+    h = ref.shape[0] // 4
+    return ref.at[at(c * h, h, 16), :]
+
+
+def gather_kernel(*refs):
+    shards, fulls = refs[:4], refs[4:8]
+    local_sem, send_sem, z_sem, xy_sem, pair_sem = refs[8:]
+    f, c, t = whereabouts()
+    meet(f, c, t)
+    partner = (1 - f, c, t)
+    started = []
+    local = []
+    for m in range(4):
+        for k in range(1, 4):
+            peer = (f, c, lax.rem(t + k, 4))
+            started.append(send(quarter(shards[m], m, c), piece(fulls[m], m, f, c, t),
+                                send_sem.at[m], z_sem.at[m, k], peer))
+    for m in range(4):
+        copy = pltpu.make_async_copy(shards[m], shard(fulls[m], m, f, t), local_sem.at[m])
+        copy.start()
+        local.append(copy)
+        started.append(send(shards[m], shard(fulls[m], m, f, t), send_sem.at[m], pair_sem.at[m], partner))
+    for m in range(4):
+        for k in range(1, 4):
+            source = lax.rem(t + 4 - k, 4)
+            got = piece(fulls[m], m, f, c, source)
+            arrived(got, z_sem.at[m, k])
+            for j in range(1, 4):
+                started.append(send(got, got, send_sem.at[m], xy_sem.at[m, k, j], (f, c ^ j, t)))
+            started.append(send(got, got, send_sem.at[m], pair_sem.at[m], partner))
+    for m in range(4):
+        for k in range(1, 4):
+            source = lax.rem(t + 4 - k, 4)
+            for j in range(1, 4):
+                got = piece(fulls[m], m, f, c ^ j, source)
+                arrived(got, xy_sem.at[m, k, j])
+                started.append(send(got, got, send_sem.at[m], pair_sem.at[m], partner))
+    for m in range(4):
+        arrived(half(fulls[m], m, 1 - f), pair_sem.at[m])
+        local[m].wait()
+    for copy in started:
+        copy.wait_send()
+
+
+def gather_weights(shards):
+    d = shards[0].shape[2] * 2
+    ff = shards[2].shape[1] * 4
+    shapes = [(3, d, d), (d, d), (d, ff), (d, ff)]
+    dma = pltpu.SemaphoreType.DMA
+    return pl.pallas_call(
+        gather_kernel,
+        out_shape=[jax.ShapeDtypeStruct(s, bf16) for s in shapes],
+        in_specs=[pl.BlockSpec(memory_space=pl.ANY)] * 4,
+        out_specs=[pl.BlockSpec(memory_space=pltpu.VMEM)] * 4,
+        scratch_shapes=[dma((4,)), dma((4,)), dma((4, 4)), dma((4, 4, 4)), dma((4,))],
+        compiler_params=pltpu.CompilerParams(collective_id=0, has_side_effects=True, vmem_limit_bytes=60 << 20),
+        name="gather_weights",
+    )(*shards)
+
+
+def scan_kernel(backward, s_ref, z_ref, p_ref, q_ref, s_in, z_in, s_out, z_out, own_sem, send_sem, s_sem, z_sem, p_sem, q_sem):
+    f, c, t = whereabouts()
+    n = c * 4 + t
+    peers = neighbours(f, c, t)
+    meet(f, c, t)
+    rows = s_ref.shape[1] // 16
+    started = []
+    for k in range(1, 16):
+        other = lax.rem(n + k, 16)
+        started.append(send(s_ref.at[:, at(other * rows, rows, 16), :], s_in.at[n], send_sem, s_sem, peers[k]))
+        started.append(send(z_ref.at[other], z_in.at[n], send_sem, z_sem, peers[k]))
+    a = pltpu.make_async_copy(s_ref.at[:, at(n * rows, rows, 16), :], s_in.at[n], own_sem.at[0])
+    b = pltpu.make_async_copy(z_ref.at[n], z_in.at[n], own_sem.at[1])
+    a.start()
+    b.start()
+    a.wait()
+    b.wait()
+    arrived(s_in.at[pl.ds(0, 15)], s_sem)
+    arrived(z_in.at[pl.ds(0, 15)], z_sem)
+    total = jnp.zeros(s_in.shape[1:], f32)
+    sums = jnp.zeros(z_in.shape[1:], f32)
+    order = range(15, -1, -1) if backward else range(16)
+    for i in order:
+        s_out[i] = total.astype(bf16)
+        z_out[i] = sums
+        total = total + s_in[i].astype(f32)
+        sums = sums + z_in[i]
+    back = []
+    for k in range(1, 16):
+        other = lax.rem(n + k, 16)
+        back.append(send(s_out.at[other], p_ref.at[:, at(n * rows, rows, 16), :], send_sem, p_sem, peers[k]))
+        back.append(send(z_out.at[other], q_ref.at[n], send_sem, q_sem, peers[k]))
+    a = pltpu.make_async_copy(s_out.at[n], p_ref.at[:, at(n * rows, rows, 16), :], own_sem.at[0])
+    b = pltpu.make_async_copy(z_out.at[n], q_ref.at[n], own_sem.at[1])
+    a.start()
+    b.start()
+    a.wait()
+    b.wait()
+    arrived(s_in.at[pl.ds(0, 15)], p_sem)
+    arrived(z_in.at[pl.ds(0, 15)], q_sem)
+    for copy in started + back:
+        copy.wait_send()
+
+
+def scan_states(states, sums, backward):
+    seqs, rows, lanes = states.shape
+    dma = pltpu.SemaphoreType.DMA
+    return pl.pallas_call(
+        functools.partial(scan_kernel, backward),
+        out_shape=[jax.ShapeDtypeStruct(states.shape, bf16), jax.ShapeDtypeStruct(sums.shape, f32)],
+        in_specs=[pl.BlockSpec(memory_space=pltpu.VMEM)] * 2,
+        out_specs=[pl.BlockSpec(memory_space=pltpu.VMEM)] * 2,
+        scratch_shapes=[
+            pltpu.VMEM((16, seqs, rows // 16, lanes), bf16), pltpu.VMEM((16,) + sums.shape[1:], f32),
+            pltpu.VMEM((16, seqs, rows // 16, lanes), bf16), pltpu.VMEM((16,) + sums.shape[1:], f32),
+            dma((2,)), dma(()), dma(()), dma(()), dma(()), dma(()),
+        ],
+        compiler_params=pltpu.CompilerParams(
+            collective_id=2 if backward else 1, has_side_effects=True, vmem_limit_bytes=32 << 20
+        ),
+        name="scan_states",
+    )(states, sums)
+
+
+def summed(m, t_count, refs):
+    total = refs[0][...].astype(f32)
+    for ref in refs[1:]:
+        total = total + ref[...].astype(f32)
+    return total
+
+
+def reduce_kernel(*refs):
+    grads, small, rows_out, rows_in = refs[:4], refs[4], refs[5], refs[6]
+    outs, small_out, all_out, all_in = refs[7:11], refs[11], refs[12], refs[13]
+    own, pair_in, sums, xy_in, z_in, last = (refs[14 + 4 * i : 18 + 4 * i] for i in range(6))
+    small_pair, small_own, small_in, small_sum = refs[38:42]
+    local_sem, send_sem, rows_sem, pair_sem, xy_sem, z_sem, last_sem, small_sem = refs[42:]
+    f, c, t = whereabouts()
+    n = c * 4 + t
+    peers = neighbours(f, c, t)
+    partner = peers[0]
+    meet(f, c, t)
+    started = []
+    for i, (src, dst) in enumerate(((rows_out, all_out), (rows_in, all_in))):
+        for k in range(1, 4):
+            peer = (f, c, lax.rem(t + k, 4))
+            started.append(send(src, dst.at[:, t], send_sem, rows_sem.at[i, k], peer))
+    copies = []
+    for i, (src, dst) in enumerate(((rows_out, all_out), (rows_in, all_in))):
+        copy = pltpu.make_async_copy(src, dst.at[:, t], local_sem.at[i])
+        copy.start()
+        copies.append(copy)
+    for m in range(4):
+        started.append(send(half(grads[m], m, 1 - f), pair_in[m], send_sem, pair_sem.at[m], partner))
+    started.append(send(small, small_pair, send_sem, small_sem.at[0], partner))
+    for m in range(4):
+        copy = pltpu.make_async_copy(half(grads[m], m, f), own[m], local_sem.at[2 + m])
+        copy.start()
+        copies.append(copy)
+    for copy in copies:
+        copy.wait()
+    arrived(small_pair, small_sem.at[0])
+    small_own[...] = (small[...] + small_pair[...]).astype(bf16)
+    for k in range(1, 16):
+        other = lax.rem(n + k, 16)
+        started.append(send(small_own.at[other], small_in.at[n], send_sem, small_sem.at[1], peers[k]))
+    copy = pltpu.make_async_copy(small_own.at[n], small_in.at[n], local_sem.at[6])
+    copy.start()
+    copy.wait()
+    for m in range(4):
+        arrived(pair_in[m], pair_sem.at[m])
+        own[m][...] = (own[m][...].astype(f32) + pair_in[m][...].astype(f32)).astype(bf16)
+        for j in range(1, 4):
+            started.append(send(context_part(own[m], m, c ^ j), xy_in[m].at[j - 1], send_sem, xy_sem.at[m, j], (f, c ^ j, t)))
+    arrived(small_in.at[pl.ds(0, 15)], small_sem.at[1])
+    total = jnp.zeros(small_in.shape[1:], f32)
+    for i in range(16):
+        total = total + small_in[i].astype(f32)
+    small_sum[...] = total
+    for k in range(1, 16):
+        started.append(send(small_sum, small_out.at[n], send_sem, small_sem.at[2], peers[k]))
+    copy = pltpu.make_async_copy(small_sum, small_out.at[n], local_sem.at[6])
+    copy.start()
+    copy.wait()
+    for m in range(4):
+        copy = pltpu.make_async_copy(context_part(own[m], m, c), sums[m], local_sem.at[7 + m])
+        copy.start()
+        copy.wait()
+        for j in range(1, 4):
+            arrived(xy_in[m].at[j - 1], xy_sem.at[m, j])
+        total = sums[m][...].astype(f32)
+        for j in range(3):
+            total = total + xy_in[m][j].astype(f32)
+        sums[m][...] = total.astype(bf16)
+        for k in range(1, 4):
+            other = lax.rem(t + k, 4)
+            started.append(send(tensor_part(sums[m], m, other), z_in[m].at[k - 1], send_sem, z_sem.at[m, k], (f, c, other)))
+    for m in range(4):
+        copy = pltpu.make_async_copy(tensor_part(sums[m], m, t), last[m], local_sem.at[11 + m])
+        copy.start()
+        copy.wait()
+        for k in range(1, 4):
+            arrived(z_in[m].at[k - 1], z_sem.at[m, k])
+        total = last[m][...].astype(f32)
+        for k in range(3):
+            total = total + z_in[m][k].astype(f32)
+        last[m][...] = total.astype(bf16)
+        for j in range(1, 4):
+            started.append(send(last[m], quarter(outs[m], m, c), send_sem, last_sem.at[m, j], (f, c ^ j, t)))
+        copy = pltpu.make_async_copy(last[m], quarter(outs[m], m, c), local_sem.at[15 + m])
+        copy.start()
+        copy.wait()
+    for m in range(4):
+        for j in range(1, 4):
+            arrived(last[m], last_sem.at[m, j])
+    arrived(small_out.at[pl.ds(0, 15)], small_sem.at[2])
+    for i, dst in enumerate((all_out, all_in)):
+        for k in range(1, 4):
+            arrived(dst.at[:, 0], rows_sem.at[i, k])
+    for copy in started:
+        copy.wait_send()
+
+
+def context_part(ref, m, c):
+    if m == 0:
+        h = ref.shape[2] // 4
+        return ref.at[:, :, at(c * h, h, 16), :]
+    if m == 1:
+        h = ref.shape[1] // 4
+        return ref.at[:, at(c * h, h, 16), :]
+    h = ref.shape[0] // 4
+    return ref.at[at(c * h, h, 16), :]
+
+
+def tensor_part(ref, m, t):
+    if m == 0:
+        return ref.at[:, t]
+    if m == 1:
+        return ref.at[t]
+    w = ref.shape[1] // 4
+    return ref.at[:, at(t * w, w, 128)]
+
+
+def reduce_grads(grads, small, rows_out, rows_in):
+    dma = pltpu.SemaphoreType.DMA
+    d, ff = grads[2].shape
+    own = [(3, 4, d // 4, d // 2), (4, d // 4, d // 2), (d // 2, ff), (d // 2, ff)]
+    sums = [(3, 4, d // 16, d // 2), (4, d // 16, d // 2), (d // 8, ff), (d // 8, ff)]
+    last = [(3, d // 16, d // 2), (d // 16, d // 2), (d // 8, ff // 4), (d // 8, ff // 4)]
+    outs = [(3, d // 4, d // 2), (d // 4, d // 2), (d // 2, ff // 4), (d // 2, ff // 4)]
+    piece_rows = small.shape[1:]
+    scratch = []
+    for m in range(4):
+        pass
+    scratch += [pltpu.VMEM(s, bf16) for s in own]
+    scratch += [pltpu.VMEM(s, bf16) for s in own]
+    scratch += [pltpu.VMEM(s, bf16) for s in sums]
+    scratch += [pltpu.VMEM((3,) + s, bf16) for s in sums]
+    scratch += [pltpu.VMEM((3,) + s, bf16) for s in last]
+    scratch += [pltpu.VMEM(s, bf16) for s in last]
+    scratch += [
+        pltpu.VMEM(small.shape, f32), pltpu.VMEM(small.shape, bf16), pltpu.VMEM(small.shape, bf16),
+        pltpu.VMEM(piece_rows, f32),
+    ]
+    scratch += [dma((19,)), dma(()), dma((2, 4)), dma((4,)), dma((4, 4)), dma((4, 4)), dma((4, 4)), dma((3,))]
+    spread_rows = (rows_out.shape[0], 4) + rows_out.shape[1:]
+    return pl.pallas_call(
+        reduce_kernel,
+        out_shape=[jax.ShapeDtypeStruct(s, bf16) for s in outs]
+        + [jax.ShapeDtypeStruct(small.shape, f32)]
+        + [jax.ShapeDtypeStruct(spread_rows, bf16)] * 2,
+        in_specs=[pl.BlockSpec(memory_space=pltpu.VMEM)] * 7,
+        out_specs=[pl.BlockSpec(memory_space=pltpu.VMEM)] * 7,
+        scratch_shapes=scratch,
+        compiler_params=pltpu.CompilerParams(collective_id=3, has_side_effects=True, vmem_limit_bytes=60 << 20),
+        name="reduce_grads",
+    )(*grads, small, rows_out, rows_in)
+
+
 def per_device(
+    meshed,
     inputs,
     cotangent,
     picture_starts,
@@ -135,10 +505,14 @@
     position = jnp.arange(BLK, dtype=jnp.int32)
     causal = position[None, :] <= position[:, None]
 
-    in_full = full_in(qkv_weight)
-    out_full = full_rows(out_weight)
-    up_full = full_in(up_weight[None])[0]
-    down_full = full_rows(down_weight)
+    shards = (qkv_weight.transpose(0, 2, 1), out_weight, up_weight, down_weight.T)
+    if meshed:
+        in_full, out_full, up_full, down_full = gather_weights(shards)
+    else:
+        in_full = full_in(qkv_weight).transpose(0, 2, 1)
+        out_full = full_rows(out_weight)
+        up_full = full_in(up_weight[None])[0]
+        down_full = full_rows(down_weight).T
     qmap_full, kmap_full = full_maps(query_map), full_maps(key_map)
     norms = lax.all_gather(jnp.stack([first_gain, first_bias, second_gain, second_bias]), "fsdp", axis=1, tiled=True)
     gain_first, bias_first, gain_second, bias_second = norms.astype(jnp.float32)
@@ -158,7 +532,7 @@
     normed_one = layer_norm(source, gain_first, bias_first)
     normed_low = normed_one.astype(jnp.bfloat16)
     projected = jnp.einsum(
-        "rd,cde->cre", normed_low, in_full, preferred_element_type=jnp.float32
+        "rd,ced->cre", normed_low, in_full, preferred_element_type=jnp.float32
     ).astype(jnp.bfloat16)
     heads_local = projected.shape[2] // head_size
     queries = projected[0].reshape(row_count, heads_local, head_size)
@@ -192,15 +566,7 @@
     key_sums = jnp.sum(key_blocks.astype(jnp.float32), 1).reshape(
         seq_count, blocks_local, heads_local, feat_size
     )
-    state_total = jnp.sum(states, 1)
-    sums_total = jnp.sum(key_sums, 1)
-    carried = carried_in(state_total.astype(jnp.bfloat16), False)
-    carried_sums = carried_in(sums_total, False)
-    prior_states = (carried[:, None] + prefix_before(states)).astype(jnp.bfloat16)
-    prior_states = prior_states.reshape(block_total, heads_local, feat_size, head_size)
-    prior_sums = (carried_sums[:, None] + prefix_before(key_sums)).reshape(
-        block_total, heads_local, feat_size
-    )
+    prior_states, prior_sums = carried_states(meshed, states, key_sums, False)
     numerator = jnp.einsum(
         "nhts,nshe->nthe", weights_low, value_blocks, preferred_element_type=jnp.float32
     )
@@ -222,16 +588,15 @@
     normed_two_low = normed_two.astype(jnp.bfloat16)
     hidden_pre = jnp.dot(normed_two_low, up_full, preferred_element_type=jnp.float32)
     hidden_low = gelu_tanh(hidden_pre).astype(jnp.bfloat16)
-    branch = jnp.dot(hidden_low, down_full, preferred_element_type=jnp.float32)
-    output = (middle + branch).astype(jnp.bfloat16).reshape(micro, seq_local, span, model_width)
-    output = lax.all_gather(output, "tensor", axis=2, tiled=True)
+    branch = jnp.einsum("rk,dk->rd", hidden_low, down_full, preferred_element_type=jnp.float32)
+    output = (middle + branch).astype(jnp.bfloat16)
     upstream_low = own(cotangent)
     upstream = upstream_low.astype(jnp.float32)
     grad_down = jnp.einsum(
-        "rk,rd->kd", hidden_low, upstream_low, preferred_element_type=jnp.float32
+        "rk,rd->dk", hidden_low, upstream_low, preferred_element_type=jnp.float32
     )
     hidden_grad = jnp.einsum(
-        "rd,kd->rk", upstream_low, down_full, preferred_element_type=jnp.float32
+        "rd,dk->rk", upstream_low, down_full, preferred_element_type=jnp.float32
     )
     gelu_result, gelu_pull = jax.vjp(gelu_tanh, hidden_pre)
     pre_grad = gelu_pull(hidden_grad)[0].astype(jnp.bfloat16)
@@ -280,15 +645,7 @@
         "nthf,nth->nhf", query_blocks.astype(jnp.float32), denom_grad, precision=highest
     )
     prior_sums_grad = prior_sums_grad.reshape(seq_count, blocks_local, heads_local, feat_size)
-    grad_total = jnp.sum(prior_grad, 1)
-    grad_sums_total = jnp.sum(prior_sums_grad, 1)
-    later_states = carried_in(grad_total.astype(jnp.bfloat16), True)
-    later_sums = carried_in(grad_sums_total, True)
-    state_grad = (later_states[:, None] + suffix_after(prior_grad)).astype(jnp.bfloat16)
-    state_grad = state_grad.reshape(block_total, heads_local, feat_size, head_size)
-    sums_grad = (later_sums[:, None] + suffix_after(prior_sums_grad)).reshape(
-        block_total, heads_local, feat_size
-    )
+    state_grad, sums_grad = carried_states(meshed, prior_grad, prior_sums_grad, True)
     key_grad = key_grad + jnp.einsum(
         "nshe,nhfe->nshf", value_blocks, state_grad, preferred_element_type=jnp.float32
     )
@@ -324,34 +681,86 @@
         ]
     ).astype(jnp.bfloat16)
     grad_in = jnp.einsum(
-        "rd,cre->cde", normed_low, projected_grad, preferred_element_type=jnp.float32
+        "rd,cre->ced", normed_low, projected_grad, preferred_element_type=jnp.float32
     )
     normed_one_grad = jnp.einsum(
-        "cre,cde->rd", projected_grad, in_full, preferred_element_type=jnp.float32
+        "cre,ced->rd", projected_grad, in_full, preferred_element_type=jnp.float32
     )
     first_result, first_pull = jax.vjp(layer_norm, source, gain_first, bias_first)
     source_part, grad_gain_first, grad_bias_first = first_pull(normed_one_grad)
     input_grad = (middle_grad + source_part).astype(jnp.bfloat16)
-    input_grad = input_grad.reshape(micro, seq_local, span, model_width)
-    input_grad = lax.all_gather(input_grad, "tensor", axis=2, tiled=True).astype(jnp.float32)
     norm_grads = jnp.stack([grad_gain_first, grad_bias_first, grad_gain_second, grad_bias_second])
-    grad_qmap, grad_kmap, norm_grads = lax.psum((grad_qmap, grad_kmap, norm_grads), EVERY)
     share = first_gain.shape[0]
+    if not meshed:
+        grad_qmap, grad_kmap, norm_grads = lax.psum((grad_qmap, grad_kmap, norm_grads), EVERY)
+        norm_grads = lax.dynamic_slice_in_dim(norm_grads, lax.axis_index("fsdp") * share, share, 1)
+        rows = (output.reshape(micro, seq_local, span, -1), input_grad.reshape(micro, seq_local, span, -1))
+        all_out, all_in = (lax.all_gather(part, "tensor", axis=2, tiled=True) for part in rows)
+        return (
+            all_out,
+            all_in.astype(jnp.float32),
+            share_in(grad_in.transpose(0, 2, 1)),
+            share_rows(grad_out),
+            share_in(grad_up[None])[0],
+            share_rows(grad_down.T),
+            own_maps(grad_qmap),
+            own_maps(grad_kmap),
+            norm_grads[0],
+            norm_grads[1],
+            norm_grads[2],
+            norm_grads[3],
+        )
+    heads = grad_qmap.shape[0]
+    pairs = jnp.stack([grad_qmap, grad_kmap]).reshape(heads, 2, head_size, head_size)
+    pairs = pairs.transpose(0, 2, 1, 3).reshape(-1, 2 * head_size)
+    small = jnp.concatenate([pairs, norm_grads.reshape(-1, 2 * head_size)])
+    small = jnp.pad(small, ((0, -small.shape[0] % 256), (0, 0))).reshape(16, -1, 2 * head_size)
+    quarter_rows = model_width // 4
+    grads = (
+        grad_in.astype(bf16).reshape(3, 4, quarter_rows, model_width),
+        grad_out.astype(bf16).reshape(4, quarter_rows, model_width),
+        grad_up.astype(bf16),
+        grad_down.astype(bf16),
+    )
+    share_0, share_1, share_2, share_3, small, all_out, all_in = reduce_grads(
+        grads, small, output.reshape(micro, span, model_width), input_grad.reshape(micro, span, model_width)
+    )
+    small = small.reshape(-1, 2 * head_size)
+    pairs = small[: heads * head_size].reshape(heads, head_size, 2, head_size)
+    pairs = pairs.transpose(0, 2, 1, 3).reshape(2, heads, head_size, head_size)
+    norm_grads = small[heads * head_size :].reshape(-1)[: norm_grads.size].reshape(norm_grads.shape)
     norm_grads = lax.dynamic_slice_in_dim(norm_grads, lax.axis_index("fsdp") * share, share, 1)
     return (
-        output,
-        input_grad,
-        share_in(grad_in),
-        share_rows(grad_out),
-        share_in(grad_up[None])[0],
-        share_rows(grad_down),
-        own_maps(grad_qmap),
-        own_maps(grad_kmap),
+        all_out.reshape(inputs.shape),
+        all_in.reshape(inputs.shape).astype(jnp.float32),
+        share_0.astype(jnp.float32).transpose(0, 2, 1),
+        share_1.astype(jnp.float32),
+        share_2.astype(jnp.float32),
+        share_3.astype(jnp.float32).T,
+        own_maps(pairs[0]),
+        own_maps(pairs[1]),
         norm_grads[0],
         norm_grads[1],
         norm_grads[2],
         norm_grads[3],
     )
+
+
+def carried_states(meshed, states, sums, backward):
+    seqs, blocks, heads, feats, head = states.shape
+    if not meshed:
+        inside = suffix_after if backward else prefix_before
+        carried = carried_in(jnp.sum(states, 1).astype(bf16), backward)
+        carried_sums = carried_in(jnp.sum(sums, 1), backward)
+        states = (carried[:, None] + inside(states)).astype(bf16)
+        sums = carried_sums[:, None] + inside(sums)
+        return states.reshape((-1,) + states.shape[2:]), sums.reshape((-1,) + sums.shape[2:])
+    packed = states.reshape(seqs, heads // 2, 2, feats, head).transpose(0, 1, 3, 2, 4)
+    packed = packed.reshape(seqs, heads // 2 * feats, 2 * head).astype(bf16)
+    rows = jnp.pad(sums.reshape(seqs, heads, feats).transpose(1, 0, 2), ((0, 16 - heads), (0, 8 - seqs), (0, 0)))
+    packed, rows = scan_states(packed, rows, backward)
+    packed = packed.reshape(seqs, heads // 2, feats, 2, head).transpose(0, 1, 3, 2, 4)
+    return packed.reshape(seqs, heads, feats, head), rows[:heads, :seqs].transpose(1, 0, 2)
 
 
 def solution(mesh):
@@ -384,6 +793,7 @@
         P("fsdp"),
         P("fsdp"),
     )
+    sizes = tuple(mesh.shape[name] for name in EVERY)
     return jax.shard_map(
-        per_device, mesh=mesh, in_specs=in_specs, out_specs=out_specs, check_vma=False
-    )
+        functools.partial(per_device, sizes == (2, 4, 4)), mesh=mesh, in_specs=in_specs, out_specs=out_specs, check_vma=False
+    )

time: 1160 us -> 591 us (0.51)
  waiting for transfers between devices: 637 us -> 0 us
  Pallas kernels: 0 us -> 340 us
  blocking collectives: 179 us -> 52.5 us
  local copies, waits for them, and re-layouts: 168 us -> 67.6 us
  matrix products: 93.7 us -> 79.1 us
  between operations: 15.6 us -> 2.13 us
    pallas_call x0 -> x4, Pallas kernels: none -> 340 us  [the longest x1 210 us: reduce_grads(): pl.pallas_call(reduce_kernel, out_shape=[jax.ShapeDtypeStruct(s, bf16) fo...]
    reduce_scatter x4 -> x0, waiting for transfers between devices: 309 us -> none  [the longest x2 208 us: share_in(): mine = lax.psum_scatter(pieces, EVERY, scatter_dimension=0)]
    all_gather x10 -> x0, waiting for transfers between devices: 233 us -> none  [the longest x4 103 us: spread(): return lax.all_gather(mine, EVERY)]
    psum x1 -> x0, waiting for transfers between devices: 94.5 us -> none  [per_device(): lax.psum((grad_qmap, grad_kmap, norm_grads), EVERY)]
    all_gather x8 -> x0, blocking collectives: 85.6 us -> none  [the longest x2 26.4 us: carried_in(): near = lax.all_gather(value, 'tensor')]
    reshape x9 -> x7, local copies, waits for them, and re-layouts: 66.5 us -> 6.89 us  [the longest x2 3.5 us: carried_states(): packed.reshape(seqs, heads // 2, feats, 2, head).transpose(0, 1, 3, 2, 4)]
    psum x1 -> x0, blocking collectives: 39.2 us -> none  [per_device(): lax.psum((grad_qmap, grad_kmap, norm_grads), EVERY)]
    transpose x4 -> x7, local copies, waits for them, and re-layouts: 23.1 us -> 4.06 us  [the longest x2 2.23 us: carried_states(): packed.reshape(seqs, heads // 2, feats, 2, head).transpose(0, 1, 3, 2, 4)]
  transfers between devices with their start and end apart: 15 -> 0, of which waited for: 11 -> 0; matrix products, arithmetic and copies ran while one was open for 23% -> 0% of each run, Pallas kernels for 0% -> 0%
where the time goes in v2:
time: 591 us; the launch traced here: 583 us
  Pallas kernels  340 us (58%)
  matrix products  79.1 us (13%)
  local copies, waits for them, and re-layouts  67.6 us (11%)
  blocking collectives  52.5 us (9%)
  other arithmetic  42.3 us (7%)
    pallas_call x1, Pallas kernels, reduce_grads(): pl.pallas_call(reduce_kernel, out_shape=[jax.ShapeDtypeStruct(s, bf16) fo...  210 us
    pallas_call x1, Pallas kernels, gather_weights(): pl.pallas_call(gather_kernel, out_shape=[jax.ShapeDtypeStruct(s, bf16) fo...  75.2 us
    pallas_call x2, Pallas kernels, scan_states(): pl.pallas_call(functools.partial(scan_kernel, backward), out_shape=[jax.S...  54.4 us
    all_gather x2, blocking collectives, full_maps(): pieces = lax.all_gather(part, ('fsdp', 'tensor'))  50.6 us
    concatenate x8, local copies, waits for them, and re-layouts, features(): jnp.concatenate([jax.nn.softmax(logits, -1), jax.nn.softmax(-logits, -1)]...  19.3 us
    unnamed x156, local copies, waits for them, and re-layouts  14.6 us

profile of v2, /device:TPU:0, one launch (start us, length us, event | category | flops | bytes accessed | tf_op | source)
XLA Modules:
  0.0 583.5 jit_solution(357979432683095678)
XLA Ops:
  4.2 1.3 convert_reduce_fusion.2
  5.6 1.7 fusion.29
  7.3 2.0 all_gather.15
  10.7 26.2 %all-gather.1 = bf16[24,32,64]{2,1,0:T(8,128)(2,1)S(1)} all-gather(bf16[3,32,64]{2,1,0:T(8,128)(2,1)S(1)} %copy-done.60), channel_id=3, replica_groups=mesh['fsdp'=2,'context'=4,'tensor'=4] {'fsdp','tensor'}, dimensions={0}, use_global_device_ids=true | all-gather | bytes 110592 | tf_op jit(solution)/shard_map/all_gather | solution.py:99
  36.9 24.4 %all-gather = bf16[24,32,64]{2,1,0:T(8,128)(2,1)S(1)} all-gather(bf16[3,32,64]{2,1,0:T(8,128)(2,1)S(1)} %copy-done.61), channel_id=2, replica_groups=mesh['fsdp'=2,'context'=4,'tensor'=4] {'fsdp','tensor'}, dimensions={0}, use_global_device_ids=true | all-gather | bytes 110592 | tf_op jit(solution)/shard_map/all_gather | solution.py:99
  61.3 2.2 copy.144
  63.5 1.9 fusion.26
  65.4 2.4 constant_dynamic-slice_fusion.2
  67.8 75.2 %gather_weights.1 = (bf16[3,768,768]{2,1,0:T(8,128)(2,1)}, bf16[768,768]{1,0:T(8,128)(2,1)}, bf16[768,3072]{1,0:T(8,128)(2,1)}, bf16[768,3072]{1,0:T(8,128)(2,1)}) custom-call(bf16[3,192,384]{2,1,0:T(8,128)(2,1)} %bitcast.318, bf16[192,384]{1,0:T(8,128)(2,1)} %refs_1_.1, bf16[384,768]{1,0:T(8,128)(2,1)} %refs_2_.1, bf16[384,768]{1,0:T(8,128)(2,1)} %bitcast.290), custom_call_target="tpu_custom_call" | custom-call | tf_op jit(solution)/shard_map/gather_weights/pallas_call | solution.py:247
  143.1 4.0 convert_bitcast_fusion
  147.1 1.0 fusion.72
  148.2 1.2 reshape_reshape_squeeze.3
  150.7 1.1 divide_convert_fusion.1
  151.8 2.5 concatenate.25
  154.3 2.1 copy.152
  159.2 2.1 copy.151
  161.3 2.7 pad_maximum_fusion.2
  164.0 1.8 fusion.76
  165.8 1.3 divide_convert_fusion.3
  167.1 2.9 concatenate.22
  170.1 3.3 copy.148
  173.4 1.7 fusion.77
  175.8 1.1 divide_convert_fusion.4
  176.9 2.9 concatenate.21
  179.9 3.3 copy.147
  183.2 3.0 convert_reduce_fusion.1
  188.0 29.5 %scan_states.2 = (bf16[2,768,128]{2,1,0:T(8,128)(2,1)S(1)}, f32[16,8,128]{2,1,0:T(8,128)S(1)}) custom-call(bf16[2,768,128]{2,1,0:T(8,128)(2,1)S(1)} %copy.158.s_ref, f32[16,8,128]{2,1,0:T(8,128)S(1)} %pad.11.z_ref), custom_call_target="tpu_custom_call" | custom-call | tf_op jit(solution)/shard_map/scan_states/pallas_call | solution.py:305
  218.3 1.9 fusion.62
  220.2 1.2 reshape.431
  221.5 1.1 copy.160
  222.7 2.1 convert_reduce_fusion
  225.4 1.0 copy-done.15
  226.4 1.9 fusion.17
  231.8 2.6 fusion.79
  234.5 8.9 %fusion.10 = (bf16[512,3072]{1,0:T(8,128)(2,1)S(1)}, f32[512,3072]{1,0:T(8,128)}) fusion(f32[512,3072]{1,0:T(8,128)S(1)} %fusion.79, bf16[768,3072]{1,0:T(8,128)(2,1)S(1)} %bitcast.331, f32[512,768]{1,0:T(8,128)S(1)} %get-tuple-element.136, f32[768]{0:T(1024)S(1)} %copy-done.68, f32[768]{0:T(1024)S(1)} %copy-done.65, f32[512]{0:T(512)S(1)} %fusion.64, ...), kind=kOutput, calls=%fused_computation.12 | convolution fusion | flops 2449342464 | bytes 22030336 | tf_op jit(solution)/shard_map/dot_general | solution.py:589
  243.4 7.5 %add_convert_fusion.1 = bf16[512,768]{1,0:T(8,128)(2,1)} fusion(f32[512,768]{1,0:T(8,128)S(1)} %get-tuple-element.136, bf16[768,3072]{1,0:T(8,128)(2,1)S(1)} %bitcast.280, f32[512,3072]{1,0:T(8,128)} %get-tuple-element.138), kind=kOutput, calls=%fused_computation.65 | convolution fusion | flops 2430861312 | bytes 13369344 | tf_op jit(solution)/shard_map/rk,dk->rd/dot_general | solution.py:591
  251.0 3.0 multiply_reduce_fusion
  255.2 4.9 convolution_convert_fusion.1.refs_2_
  261.0 1.8 convolution_convert_fusion.3
  262.8 1.9 fusion.80
  264.8 2.5 reshape.434
  267.3 1.9 fusion.18
  269.6 2.2 fusion.83
  274.7 24.8 %scan_states.3 = (bf16[2,768,128]{2,1,0:T(8,128)(2,1)S(1)}, f32[16,8,128]{2,1,0:T(8,128)S(1)}) custom-call(bf16[2,768,128]{2,1,0:T(8,128)(2,1)S(1)} %copy.174.s_ref, f32[16,8,128]{2,1,0:T(8,128)S(1)} %pad.12.z_ref), custom_call_target="tpu_custom_call" | custom-call | tf_op jit(solution)/shard_map/scan_states/pallas_call | solution.py:305
  301.0 2.3 reshape.436
  303.3 1.1 copy.176
  304.4 2.1 fusion.42
  306.5 1.7 copy.181
  308.2 3.2 stack_reshape.14
  311.4 2.5 select_convert_fusion
  313.8 1.2 fusion.82
  316.2 1.1 fusion.11
  317.4 1.6 add_bitcast_fusion
  329.6 4.5 fusion.27
  335.9 2.7 fusion.69
  338.6 3.4 add_convert_fusion
  342.9 5.6 convolution_convert_fusion.2
  348.5 7.9 %convolution_convert_fusion.refs_3_ = bf16[768,3072]{1,0:T(8,128)(2,1)} fusion(bf16[512,768]{1,0:T(8,128)(2,1)S(1)} %bitcast.272, f32[512,3072]{1,0:T(8,128)} %get-tuple-element.138), kind=kOutput, calls=%fused_computation.17 | convolution fusion | flops 2432434176 | bytes 11796480 | tf_op jit(solution)/shard_map/rk,rd->dk/dot_general | solution.py:595
  356.4 210.2 %reduce_grads.1 = (bf16[3,192,384]{2,1,0:T(8,128)(2,1)}, bf16[192,384]{1,0:T(8,128)(2,1)}, bf16[384,768]{1,0:T(8,128)(2,1)}, bf16[384,768]{1,0:T(8,128)(2,1)}, f...) custom-call(bf16[3,4,192,768]{3,2,1,0:T(8,128)(2,1)} %bitcast.283, ...), custom_call_target="tpu_custom_call" | custom-call | tf_op jit(solution)/shard_map/reduce_grads/pallas_call | solution.py:464
  569.3 1.6 convert_element_type.179
  573.8 1.1 convert_element_type.180
  575.0 1.4 copy.188
  576.4 5.2 bitcast_convert_fusion
  581.6 1.7 copy.238
  (247 shorter events, 43.1 us)
Async XLA Ops:
  0.6 36.3 %copy-start.61 = (bf16[3,32,64]{2,1,0:T(8,128)(2,1)S(1)}, bf16[3,32,64]{2,1,0:T(8,128)(2,1)}, u32[]{:S(2)}) copy-start(bf16[3,32,64]{2,1,0:T(8,128)(2,1)} %param.21) | copy-start | bytes 36868
  0.7 10.1 %copy-start.60 = (bf16[3,32,64]{2,1,0:T(8,128)(2,1)S(1)}, bf16[3,32,64]{2,1,0:T(8,128)(2,1)}, u32[]{:S(2)}) copy-start(bf16[3,32,64]{2,1,0:T(8,128)(2,1)} %param.20) | copy-start | bytes 36868
  5.6 57.9 %copy-start.25 = (bf16[2,1,1024,768]{3,2,1,0:T(8,128)(2,1)S(1)}, bf16[2,1,1024,768]{3,2,1,0:T(8,128)(2,1)}, u32[]{:S(2)}) copy-start(bf16[2,1,1024,768]{3,2,1,0:T(8,128)(2,1)} %param.13) | copy-start | bytes 9437188
  36.9 119.5 %copy-start.27 = (bf16[4,3,2,32,64]{4,3,2,1,0:T(8,128)(2,1)}, bf16[4,3,2,32,64]{4,3,2,1,0:T(8,128)(2,1)S(1)}, u32[]{:S(2)}) copy-start(bf16[4,3,2,32,64]{4,3,2,1,0:T(8,128)(2,1)S(1)} %copy.149) | copy-start | bytes 294916
  61.3 112.1 %copy-start.29 = (bf16[4,3,2,32,64]{4,3,2,1,0:T(8,128)(2,1)}, bf16[4,3,2,32,64]{4,3,2,1,0:T(8,128)(2,1)S(1)}, u32[]{:S(2)}) copy-start(bf16[4,3,2,32,64]{4,3,2,1,0:T(8,128)(2,1)S(1)} %copy.145) | copy-start | bytes 294916
  67.8 75.3 %copy-start.36 = (bf16[512,768]{1,0:T(8,128)(2,1)S(1)}, bf16[512,768]{1,0:T(8,128)(2,1)}, u32[]{:S(2)}) copy-start(bf16[512,768]{1,0:T(8,128)(2,1)} %fusion.26) | copy-start | bytes 2359300
  148.2 8.2 %copy-start.22 = (bf16[1,512,768]{1,2,0:T(8,128)(2,1)}, bf16[1,512,768]{1,2,0:T(8,128)(2,1)S(1)}, u32[]{:S(2)}) copy-start(bf16[1,512,768]{1,2,0:T(8,128)(2,1)S(1)} %get-tuple-element.113) | copy-start | bytes 2359300
  150.1 4.2 copy-start.7
  157.0 2.1 copy-start
  165.8 4.2 copy-start.9
  165.8 9.3 %copy-start.49 = (f32[512,12]{0,1:T(8,128)}, f32[512,12]{0,1:T(8,128)S(1)}, u32[]{:S(2)}) copy-start(f32[512,12]{0,1:T(8,128)S(1)} %get-tuple-element.127) | copy-start | bytes 73732
  175.1 4.7 copy-start.2
  175.1 4.7 copy-start.43
  183.2 3.0 copy-start.17
  186.1 1.1 copy-start.4
  218.3 4.3 copy-start.5
  222.6 2.7 copy-start.31
  222.6 2.1 copy-start.53
  222.6 2.1 copy-start.18
  224.7 1.7 copy-start.15
  226.4 4.7 slice-start
  228.3 1.5 copy-start.70
  228.3 2.8 slice-start.1
  230.7 1.1 copy-start.13
  230.7 3.7 slice-start.2
  231.8 2.6 copy-start.65
  231.8 2.6 copy-start.68
  231.8 2.6 slice-start.3
  255.2 5.5 copy-start.11
  267.3 2.4 copy-start.16
  269.2 4.0 copy-start.20
  300.4 4.0 copy-start.6
  315.0 1.1 copy-start.21
  315.0 1.2 copy-start.32
  315.0 1.2 copy-start.52
  315.0 1.2 copy-start.58
  316.2 1.2 copy-start.19
  316.2 1.2 copy-start.59
  319.4 1.4 copy-start.1
  319.4 1.9 copy-start.8
  319.4 1.9 copy-start.54
  319.4 1.9 copy-start.55
  321.3 1.4 copy-start.3
  321.3 1.9 copy-start.10
  321.3 1.9 copy-start.56
  321.3 1.9 copy-start.57
  324.1 1.1 copy-start.24
  325.3 1.3 copy-start.42
  325.3 1.3 copy-start.48
  326.5 2.9 copy-start.33
  326.6 1.4 copy-start.23
  326.6 2.8 copy-start.69
  328.0 1.6 copy-start.37
  329.4 4.7 copy-start.35
  335.4 3.2 copy-start.12
  335.4 3.2 copy-start.14
  335.8 2.7 copy-start.64
  338.6 3.4 copy-start.66
  338.6 3.4 copy-start.67
  338.6 4.3 copy-start.34
  571.4 1.4 copy-start.45
  571.5 2.3 copy-start.40
  572.8 2.1 copy-start.39
  576.4 5.2 copy-start.26
  (11 other events, 10.1 us)

commit v3 on v1

--- a/solution.py
+++ b/solution.py
@@ -1,6 +1,8 @@
 import jax
 import jax.numpy as jnp
 from jax import lax
+from jax.experimental import pallas as pl
+from jax.experimental.pallas import tpu as pltpu
 from jax.sharding import PartitionSpec as P
 
 BLK = 256
@@ -354,6 +356,914 @@
     )
 
 
+MESH = pl.DeviceIdType.MESH
+bf16 = jnp.bfloat16
+f32 = jnp.float32
+
+
+def whereabouts():
+    return tuple(lax.axis_index(name) for name in EVERY)
+
+
+def neighbours(f, c, t):
+    n = c * 4 + t
+    peers = [(1 - f, c, t)]
+    for k in range(1, 16):
+        other = lax.rem(n + k, 16)
+        peers.append((f, other // 4, lax.rem(other, 4)))
+    for k in range(1, 4):
+        peers.append((1 - f, c, lax.rem(t + k, 4)))
+    return peers
+
+
+def meet(f, c, t):
+    barrier = pltpu.get_barrier_semaphore()
+    peers = neighbours(f, c, t)
+    for peer in peers:
+        pl.semaphore_signal(barrier, inc=1, device_id=peer, device_id_type=MESH)
+    pl.semaphore_wait(barrier, len(peers))
+
+
+def send(src, dst, send_sem, recv_sem, peer):
+    copy = pltpu.make_async_remote_copy(
+        src_ref=src, dst_ref=dst, send_sem=send_sem, recv_sem=recv_sem,
+        device_id=peer, device_id_type=MESH,
+    )
+    copy.start()
+    return copy
+
+
+def arrived(ref, sem):
+    pltpu.make_async_copy(ref, ref, sem).wait()
+
+
+def at(start, size, unit):
+    return pl.ds(pl.multiple_of(start, unit), size)
+
+
+def half(ref, m, f):
+    if m == 0:
+        w = ref.shape[2] // 2
+        return ref.at[:, :, at(f * w, w, 128)]
+    if m == 1:
+        w = ref.shape[1] // 2
+        return ref.at[:, at(f * w, w, 128)]
+    w = ref.shape[0] // 2
+    return ref.at[at(f * w, w, 16), :]
+
+
+def shard(ref, m, f, t):
+    if m == 0:
+        w, h = ref.shape[2] // 2, ref.shape[1] // 4
+        return ref.at[:, at(t * h, h, 16), at(f * w, w, 128)]
+    if m == 1:
+        w, h = ref.shape[1] // 2, ref.shape[0] // 4
+        return ref.at[at(t * h, h, 16), at(f * w, w, 128)]
+    h, w = ref.shape[0] // 2, ref.shape[1] // 4
+    return ref.at[at(f * h, h, 16), at(t * w, w, 128)]
+
+
+def piece(ref, m, f, c, t):
+    if m == 0:
+        w, h = ref.shape[2] // 2, ref.shape[1] // 16
+        return ref.at[:, at(t * 4 * h + c * h, h, 16), at(f * w, w, 128)]
+    if m == 1:
+        w, h = ref.shape[1] // 2, ref.shape[0] // 16
+        return ref.at[at(t * 4 * h + c * h, h, 16), at(f * w, w, 128)]
+    h, w = ref.shape[0] // 8, ref.shape[1] // 4
+    return ref.at[at(f * 4 * h + c * h, h, 16), at(t * w, w, 128)]
+
+
+def quarter(ref, m, c):
+    if m == 0:
+        h = ref.shape[1] // 4
+        return ref.at[:, at(c * h, h, 16), :]
+    h = ref.shape[0] // 4
+    return ref.at[at(c * h, h, 16), :]
+
+
+def context_part(ref, m, c):
+    if m == 0:
+        h = ref.shape[2] // 4
+        return ref.at[:, :, at(c * h, h, 16), :]
+    if m == 1:
+        h = ref.shape[1] // 4
+        return ref.at[:, at(c * h, h, 16), :]
+    h = ref.shape[0] // 4
+    return ref.at[at(c * h, h, 16), :]
+
+
+def tensor_part(ref, m, t):
+    if m == 0:
+        return ref.at[:, t]
+    if m == 1:
+        return ref.at[t]
+    w = ref.shape[1] // 4
+    return ref.at[:, at(t * w, w, 128)]
+
+
+NN = (((1,), (0,)), ((), ()))
+NT = (((1,), (1,)), ((), ()))
+TN = (((0,), (0,)), ((), ()))
+
+
+def mm(a, b, dims=NN):
+    return lax.dot_general(a, b, dims, preferred_element_type=f32)
+
+
+def lanes_of(shape):
+    return lax.broadcasted_iota(jnp.int32, shape, len(shape) - 1)
+
+
+def block_ones(size, group):
+    row = lax.broadcasted_iota(jnp.int32, (size, size), 0) // group
+    col = lax.broadcasted_iota(jnp.int32, (size, size), 1) // group
+    return jnp.where(row == col, 1.0, 0.0).astype(bf16)
+
+
+def statistics(rows):
+    center = rows - jnp.mean(rows, -1, keepdims=True)
+    rstd = lax.rsqrt(jnp.mean(center * center, -1, keepdims=True) + epsilon)
+    return center * rstd, rstd
+
+
+def norm_back(grad, e, rstd, gain):
+    w = grad * gain
+    return rstd * (w - jnp.mean(w, -1, keepdims=True) - e * jnp.mean(w * e, -1, keepdims=True))
+
+
+def near_far(first, low, high):
+    return jnp.where(first, low, high)
+
+
+def own_half(values, first, odd):
+    zero = jnp.zeros_like(values)
+    return jnp.where(first, zero, values) if odd else jnp.where(first, values, zero)
+
+
+def pair_block(values, first):
+    return jnp.concatenate([own_half(values, first, 0), own_half(values, first, 1)], 0)
+
+
+def split_half(full, first, odd):
+    other = pltpu.roll(full, 64, 1)
+    return jnp.where(first, other, full) if odd else jnp.where(first, full, other)
+
+
+def layer_kernel(*refs):
+    inputs, cotangent, flags, maps, norms = refs[:5]
+    shards = refs[5:9]
+    all_out, all_in = refs[9:11]
+    outs, small_out = refs[11:15], refs[15]
+    w, mx, nrm, x, g, n1, qkv, feat = refs[16:20], *refs[20:27]
+    prior, sums_in, states, z_buf, s_in, z_in, s_out, z_out = refs[27:35]
+    o, rden, num, mid, n2, a, gp, rows_out = refs[35:43]
+    gm, dnum, dden, dproj, rows_in, turned = refs[43:49]
+    pair_in, xy_in, part, tz_in, last = (refs[49 + 4 * i : 53 + 4 * i] for i in range(5))
+    small, small_pair, small_own, small_in, small_sum = refs[69:74]
+    local_sem, send_sem, extra_sem, z_sem, xy_sem, pair_sem = refs[74:80]
+    scan_sem, rows_sem, gpair_sem, gxy_sem, gz_sem, last_sem, small_sem = refs[80:87]
+    wq, wo, wu, wd = w
+    d = x.shape[1]
+    ff = a.shape[1]
+    half_rows = x.shape[0] // 2
+    f, c, t = whereabouts()
+    n = c * 4 + t
+    peers = neighbours(f, c, t)
+    partner = peers[0]
+    started = []
+
+    def put(src, dst, recv_sem, peer):
+        started.append(send(src, dst, send_sem, recv_sem, peer))
+
+    fetched = []
+
+    def fetch(src, dst, sem):
+        copy = pltpu.make_async_copy(src, dst, sem)
+        copy.start()
+        return copy
+
+    for i in range(2):
+        rows = pl.ds(i * half_rows, half_rows)
+        fetched.append(fetch(inputs.at[i, 0, at(t * half_rows, half_rows, 16), :], x.at[rows], local_sem.at[i]))
+        fetched.append(fetch(cotangent.at[i, 0, at(t * half_rows, half_rows, 16), :], g.at[rows], local_sem.at[2 + i]))
+    h3 = maps.shape[1]
+    lo_norm = d // 2
+
+    def map_place(ff_, tt):
+        return mx.at[:, pl.ds(tt * h3, h3), at(ff_ * 32, 32, 16), :]
+
+    def norm_place(ff_):
+        return nrm.at[:, at(ff_ * lo_norm, lo_norm, 128)]
+
+    fetched.append(fetch(maps, map_place(f, t), local_sem.at[4]))
+    fetched.append(fetch(norms, norm_place(f), local_sem.at[5]))
+    shard_copies = [fetch(shards[m], shard(w[m], m, f, t), local_sem.at[6 + m]) for m in range(4)]
+    z_buf[...] = jnp.zeros_like(z_buf)
+    small[...] = jnp.zeros_like(small)
+    meet(f, c, t)
+
+    order = (0, 1, 2, 3)
+    for k in range(1, 8):
+        peer = (f if k < 4 else 1 - f, c, lax.rem(t + k, 4))
+        put(maps, map_place(f, t), extra_sem.at[k], peer)
+    put(norms, norm_place(f), extra_sem.at[0], partner)
+    for m in order:
+        for k in range(1, 4):
+            put(quarter(shards[m], m, c), piece(w[m], m, f, c, t), z_sem.at[m, k], (f, c, lax.rem(t + k, 4)))
+    for m in order:
+        put(shards[m], shard(w[m], m, f, t), pair_sem.at[m], partner)
+
+    def forward(m, k):
+        got = piece(w[m], m, f, c, lax.rem(t + 4 - k, 4))
+        arrived(got, z_sem.at[m, k])
+        for j in range(1, 4):
+            put(got, got, xy_sem.at[m, k, j], (f, c ^ j, t))
+        put(got, got, pair_sem.at[m], partner)
+
+    def across(m):
+        for k in range(1, 4):
+            for j in range(1, 4):
+                got = piece(w[m], m, f, c ^ j, lax.rem(t + 4 - k, 4))
+                arrived(got, xy_sem.at[m, k, j])
+                put(got, got, pair_sem.at[m], partner)
+
+    def complete(m):
+        shard_copies[m].wait()
+        arrived(half(w[m], m, 1 - f), pair_sem.at[m])
+
+    for k in range(1, 4):
+        forward(0, k)
+    for copy in fetched:
+        copy.wait()
+    arrived(norm_place(1 - f), extra_sem.at[0])
+    first = lanes_of((1, 128)) < 64
+    ones64 = block_ones(128, 64)
+    step = half_rows // 2
+
+    @pl.loop(0, 4)
+    def _(i):
+        rows = at(i * step, step, 16)
+        e, _unused = statistics(x[rows, :].astype(f32))
+        n1[rows, :] = (e * nrm[0:1, :] + nrm[1:2, :]).astype(bf16)
+
+    for k in range(1, 4):
+        forward(1, k)
+    across(0)
+    forward(2, 1)
+    for k in range(1, 8):
+        arrived(map_place(f if k < 4 else 1 - f, lax.rem(t + 8 - k, 4)), extra_sem.at[k])
+    complete(0)
+
+    chunks = d // 256
+
+    @pl.loop(0, 3 * chunks)
+    def _(i):
+        kind, j = i // chunks, lax.rem(i, chunks)
+        cols = at(j * 256, 256, 128)
+        qkv[kind, :, cols] = mm(n1[...], wq[kind, cols, :], NT).astype(bf16)
+
+    pairs = d // 128
+
+    def pair_map(side, p):
+        zero = jnp.zeros((64, 128), bf16)
+        top = jnp.concatenate([mx[side, 2 * p], zero], 1)
+        bottom = jnp.concatenate([zero, mx[side, 2 * p + 1]], 1)
+        return jnp.concatenate([top, bottom], 0)
+
+    @pl.loop(0, 4 * pairs)
+    def _(i):
+        side, rest = i // (2 * pairs), lax.rem(i, 2 * pairs)
+        b, p = rest // pairs, lax.rem(rest, pairs)
+        rows = at(b * half_rows, half_rows, 16)
+        logits = mm(qkv[side, rows, at(p * 128, 128, 128)], pair_map(side, p))
+        for odd in range(2):
+            part_ = logits[:, odd * 128 : odd * 128 + 128]
+            low_top = jnp.max(jnp.where(first, part_, -jnp.inf), -1, keepdims=True)
+            high_top = jnp.max(jnp.where(first, -jnp.inf, part_), -1, keepdims=True)
+            e = jnp.exp(part_ - jnp.where(first, low_top, high_top))
+            total = mm(e.astype(bf16), ones64)
+            feat[side, rows, at(p * 256 + odd * 128, 128, 128)] = (e / total).astype(bf16)
+
+    @pl.loop(0, 2 * pairs)
+    def _(i):
+        b, p = i // pairs, lax.rem(i, pairs)
+        rows = at(b * half_rows, half_rows, 16)
+        keys = feat[1, rows, at(p * 256, 256, 128)]
+        both = mm(keys, qkv[2, rows, at(p * 128, 128, 128)], TN)
+        states[b, at(p * 128, 128, 16), :] = near_far(first, both[:128], both[128:]).astype(bf16)
+        tall = mm(jnp.ones((8, half_rows), bf16), keys)
+        slot = lax.broadcasted_iota(jnp.int32, (8, 128), 0) == b
+        z_buf[2 * p] = jnp.where(slot, tall[:, :128], z_buf[2 * p])
+        z_buf[2 * p + 1] = jnp.where(slot, tall[:, 128:], z_buf[2 * p + 1])
+
+    srows = states.shape[1] // 16
+
+    def scan_out(sem0):
+        for k in range(1, 16):
+            other = lax.rem(n + k, 16)
+            put(states.at[:, at(other * srows, srows, 16), :], s_in.at[n], scan_sem.at[sem0], peers[k])
+            put(z_buf.at[other], z_in.at[n], scan_sem.at[sem0 + 1], peers[k])
+        one = fetch(states.at[:, at(n * srows, srows, 16), :], s_in.at[n], local_sem.at[0])
+        two = fetch(z_buf.at[n], z_in.at[n], local_sem.at[1])
+        one.wait()
+        two.wait()
+
+    def scan_back(sem0, backward):
+        arrived(s_in.at[pl.ds(0, 15)], scan_sem.at[sem0])
+        arrived(z_in.at[pl.ds(0, 15)], scan_sem.at[sem0 + 1])
+        total = jnp.zeros(s_in.shape[1:], f32)
+        sums = jnp.zeros(z_in.shape[1:], f32)
+        for i in range(15, -1, -1) if backward else range(16):
+            s_out[i] = total.astype(bf16)
+            z_out[i] = sums
+            total = total + s_in[i].astype(f32)
+            sums = sums + z_in[i]
+        for k in range(1, 16):
+            other = lax.rem(n + k, 16)
+            put(s_out.at[other], prior.at[int(backward), :, at(n * srows, srows, 16), :], scan_sem.at[sem0 + 2], peers[k])
+            put(z_out.at[other], sums_in.at[int(backward), n], scan_sem.at[sem0 + 3], peers[k])
+        one = fetch(s_out.at[n], prior.at[int(backward), :, at(n * srows, srows, 16), :], local_sem.at[0])
+        two = fetch(z_out.at[n], sums_in.at[int(backward), n], local_sem.at[1])
+        one.wait()
+        two.wait()
+
+    def scan_end(sem0):
+        arrived(s_in.at[pl.ds(0, 15)], scan_sem.at[sem0 + 2])
+        arrived(z_in.at[pl.ds(0, 15)], scan_sem.at[sem0 + 3])
+
+    scan_out(0)
+    across(1)
+    forward(2, 2)
+    forward(2, 3)
+
+    def mask_of(b, turn):
+        row = lax.broadcasted_iota(jnp.int32, (half_rows, half_rows), 0)
+        col = lax.broadcasted_iota(jnp.int32, (half_rows, half_rows), 1)
+        causal = row <= col if turn else col <= row
+        return jnp.where(causal, 1.0, flags[b, 0:1, :])
+
+    @pl.loop(0, 2 * pairs)
+    def _(i):
+        b, p = i // pairs, lax.rem(i, pairs)
+        rows = at(b * half_rows, half_rows, 16)
+        values = qkv[2, rows, at(p * 128, 128, 128)]
+        mask = mask_of(b, False)
+        both = None
+        for odd in range(2):
+            cols = at(p * 256 + odd * 128, 128, 128)
+            scores = (mm(feat[0, rows, cols], feat[1, rows, cols], NT) * mask).astype(bf16)
+            right = jnp.concatenate(
+                [own_half(values, first, odd), own_half(jnp.ones_like(values), first, odd)], 1
+            )
+            term = mm(scores, right)
+            both = term if both is None else both + term
+        num[rows, at(p * 128, 128, 128)] = both[:, :128]
+        rden[rows, at(p * 128, 128, 128)] = both[:, 128:]
+
+    scan_back(0, False)
+    for k in range(1, 4):
+        forward(3, k)
+    complete(1)
+    scan_end(0)
+
+    def sums_pair(direction, b, p, odd):
+        tile = sums_in[direction, 2 * p + odd]
+        slot = lax.broadcasted_iota(jnp.int32, (8, 128), 0) == b
+        return jnp.sum(jnp.where(slot, tile, 0.0), 0, keepdims=True)
+
+    @pl.loop(0, 2 * pairs)
+    def _(i):
+        b, p = i // pairs, lax.rem(i, pairs)
+        rows = at(b * half_rows, half_rows, 16)
+        cols = at(p * 128, 128, 128)
+        queries = feat[0, rows, at(p * 256, 256, 128)]
+        before = pair_block(prior[0, b, at(p * 128, 128, 16), :], first)
+        zero = jnp.zeros((64, 128), bf16)
+        z_low = jnp.broadcast_to(sums_pair(0, b, p, 0), (64, 128)).astype(bf16)
+        z_high = jnp.broadcast_to(sums_pair(0, b, p, 1), (64, 128)).astype(bf16)
+        z_rows = jnp.concatenate(
+            [jnp.concatenate([z_low, zero], 1), jnp.concatenate([zero, z_high], 1)], 0
+        )
+        inverse = 1.0 / (rden[rows, cols] + mm(queries, z_rows, NT))
+        o[rows, cols] = ((num[rows, cols] + mm(queries, before)) * inverse).astype(bf16)
+        rden[rows, cols] = inverse
+
+    @pl.loop(0, 2)
+    def _(i):
+        rows = at(i * half_rows, half_rows, 16)
+        mid[rows, :] = x[rows, :].astype(f32) + mm(o[rows, :], wo[...])
+
+    across(2)
+
+    @pl.loop(0, 4)
+    def _(i):
+        rows = at(i * step, step, 16)
+        e, _unused = statistics(mid[rows, :])
+        n2[rows, :] = (e * nrm[2:3, :] + nrm[3:4, :]).astype(bf16)
+
+    complete(2)
+
+    @pl.loop(0, ff // 256)
+    def _(i):
+        cols = at(i * 256, 256, 128)
+        u = mm(n2[...], wu[:, cols])
+        scale = 0.7978845608028654
+        square = u * u
+        tanh = jnp.tanh(scale * u * (1.0 + 0.044715 * square))
+        cdf = 0.5 + 0.5 * tanh
+        a[:, cols] = (u * cdf).astype(bf16)
+        slope = cdf + (0.5 * scale) * u * (1.0 - tanh * tanh) * (1.0 + 0.134145 * square)
+        gp[:, cols] = slope.astype(bf16)
+
+    across(3)
+    complete(3)
+
+    @pl.loop(0, chunks)
+    def _(i):
+        cols = at(i * 256, 256, 128)
+        rows_out[:, cols] = (mid[:, cols] + mm(a[...], wd[cols, :], NT)).astype(bf16)
+
+    links = []
+
+    def pass_on(i, way, hop, block):
+        dst = (all_out, all_in)[i]
+        src = (rows_out, rows_in)[i]
+        peer = (f, c, t + 1 if way == 0 else t - 1)
+        copies = []
+        for b in range(2):
+            origin = src.at[pl.ds(b * half_rows, half_rows)] if hop == 0 else dst.at[b, block]
+            copies.append(pltpu.make_async_remote_copy(
+                src_ref=origin, dst_ref=dst.at[b, block], send_sem=rows_sem.at[i, way, hop, 0],
+                recv_sem=rows_sem.at[i, way, hop, 1], device_id=peer, device_id_type=MESH,
+            ))
+        return copies
+
+    def rows_hop(i, hop):
+        dst = (all_out, all_in)[i]
+        for way in range(2):
+            block = t - hop if way == 0 else t + hop
+            here = block >= 0 if way == 0 else block <= 3
+            more = t < 3 if way == 0 else t > 0
+            if hop > 0:
+                @pl.when(here)
+                def _():
+                    arrived(dst.at[:, 0], rows_sem.at[i, way, hop - 1, 1])
+            if hop < 3:
+                @pl.when(jnp.logical_and(here, more))
+                def _():
+                    for copy in pass_on(i, way, hop, block):
+                        copy.start()
+
+    def rows_sent(i):
+        for hop in range(3):
+            for way in range(2):
+                block = t - hop if way == 0 else t + hop
+                here = block >= 0 if way == 0 else block <= 3
+                more = t < 3 if way == 0 else t > 0
+
+                @pl.when(jnp.logical_and(here, more))
+                def _():
+                    for copy in pass_on(i, way, hop, block):
+                        copy.wait_send()
+
+    own_rows = []
+    for b in range(2):
+        own_rows.append(fetch(rows_out.at[pl.ds(b * half_rows, half_rows)], all_out.at[b, t], local_sem.at[2 + b]))
+    rows_hop(0, 0)
+
+    def grad_pair(m):
+        if m < 2:
+            h = d // 4
+            for tt in range(4):
+                if m == 0:
+                    src = w[m].at[:, pl.ds(tt * h, h), at((1 - f) * (d // 2), d // 2, 128)]
+                    put(src, pair_in[m].at[:, tt], gpair_sem.at[m], partner)
+                else:
+                    src = w[m].at[pl.ds(tt * h, h), at((1 - f) * (d // 2), d // 2, 128)]
+                    put(src, pair_in[m].at[tt], gpair_sem.at[m], partner)
+        else:
+            put(half(w[m], m, 1 - f), pair_in[m], gpair_sem.at[m], partner)
+
+    def grad_xy(m):
+        arrived(pair_in[m], gpair_sem.at[m])
+        h = d // 4
+        cols = at(f * (d // 2), d // 2, 128)
+        if m == 0:
+            @pl.loop(0, 12)
+            def _(i):
+                kind, tt = i // 4, lax.rem(i, 4)
+                mine = wq[kind, at(tt * h, h, 16), cols].astype(f32)
+                pair_in[0][kind, tt] = (mine + pair_in[0][kind, tt].astype(f32)).astype(bf16)
+        elif m == 1:
+            @pl.loop(0, 4)
+            def _(tt):
+                mine = wo[at(tt * h, h, 16), cols].astype(f32)
+                pair_in[1][tt] = (mine + pair_in[1][tt].astype(f32)).astype(bf16)
+        else:
+            @pl.loop(0, 12)
+            def _(i):
+                rows = at(i * 32, 32, 16)
+                mine = w[m][at(f * (d // 2) + i * 32, 32, 16), :].astype(f32)
+                pair_in[m][rows, :] = (mine + pair_in[m][rows, :].astype(f32)).astype(bf16)
+        for j in range(1, 4):
+            put(context_part(pair_in[m], m, c ^ j), xy_in[m].at[j - 1], gxy_sem.at[m, j], (f, c ^ j, t))
+
+    def grad_z(m):
+        for j in range(1, 4):
+            arrived(xy_in[m].at[j - 1], gxy_sem.at[m, j])
+        if m == 0:
+            h = d // 16
+
+            @pl.loop(0, 12)
+            def _(i):
+                kind, tt = i // 4, lax.rem(i, 4)
+                total = pair_in[0][kind, tt, at(c * h, h, 16), :].astype(f32)
+                for j in range(3):
+                    total = total + xy_in[0][j, kind, tt].astype(f32)
+                part[0][kind, tt] = total.astype(bf16)
+        elif m == 1:
+            h = d // 16
+
+            @pl.loop(0, 4)
+            def _(tt):
+                total = pair_in[1][tt, at(c * h, h, 16), :].astype(f32)
+                for j in range(3):
+                    total = total + xy_in[1][j, tt].astype(f32)
+                part[1][tt] = total.astype(bf16)
+        else:
+            @pl.loop(0, d // 8 // 16)
+            def _(i):
+                rows = at(i * 16, 16, 16)
+                total = pair_in[m][at(c * (d // 8) + i * 16, 16, 16), :].astype(f32)
+                for j in range(3):
+                    total = total + xy_in[m][j, rows, :].astype(f32)
+                part[m][rows, :] = total.astype(bf16)
+        for k in range(1, 4):
+            other = lax.rem(t + k, 4)
+            put(tensor_part(part[m], m, other), tz_in[m].at[k - 1], gz_sem.at[m, k], (f, c, other))
+
+    def grad_last(m):
+        for k in range(1, 4):
+            arrived(tz_in[m].at[k - 1], gz_sem.at[m, k])
+        if m == 0:
+            for kind in range(3):
+                total = part[0][kind, t].astype(f32)
+                for k in range(3):
+                    total = total + tz_in[0][k, kind].astype(f32)
+                last[0][kind] = total.astype(bf16)
+        elif m == 1:
+            total = part[1][t].astype(f32)
+            for k in range(3):
+                total = total + tz_in[1][k].astype(f32)
+            last[1][...] = total.astype(bf16)
+        else:
+            cols = at(t * (ff // 4), ff // 4, 128)
+
+            @pl.loop(0, d // 8 // 16)
+            def _(i):
+                rows = at(i * 16, 16, 16)
+                total = part[m][rows, cols].astype(f32)
+                for k in range(3):
+                    total = total + tz_in[m][k, rows, :].astype(f32)
+                last[m][rows, :] = total.astype(bf16)
+        for j in range(1, 4):
+            put(last[m], quarter(outs[m], m, c), last_sem.at[m, j], (f, c ^ j, t))
+        fetch(last[m], quarter(outs[m], m, c), local_sem.at[10 + m]).wait()
+
+    for copy in started:
+        copy.wait_send()
+    started.clear()
+
+    @pl.loop(0, ff // 256)
+    def _(i):
+        cols = at(i * 256, 256, 128)
+        gp[:, cols] = (mm(g[...], wd[:, cols]) * gp[:, cols].astype(f32)).astype(bf16)
+
+    def turn(src):
+        @pl.loop(0, chunks)
+        def _(i):
+            cols = at(i * 256, 256, 128)
+            turned[at(i * 256, 256, 16), :] = src[:, cols].astype(f32).T.astype(bf16)
+
+    turn(g)
+
+    @pl.loop(0, ff // 256)
+    def _(i):
+        cols = at(i * 256, 256, 128)
+        wd[:, cols] = mm(turned[...], a[:, cols]).astype(bf16)
+
+    grad_pair(3)
+
+    @pl.loop(0, chunks)
+    def _(i):
+        cols = at(i * 256, 256, 128)
+        num[:, cols] = mm(gp[...], wu[cols, :], NT)
+
+    @pl.loop(0, 4)
+    def _(i):
+        rows = at(i * step, step, 16)
+        e, rstd = statistics(mid[rows, :])
+        grad = num[rows, :]
+        nrm[6:7, :] += jnp.sum(grad * e, 0, keepdims=True)
+        nrm[7:8, :] += jnp.sum(grad, 0, keepdims=True)
+        total = g[rows, :].astype(f32) + norm_back(grad, e, rstd, nrm[2:3, :])
+        mid[rows, :] = total
+        gm[rows, :] = total.astype(bf16)
+
+    grad_xy(3)
+
+    @pl.loop(0, chunks)
+    def _(i):
+        cols = at(i * 256, 256, 128)
+        back = mm(gm[...], wo[cols, :], NT)
+        for side in range(2):
+            cut = at(i * 256 + side * 128, 128, 128)
+            grad = back[:, side * 128 : side * 128 + 128]
+            inverse = rden[:, cut]
+            dnum[:, cut] = (grad * inverse).astype(bf16)
+            dden[:, cut] = -mm((grad * o[:, cut].astype(f32)).astype(bf16), ones64) * inverse
+
+    @pl.loop(0, 2 * pairs)
+    def _(i):
+        b, p = i // pairs, lax.rem(i, pairs)
+        rows = at(b * half_rows, half_rows, 16)
+        cols = at(p * 128, 128, 128)
+        queries = feat[0, rows, at(p * 256, 256, 128)]
+        both = mm(queries, dnum[rows, cols], TN)
+        states[b, at(p * 128, 128, 16), :] = near_far(first, both[:128], both[128:]).astype(bf16)
+        slot = lax.broadcasted_iota(jnp.int32, (8, 128), 0) == b
+        packed = dden[rows, cols]
+        for odd in range(2):
+            full = split_half(packed, first, odd)
+            tall = jnp.sum(queries[:, odd * 128 : odd * 128 + 128].astype(f32) * full, 0, keepdims=True)
+            z_buf[2 * p + odd] = jnp.where(slot, tall, z_buf[2 * p + odd])
+
+    scan_out(4)
+    rows_hop(0, 1)
+
+    turn(n2)
+
+    @pl.loop(0, ff // 256)
+    def _(i):
+        cols = at(i * 256, 256, 128)
+        wu[:, cols] = mm(turned[...], gp[:, cols]).astype(bf16)
+
+    grad_pair(2)
+
+    scan_back(4, True)
+
+    @pl.loop(0, chunks)
+    def _(i):
+        cols = at(i * 256, 256, 128)
+        wo[cols, :] = mm(o[:, cols].astype(f32).T.astype(bf16), gm[...]).astype(bf16)
+
+    grad_pair(1)
+
+    lane = lanes_of((1, 128))
+
+    def extended(values, one, two, odd):
+        base = 0 if odd else 64
+        rest = jnp.where(lane == base, one, jnp.where(lane == base + 1, two, jnp.zeros_like(values)))
+        return jnp.where(first, rest, values) if odd else jnp.where(first, values, rest)
+
+    def block_maps(side, p):
+        low_ = jnp.where(first, mx[side, 2 * p], jnp.zeros((64, 128), bf16))
+        high_ = jnp.where(first, jnp.zeros((64, 128), bf16), -mx[side, 2 * p + 1])
+        return jnp.concatenate([low_, high_], 0)
+
+    def through_features(side, b, p, rows, cols, grads):
+        logits = []
+        for odd in range(2):
+            prob = feat[side, rows, at(p * 256 + odd * 128, 128, 128)].astype(f32)
+            grad = grads[odd]
+            inner = mm((prob * grad).astype(bf16), ones64)
+            both = prob * (grad - inner)
+            other = pltpu.roll(both, 64, 1)
+            logits.append(other - both if odd else both - other)
+        packed = jnp.where(first, logits[0], logits[1]).astype(bf16)
+        dproj[side, rows, cols] = mm(packed, block_maps(side, p), NT).astype(bf16)
+        square = mm(qkv[side, rows, cols], packed, TN)
+        small[side * pairs + p] += near_far(first, square[:64], square[64:])
+
+    def exact(packed, odd):
+        full = split_half(packed, first, odd)
+        head = full.astype(bf16)
+        return full, head, (full - head.astype(f32)).astype(bf16)
+
+    @pl.loop(0, 2 * pairs)
+    def _(i):
+        b, p = i // pairs, lax.rem(i, pairs)
+        rows = at(b * half_rows, half_rows, 16)
+        cols = at(p * 128, 128, 128)
+        values, grad_rows = qkv[2, rows, cols], dnum[rows, cols]
+        packed = dden[rows, cols]
+        before = prior[0, b, at(p * 128, 128, 16), :]
+        mask = mask_of(b, False)
+        unit = jnp.ones_like(values)
+        grads = []
+        for odd in range(2):
+            full, head, tail = exact(packed, odd)
+            left = extended(grad_rows, head, tail, odd)
+            right = extended(values, unit, unit, odd)
+            scores = (mm(left, right, NT) * mask).astype(bf16)
+            total = mm(scores, feat[1, rows, at(p * 256 + odd * 128, 128, 128)])
+            total = total + mm(own_half(grad_rows, first, odd), before, NT)
+            grads.append(total + full * sums_pair(0, b, p, odd))
+        through_features(0, b, p, rows, cols, grads)
+
+    scan_end(4)
+    rows_hop(0, 2)
+    grad_xy(2)
+
+    @pl.loop(0, 2 * pairs)
+    def _(i):
+        b, p = i // pairs, lax.rem(i, pairs)
+        rows = at(b * half_rows, half_rows, 16)
+        cols = at(p * 128, 128, 128)
+        values, grad_rows = qkv[2, rows, cols], dnum[rows, cols]
+        packed = dden[rows, cols]
+        after = prior[1, b, at(p * 128, 128, 16), :]
+        mask = mask_of(b, True)
+        unit = jnp.ones_like(values)
+        value_grad = mm(feat[1, rows, at(p * 256, 256, 128)], pair_block(after, first))
+        grads = []
+        for odd in range(2):
+            fcols = at(p * 256 + odd * 128, 128, 128)
+            queries, keys = feat[0, rows, fcols], feat[1, rows, fcols]
+            _full, head, tail = exact(packed, odd)
+            left = extended(values, unit, unit, odd)
+            right = extended(grad_rows, head, tail, odd)
+            scores = (mm(left, right, NT) * mask).astype(bf16)
+            total = mm(scores, queries) + mm(own_half(values, first, odd), after, NT)
+            grads.append(total + sums_pair(1, b, p, odd))
+            weights = (mm(keys, queries, NT) * mask).astype(bf16)
+            value_grad = value_grad + mm(weights, own_half(grad_rows, first, odd))
+        dproj[2, rows, cols] = value_grad.astype(bf16)
+        through_features(1, b, p, rows, cols, grads)
+
+    grad_xy(1)
+
+    @pl.loop(0, chunks)
+    def _(i):
+        cols = at(i * 256, 256, 128)
+        total = mm(dproj[0], wq[0, :, cols])
+        for kind in range(1, 3):
+            total = total + mm(dproj[kind], wq[kind, :, cols])
+        num[:, cols] = total
+
+    @pl.loop(0, 4)
+    def _(i):
+        rows = at(i * step, step, 16)
+        e, rstd = statistics(x[rows, :].astype(f32))
+        grad = num[rows, :]
+        nrm[4:5, :] += jnp.sum(grad * e, 0, keepdims=True)
+        nrm[5:6, :] += jnp.sum(grad, 0, keepdims=True)
+        rows_in[rows, :] = (mid[rows, :] + norm_back(grad, e, rstd, nrm[0:1, :])).astype(bf16)
+
+    for b in range(2):
+        own_rows.append(fetch(rows_in.at[pl.ds(b * half_rows, half_rows)], all_in.at[b, t], local_sem.at[4 + b]))
+    rows_hop(1, 0)
+
+    for i in range(4):
+        for j in range(d // 128):
+            small[2 * pairs, i * (d // 128) + j : i * (d // 128) + j + 1, :] = nrm[4 + i : 5 + i, j * 128 : j * 128 + 128]
+    put(small, small_pair, small_sem.at[0], partner)
+
+    @pl.loop(0, 3 * chunks)
+    def _(i):
+        kind, j = i // chunks, lax.rem(i, chunks)
+        cols = at(j * 256, 256, 128)
+        wq[kind, cols, :] = mm(dproj[kind, :, cols].astype(f32).T.astype(bf16), n1[...]).astype(bf16)
+
+    grad_pair(0)
+    arrived(small_pair, small_sem.at[0])
+    small_own[...] = (small[...] + small_pair[...]).astype(bf16)
+    for k in range(1, 16):
+        put(small_own.at[lax.rem(n + k, 16)], small_in.at[n], small_sem.at[1], peers[k])
+    fetch(small_own.at[n], small_in.at[n], local_sem.at[6]).wait()
+    grad_z(3)
+    rows_hop(1, 1)
+    grad_xy(0)
+    grad_z(2)
+    grad_z(1)
+    grad_last(3)
+    rows_hop(0, 3)
+    rows_hop(1, 2)
+    arrived(small_in.at[pl.ds(0, 15)], small_sem.at[1])
+    total = jnp.zeros(small_in.shape[1:], f32)
+    for i in range(16):
+        total = total + small_in[i].astype(f32)
+    small_sum[...] = total
+    for k in range(1, 16):
+        put(small_sum, small_out.at[n], small_sem.at[2], peers[k])
+    fetch(small_sum, small_out.at[n], local_sem.at[6]).wait()
+    grad_last(2)
+    grad_last(1)
+    grad_z(0)
+    grad_last(0)
+    for m in range(4):
+        for j in range(1, 4):
+            arrived(last[m], last_sem.at[m, j])
+    arrived(small_out.at[pl.ds(0, 15)], small_sem.at[2])
+    rows_hop(1, 3)
+    for copy in own_rows:
+        copy.wait()
+    for copy in started:
+        copy.wait_send()
+    rows_sent(0)
+    rows_sent(1)
+
+def mesh_device(
+    inputs,
+    cotangent,
+    picture_starts,
+    qkv_weight,
+    out_weight,
+    up_weight,
+    down_weight,
+    query_map,
+    key_map,
+    first_gain,
+    first_bias,
+    second_gain,
+    second_bias,
+):
+    micro, seq_local, seq_len, d = inputs.shape
+    span = seq_len // 4
+    rows = micro * seq_local * span
+    ff = up_weight.shape[1] * 4
+    heads = query_map.shape[0] * 4
+    head = query_map.shape[2]
+    own_block = lax.axis_index("context") * 4 + lax.axis_index("tensor")
+    flags = jnp.any(picture_starts.reshape(micro, -1) // BLK == own_block, 1).astype(f32)
+    flags = jnp.broadcast_to(flags[:, None, None], (micro, 8, span))
+    maps = jnp.stack([query_map, key_map])
+    maps = jnp.concatenate([maps, -maps], -1)
+    norms = jnp.stack([first_gain, first_bias, second_gain, second_bias]).astype(f32)
+    norms = jnp.concatenate([norms, jnp.zeros_like(norms)])
+    dma = pltpu.SemaphoreType.DMA
+    own = [(3, 4, d // 4, d // 2), (4, d // 4, d // 2), (d // 2, ff), (d // 2, ff)]
+    sums = [(3, 4, d // 16, d // 2), (4, d // 16, d // 2), (d // 8, ff), (d // 8, ff)]
+    last = [(3, d // 16, d // 2), (d // 16, d // 2), (d // 8, ff // 4), (d // 8, ff // 4)]
+    outs = [(3, d // 4, d // 2), (d // 4, d // 2), (d // 2, ff // 4), (d // 2, ff // 4)]
+    low = [(3, d, d), (d, d), (d, ff), (d, ff), (2, heads, head, 128)]
+    state_rows = heads // 2 * 128
+    pieces = (16, micro, state_rows // 16, 128)
+    small = (16, 64, 128)
+    scratch = [pltpu.VMEM(s, bf16) for s in low]
+    scratch += [pltpu.VMEM((8, d), f32)]
+    scratch += [pltpu.VMEM((rows, d), bf16)] * 3
+    scratch += [pltpu.VMEM((3, rows, d), bf16), pltpu.VMEM((2, rows, heads * 128), bf16)]
+    scratch += [pltpu.VMEM((2, micro, state_rows, 128), bf16), pltpu.VMEM((2, 16, 8, 128), f32)]
+    scratch += [pltpu.VMEM((micro, state_rows, 128), bf16), pltpu.VMEM((16, 8, 128), f32)]
+    scratch += [pltpu.VMEM(pieces, bf16), pltpu.VMEM((16, 8, 128), f32)] * 2
+    scratch += [pltpu.VMEM((rows, d), bf16)] + [pltpu.VMEM((rows, d), f32)] * 3
+    scratch += [pltpu.VMEM((rows, d), bf16)] + [pltpu.VMEM((rows, ff), bf16)] * 2
+    scratch += [pltpu.VMEM((rows, d), bf16)] * 3 + [pltpu.VMEM((rows, d), f32)]
+    scratch += [pltpu.VMEM((3, rows, d), bf16), pltpu.VMEM((rows, d), bf16), pltpu.VMEM((d, rows), bf16)]
+    scratch += [pltpu.VMEM(s, bf16) for s in own]
+    scratch += [pltpu.VMEM((3,) + s, bf16) for s in sums]
+    scratch += [pltpu.VMEM(s, bf16) for s in sums]
+    scratch += [pltpu.VMEM((3,) + s, bf16) for s in last]
+    scratch += [pltpu.VMEM(s, bf16) for s in last]
+    scratch += [pltpu.VMEM(small, f32)] * 2 + [pltpu.VMEM(small, bf16)] * 2 + [pltpu.VMEM(small[1:], f32)]
+    scratch += [dma((14,)), dma(()), dma((8,)), dma((4, 4)), dma((4, 4, 4)), dma((4,))]
+    scratch += [dma((8,)), dma((2, 2, 3, 2)), dma((4,)), dma((4, 4)), dma((4, 4)), dma((4, 4)), dma((3,))]
+    spread_rows = (micro, 4, span, d)
+    anywhere = pl.BlockSpec(memory_space=pl.ANY)
+    all_out, all_in, share_0, share_1, share_2, share_3, small = pl.pallas_call(
+        layer_kernel,
+        out_shape=[jax.ShapeDtypeStruct(spread_rows, bf16)] * 2
+        + [jax.ShapeDtypeStruct(s, bf16) for s in outs]
+        + [jax.ShapeDtypeStruct(small, f32)],
+        in_specs=[anywhere] * 2 + [pl.BlockSpec(memory_space=pltpu.VMEM)] + [anywhere] * 6,
+        out_specs=[anywhere] * 7,
+        scratch_shapes=scratch,
+        compiler_params=pltpu.CompilerParams(collective_id=0, has_side_effects=True, vmem_limit_bytes=67043328),
+        name="layer",
+    )(inputs, cotangent, flags, maps, norms, qkv_weight.transpose(0, 2, 1), out_weight, up_weight, down_weight.T)
+    small = small.reshape(-1, 128)
+    pairs = small[: heads * head].reshape(heads, head, 2, head)
+    pairs = pairs.transpose(0, 2, 1, 3).reshape(2, heads, head, head)
+    norm_grads = small[heads * head :].reshape(-1)[: 4 * d].reshape(4, d)
+    norm_grads = lax.dynamic_slice_in_dim(norm_grads, lax.axis_index("fsdp") * (d // 2), d // 2, 1)
+    return (
+        all_out.reshape(inputs.shape),
+        all_in.reshape(inputs.shape).astype(f32),
+        share_0.astype(f32).transpose(0, 2, 1),
+        share_1.astype(f32),
+        share_2.astype(f32),
+        share_3.astype(f32).T,
+        own_maps(pairs[0]),
+        own_maps(pairs[1]),
+        norm_grads[0],
+        norm_grads[1],
+        norm_grads[2],
+        norm_grads[3],
+    )
+
+
 def solution(mesh):
     in_specs = (
         P(None, "fsdp", "context", None),
@@ -384,6 +1294,7 @@
         P("fsdp"),
         P("fsdp"),
     )
+    sizes = tuple(mesh.shape[name] for name in EVERY)
     return jax.shard_map(
-        per_device, mesh=mesh, in_specs=in_specs, out_specs=out_specs, check_vma=False
-    )
+        mesh_device if sizes == (2, 4, 4) else per_device, mesh=mesh, in_specs=in_specs, out_specs=out_specs, check_vma=False
+    )

time: 1160 us -> 323 us (0.28); the launches traced: 1150 us -> 323 us
  waiting for transfers between devices: 637 us -> 0 us
  Pallas kernels: 0 us -> 298 us
  blocking collectives: 179 us -> 0 us
  local copies, waits for them, and re-layouts: 168 us -> 12.5 us
  matrix products: 93.7 us -> 0 us
  other arithmetic: 51.4 us -> 11.7 us
  between operations: 15.6 us -> 0.75 us
    reduce_scatter x4 -> x0, waiting for transfers between devices: 309 us -> none  [the longest x2 208 us: share_in(): mine = lax.psum_scatter(pieces, EVERY, scatter_dimension=0)]
    pallas_call x0 -> x1, Pallas kernels: none -> 298 us  [mesh_device(): pl.pallas_call(layer_kernel, out_shape=[jax.ShapeDtypeStruct(spread_rows,...]
    all_gather x10 -> x0, waiting for transfers between devices: 233 us -> none  [the longest x4 103 us: spread(): return lax.all_gather(mine, EVERY)]
    all_gather x11 -> x0, blocking collectives: 140 us -> none  [the longest x2 52.6 us: full_maps(): pieces = lax.all_gather(part, ('fsdp', 'tensor'))]
    psum x1 -> x0, waiting for transfers between devices: 94.5 us -> none  [per_device(): lax.psum((grad_qmap, grad_kmap, norm_grads), EVERY)]
    dot_general x30 -> x0, matrix products: 87.8 us -> none  [the longest x1 8.85 us: per_device(): jnp.dot(normed_two_low, up_full, preferred_element_type=jnp.float32)]
    reshape x15 -> x2, local copies, waits for them, and re-layouts: 67.3 us -> 0.48 us  [the longest x1 0.47 us: mesh_device(): pairs = small[:heads * head].reshape(heads, head, 2, head)]
    psum x1 -> x0, blocking collectives: 39.2 us -> none  [per_device(): lax.psum((grad_qmap, grad_kmap, norm_grads), EVERY)]
  transfers between devices with their start and end apart: 15 -> 0, of which waited for: 11 -> 0; matrix products, arithmetic and copies ran while one was open for 23% -> 0% of each run, Pallas kernels for 0% -> 0%
where the time goes in v3:
time: 323 us
  Pallas kernels  298 us (92%)
  local copies, waits for them, and re-layouts  12.5 us (4%)
  other arithmetic  11.7 us (4%)
    pallas_call x1, Pallas kernels, mesh_device(): pl.pallas_call(layer_kernel, out_shape=[jax.ShapeDtypeStruct(spread_rows,...  298 us

profile of v3, /device:TPU:0, one launch (start us, length us, event | category | flops | bytes accessed | tf_op | source)
XLA Modules:
  0.0 323.0 jit_solution(2825979521025009411)
XLA Ops:
  0.7 0.8 compare_reduce_fusion
  1.5 0.7 broadcast_in_dim.2.refs_2_
  2.1 0.8 maximum_negate_fusion
  2.9 1.5 pad_maximum_fusion.refs_3_
  4.4 2.1 copy.25
  6.5 0.7 stack.27
  7.2 0.7 stack.28
  7.9 0.7 stack.29
  8.5 0.7 stack.30
  9.2 0.6 fusion.7.refs_4_
  9.8 298.1 %layer.1 = (bf16[2,4,256,768]{3,2,1,0:T(8,128)(2,1)}, bf16[2,4,256,768]{3,2,1,0:T(8,128)(2,1)}, bf16[3,192,384]{2,1,0:T(8,128)(2,1)}, bf16[192,384]{1,0:T(8,128)...) custom-call(bf16[2,1,1024,768]{3,2,1,0:T(8,128)(2,1)} %refs_0_.1, ...), custom_call_target="tpu_custom_call" | custom-call | tf_op jit(solution)/shard_map/layer/pallas_call | solution.py:1235
  307.9 1.0 slice.31
  309.0 0.5 reshape.69
  309.4 0.1 fusion.8
  309.6 0.7 constant_dynamic-slice_fusion
  310.3 0.9 slice.34
  311.2 0.7 dynamic-slice_reduce_fusion
  311.9 0.0 copy-start.2
  311.9 5.1 %bitcast_convert_fusion = f32[2,1,1024,768]{3,2,1,0:T(8,128)} fusion(bf16[2,1,1024,768]{3,2,1,0:T(8,128)(2,1)} %bitcast.25), kind=kLoop, calls=%fused_computation | loop fusion | flops 1572864 | bytes 9437184
  317.0 0.0 copy-start.1
  317.0 0.0 copy-start.3
  317.0 0.0 copy-done.2
  317.0 0.1 convert_bitcast_fusion
  317.1 0.0 copy-start.4
  317.1 1.4 copy.30
  318.5 0.0 copy-start
  318.5 0.0 copy-done.1
  318.5 1.1 convert_element_type.34
  319.6 0.0 copy-done.3
  319.6 1.0 convert_bitcast_fusion.1
  320.6 0.0 copy-done.4
  320.6 0.7 convert_element_type.33
  321.3 0.0 copy-done
  321.3 1.7 copy.32
  (5 shorter events, 0.1 us)
Async XLA Ops:
  311.9 5.2 %copy-start.2 = (bf16[384,768]{1,0:T(8,128)(2,1)S(1)}, bf16[384,768]{1,0:T(8,128)(2,1)}, u32[]{:S(2)}) copy-start(bf16[384,768]{1,0:T(8,128)(2,1)} %get-tuple-element.24) | copy-start | bytes 1769476
  317.0 1.5 copy-start.1
  317.0 2.6 copy-start.3
  317.1 3.5 %copy-start.4 = (bf16[192,384]{1,0:T(8,128)(2,1)S(1)}, bf16[192,384]{1,0:T(8,128)(2,1)}, u32[]{:S(2)}) copy-start(bf16[192,384]{1,0:T(8,128)(2,1)} %get-tuple-element.22) | copy-start | bytes 442372
  318.5 2.8 copy-start

commit v4 on v3

--- a/solution.py
+++ b/solution.py
@@ -514,15 +514,16 @@
     inputs, cotangent, flags, maps, norms = refs[:5]
     shards = refs[5:9]
     all_out, all_in = refs[9:11]
-    outs, small_out = refs[11:15], refs[15]
-    w, mx, nrm, x, g, n1, qkv, feat = refs[16:20], *refs[20:27]
-    prior, sums_in, states, z_buf, s_in, z_in, s_out, z_out = refs[27:35]
-    o, rden, num, mid, n2, a, gp, rows_out = refs[35:43]
-    gm, dnum, dden, dproj, rows_in, turned = refs[43:49]
-    pair_in, xy_in, part, tz_in, last = (refs[49 + 4 * i : 53 + 4 * i] for i in range(5))
-    small, small_pair, small_own, small_in, small_sum = refs[69:74]
-    local_sem, send_sem, extra_sem, z_sem, xy_sem, pair_sem = refs[74:80]
-    scan_sem, rows_sem, gpair_sem, gxy_sem, gz_sem, last_sem, small_sem = refs[80:87]
+    outs, maps_out, norms_out = refs[11:15], refs[15:17], refs[17]
+    w, mx, nrm, x, g, n1, qkv, feat = refs[18:22], *refs[22:29]
+    prior, sums_in, states, z_buf, s_in, z_in, s_out, z_out = refs[29:37]
+    o, rden, num, mid, n2, a, gp, rows_out = refs[37:45]
+    gm, dnum, dden, dproj, rows_in, turned = refs[45:51]
+    pair_in, xy_in, part, tz_in, last = (refs[51 + 4 * i : 55 + 4 * i] for i in range(5))
+    small, small_pair, small_own, small_in, small_sum, small_all = refs[71:77]
+    vec, vec_pair, vec_own, vec_in, vec_sum, vec_all = refs[77:83]
+    local_sem, send_sem, extra_sem, z_sem, xy_sem, pair_sem = refs[83:89]
+    scan_sem, rows_sem, gpair_sem, gxy_sem, gz_sem, last_sem, small_sem = refs[89:96]
     wq, wo, wu, wd = w
     d = x.shape[1]
     ff = a.shape[1]
@@ -548,6 +549,8 @@
         fetched.append(fetch(inputs.at[i, 0, at(t * half_rows, half_rows, 16), :], x.at[rows], local_sem.at[i]))
         fetched.append(fetch(cotangent.at[i, 0, at(t * half_rows, half_rows, 16), :], g.at[rows], local_sem.at[2 + i]))
     h3 = maps.shape[1]
+    head_rows = small.shape[1]
+    pairs_of = (0, 1, 3, 4)
     lo_norm = d // 2
 
     def map_place(ff_, tt):
@@ -561,32 +564,51 @@
     shard_copies = [fetch(shards[m], shard(w[m], m, f, t), local_sem.at[6 + m]) for m in range(4)]
     z_buf[...] = jnp.zeros_like(z_buf)
     small[...] = jnp.zeros_like(small)
+    vec[...] = jnp.zeros_like(vec)
     meet(f, c, t)
 
     order = (0, 1, 2, 3)
-    for k in range(1, 8):
-        peer = (f if k < 4 else 1 - f, c, lax.rem(t + k, 4))
-        put(maps, map_place(f, t), extra_sem.at[k], peer)
     put(norms, norm_place(f), extra_sem.at[0], partner)
+    put(maps, map_place(f, t), extra_sem.at[4], partner)
     for m in order:
         for k in range(1, 4):
             put(quarter(shards[m], m, c), piece(w[m], m, f, c, t), z_sem.at[m, k], (f, c, lax.rem(t + k, 4)))
+        if m == 0:
+            for k in range(1, 4):
+                put(maps, map_place(f, t), extra_sem.at[k], (f, c, lax.rem(t + k, 4)))
     for m in order:
         put(shards[m], shard(w[m], m, f, t), pair_sem.at[m], partner)
 
     def forward(m, k):
         got = piece(w[m], m, f, c, lax.rem(t + 4 - k, 4))
         arrived(got, z_sem.at[m, k])
-        for j in range(1, 4):
+        for j in range(1, 3):
             put(got, got, xy_sem.at[m, k, j], (f, c ^ j, t))
         put(got, got, pair_sem.at[m], partner)
 
+    def relay(m, k):
+        for j in range(1, 3):
+            got = piece(w[m], m, f, c ^ j, lax.rem(t + 4 - k, 4))
+            arrived(got, xy_sem.at[m, k, j])
+            if (m + k + j) % 2:
+                put(got, got, xy_sem.at[m, k, 3], (f, c ^ 3 ^ j, t))
+            put(got, got, pair_sem.at[m], partner)
+
     def across(m):
         for k in range(1, 4):
-            for j in range(1, 4):
-                got = piece(w[m], m, f, c ^ j, lax.rem(t + 4 - k, 4))
-                arrived(got, xy_sem.at[m, k, j])
-                put(got, got, pair_sem.at[m], partner)
+            got = piece(w[m], m, f, c ^ 3, lax.rem(t + 4 - k, 4))
+            arrived(got, xy_sem.at[m, k, 3])
+            put(got, got, pair_sem.at[m], partner)
+
+    def take_maps():
+        for k in range(1, 4):
+            got = map_place(f, lax.rem(t + 4 - k, 4))
+            arrived(got, extra_sem.at[k])
+            put(got, got, extra_sem.at[4 + k], partner)
+
+    def maps_here():
+        for k in range(4):
+            arrived(map_place(1 - f, lax.rem(t + 4 - k, 4)), extra_sem.at[4 + k])
 
     def complete(m):
         shard_copies[m].wait()
@@ -607,12 +629,12 @@
         e, _unused = statistics(x[rows, :].astype(f32))
         n1[rows, :] = (e * nrm[0:1, :] + nrm[1:2, :]).astype(bf16)
 
+    take_maps()
     for k in range(1, 4):
+        relay(0, k)
         forward(1, k)
     across(0)
     forward(2, 1)
-    for k in range(1, 8):
-        arrived(map_place(f if k < 4 else 1 - f, lax.rem(t + 8 - k, 4)), extra_sem.at[k])
     complete(0)
 
     chunks = d // 256
@@ -622,6 +644,11 @@
         kind, j = i // chunks, lax.rem(i, chunks)
         cols = at(j * 256, 256, 128)
         qkv[kind, :, cols] = mm(n1[...], wq[kind, cols, :], NT).astype(bf16)
+
+    for k in range(1, 4):
+        relay(1, k)
+    forward(2, 2)
+    maps_here()
 
     pairs = d // 128
 
@@ -631,10 +658,8 @@
         bottom = jnp.concatenate([zero, mx[side, 2 * p + 1]], 1)
         return jnp.concatenate([top, bottom], 0)
 
-    @pl.loop(0, 4 * pairs)
-    def _(i):
-        side, rest = i // (2 * pairs), lax.rem(i, 2 * pairs)
-        b, p = rest // pairs, lax.rem(rest, pairs)
+    def features_of(side, i):
+        b, p = i // pairs, lax.rem(i, pairs)
         rows = at(b * half_rows, half_rows, 16)
         logits = mm(qkv[side, rows, at(p * 128, 128, 128)], pair_map(side, p))
         for odd in range(2):
@@ -644,6 +669,14 @@
             e = jnp.exp(part_ - jnp.where(first, low_top, high_top))
             total = mm(e.astype(bf16), ones64)
             feat[side, rows, at(p * 256 + odd * 128, 128, 128)] = (e / total).astype(bf16)
+
+    @pl.loop(0, 2 * pairs)
+    def _(i):
+        features_of(1, i)
+
+    forward(2, 3)
+    across(1)
+    relay(2, 1)
 
     @pl.loop(0, 2 * pairs)
     def _(i):
@@ -693,9 +726,15 @@
         arrived(z_in.at[pl.ds(0, 15)], scan_sem.at[sem0 + 3])
 
     scan_out(0)
-    across(1)
-    forward(2, 2)
-    forward(2, 3)
+    relay(2, 2)
+    for k in range(1, 4):
+        forward(3, k)
+
+    @pl.loop(0, 2 * pairs)
+    def _(i):
+        features_of(0, i)
+
+    relay(2, 3)
 
     def mask_of(b, turn):
         row = lax.broadcasted_iota(jnp.int32, (half_rows, half_rows), 0)
@@ -723,7 +762,7 @@
 
     scan_back(0, False)
     for k in range(1, 4):
-        forward(3, k)
+        relay(3, k)
     complete(1)
     scan_end(0)
 
@@ -786,20 +825,17 @@
 
     links = []
 
-    def pass_on(i, way, hop, block):
+    def pass_on(i, b, way, hop, block):
         dst = (all_out, all_in)[i]
         src = (rows_out, rows_in)[i]
-        peer = (f, c, t + 1 if way == 0 else t - 1)
-        copies = []
-        for b in range(2):
-            origin = src.at[pl.ds(b * half_rows, half_rows)] if hop == 0 else dst.at[b, block]
-            copies.append(pltpu.make_async_remote_copy(
-                src_ref=origin, dst_ref=dst.at[b, block], send_sem=rows_sem.at[i, way, hop, 0],
-                recv_sem=rows_sem.at[i, way, hop, 1], device_id=peer, device_id_type=MESH,
-            ))
-        return copies
-
-    def rows_hop(i, hop):
+        origin = src.at[pl.ds(b * half_rows, half_rows)] if hop == 0 else dst.at[b, block]
+        return pltpu.make_async_remote_copy(
+            src_ref=origin, dst_ref=dst.at[b, block], send_sem=rows_sem.at[i, way, hop, b, 0],
+            recv_sem=rows_sem.at[i, way, hop, b, 1], device_id=(f, c, t + 1 if way == 0 else t - 1),
+            device_id_type=MESH,
+        )
+
+    def rows_hop(i, b, hop):
         dst = (all_out, all_in)[i]
         for way in range(2):
             block = t - hop if way == 0 else t + hop
@@ -808,29 +844,28 @@
             if hop > 0:
                 @pl.when(here)
                 def _():
-                    arrived(dst.at[:, 0], rows_sem.at[i, way, hop - 1, 1])
+                    arrived(dst.at[b, 0], rows_sem.at[i, way, hop - 1, b, 1])
             if hop < 3:
                 @pl.when(jnp.logical_and(here, more))
                 def _():
-                    for copy in pass_on(i, way, hop, block):
-                        copy.start()
+                    pass_on(i, b, way, hop, block).start()
 
     def rows_sent(i):
-        for hop in range(3):
-            for way in range(2):
-                block = t - hop if way == 0 else t + hop
-                here = block >= 0 if way == 0 else block <= 3
-                more = t < 3 if way == 0 else t > 0
-
-                @pl.when(jnp.logical_and(here, more))
-                def _():
-                    for copy in pass_on(i, way, hop, block):
-                        copy.wait_send()
+        for b in range(2):
+            for hop in range(3):
+                for way in range(2):
+                    block = t - hop if way == 0 else t + hop
+                    here = block >= 0 if way == 0 else block <= 3
+                    more = t < 3 if way == 0 else t > 0
+
+                    @pl.when(jnp.logical_and(here, more))
+                    def _():
+                        pass_on(i, b, way, hop, block).wait_send()
 
     own_rows = []
     for b in range(2):
         own_rows.append(fetch(rows_out.at[pl.ds(b * half_rows, half_rows)], all_out.at[b, t], local_sem.at[2 + b]))
-    rows_hop(0, 0)
+        rows_hop(0, b, 0)
 
     def grad_pair(m):
         if m < 2:
@@ -954,6 +989,7 @@
         wd[:, cols] = mm(turned[...], a[:, cols]).astype(bf16)
 
     grad_pair(3)
+    rows_hop(0, 0, 1)
 
     @pl.loop(0, chunks)
     def _(i):
@@ -965,8 +1001,8 @@
         rows = at(i * step, step, 16)
         e, rstd = statistics(mid[rows, :])
         grad = num[rows, :]
-        nrm[6:7, :] += jnp.sum(grad * e, 0, keepdims=True)
-        nrm[7:8, :] += jnp.sum(grad, 0, keepdims=True)
+        vec[2:3, :] += jnp.sum(grad * e, 0, keepdims=True)
+        vec[3:4, :] += jnp.sum(grad, 0, keepdims=True)
         total = g[rows, :].astype(f32) + norm_back(grad, e, rstd, nrm[2:3, :])
         mid[rows, :] = total
         gm[rows, :] = total.astype(bf16)
@@ -1000,7 +1036,6 @@
             z_buf[2 * p + odd] = jnp.where(slot, tall, z_buf[2 * p + odd])
 
     scan_out(4)
-    rows_hop(0, 1)
 
     turn(n2)
 
@@ -1012,6 +1047,7 @@
     grad_pair(2)
 
     scan_back(4, True)
+    rows_hop(0, 1, 1)
 
     @pl.loop(0, chunks)
     def _(i):
@@ -1072,14 +1108,12 @@
             grads.append(total + full * sums_pair(0, b, p, odd))
         through_features(0, b, p, rows, cols, grads)
 
+    grad_xy(2)
     scan_end(4)
-    rows_hop(0, 2)
-    grad_xy(2)
-
-    @pl.loop(0, 2 * pairs)
-    def _(i):
-        b, p = i // pairs, lax.rem(i, pairs)
-        rows = at(b * half_rows, half_rows, 16)
+    rows_hop(0, 0, 2)
+
+    def key_side(b, p):
+        rows = pl.ds(b * half_rows, half_rows)
         cols = at(p * 128, 128, 128)
         values, grad_rows = qkv[2, rows, cols], dnum[rows, cols]
         packed = dden[rows, cols]
@@ -1102,33 +1136,39 @@
         dproj[2, rows, cols] = value_grad.astype(bf16)
         through_features(1, b, p, rows, cols, grads)
 
-    grad_xy(1)
-
-    @pl.loop(0, chunks)
-    def _(i):
-        cols = at(i * 256, 256, 128)
-        total = mm(dproj[0], wq[0, :, cols])
-        for kind in range(1, 3):
-            total = total + mm(dproj[kind], wq[kind, :, cols])
-        num[:, cols] = total
-
-    @pl.loop(0, 4)
-    def _(i):
-        rows = at(i * step, step, 16)
-        e, rstd = statistics(x[rows, :].astype(f32))
-        grad = num[rows, :]
-        nrm[4:5, :] += jnp.sum(grad * e, 0, keepdims=True)
-        nrm[5:6, :] += jnp.sum(grad, 0, keepdims=True)
-        rows_in[rows, :] = (mid[rows, :] + norm_back(grad, e, rstd, nrm[0:1, :])).astype(bf16)
-
     for b in range(2):
+        @pl.loop(0, pairs)
+        def _(p):
+            key_side(b, p)
+
+        if b == 0:
+            grad_xy(1)
+            rows_hop(0, 1, 2)
+
+        @pl.loop(0, chunks)
+        def _(i):
+            cols = at(i * 256, 256, 128)
+            rows = pl.ds(b * half_rows, half_rows)
+            total = mm(dproj[0, rows, :], wq[0, :, cols])
+            for kind in range(1, 3):
+                total = total + mm(dproj[kind, rows, :], wq[kind, :, cols])
+            num[rows, cols] = total
+
+        @pl.loop(2 * b, 2 * b + 2)
+        def _(i):
+            rows = at(i * step, step, 16)
+            e, rstd = statistics(x[rows, :].astype(f32))
+            grad = num[rows, :]
+            vec[0:1, :] += jnp.sum(grad * e, 0, keepdims=True)
+            vec[1:2, :] += jnp.sum(grad, 0, keepdims=True)
+            rows_in[rows, :] = (mid[rows, :] + norm_back(grad, e, rstd, nrm[0:1, :])).astype(bf16)
+
         own_rows.append(fetch(rows_in.at[pl.ds(b * half_rows, half_rows)], all_in.at[b, t], local_sem.at[4 + b]))
-    rows_hop(1, 0)
-
-    for i in range(4):
-        for j in range(d // 128):
-            small[2 * pairs, i * (d // 128) + j : i * (d // 128) + j + 1, :] = nrm[4 + i : 5 + i, j * 128 : j * 128 + 128]
-    put(small, small_pair, small_sem.at[0], partner)
+        rows_hop(1, b, 0)
+
+    lo_map = head_rows // 2
+    put(small.at[:, at((1 - f) * lo_map, lo_map, 16), :], small_pair, small_sem.at[0], partner)
+    put(vec.at[:, at((1 - f) * lo_norm, lo_norm, 128)], vec_pair, small_sem.at[1], partner)
 
     @pl.loop(0, 3 * chunks)
     def _(i):
@@ -1138,35 +1178,76 @@
 
     grad_pair(0)
     arrived(small_pair, small_sem.at[0])
-    small_own[...] = (small[...] + small_pair[...]).astype(bf16)
-    for k in range(1, 16):
-        put(small_own.at[lax.rem(n + k, 16)], small_in.at[n], small_sem.at[1], peers[k])
-    fetch(small_own.at[n], small_in.at[n], local_sem.at[6]).wait()
+    arrived(vec_pair, small_sem.at[1])
+    for tt in range(4):
+        for side in range(2):
+            for q in range(2):
+                p = side * pairs + pairs_of[tt] + q
+                mine = small[p, at(f * lo_map, lo_map, 16), :] + small_pair[p]
+                small_own[tt, 2 * side + q] = mine.astype(bf16)
+    vec_own[...] = vec[:, at(f * lo_norm, lo_norm, 128)] + vec_pair[...]
+    for k in range(1, 4):
+        other = lax.rem(t + k, 4)
+        put(small_own.at[other], small_in.at[t], small_sem.at[2], (f, c, other))
+        put(vec_own, vec_in.at[t], small_sem.at[3], (f, c, other))
+    own_small = [
+        fetch(small_own.at[t], small_in.at[t], local_sem.at[6]),
+        fetch(vec_own, vec_in.at[t], local_sem.at[7]),
+    ]
     grad_z(3)
-    rows_hop(1, 1)
+    rows_hop(1, 0, 1)
     grad_xy(0)
+    for copy in own_small:
+        copy.wait()
+    arrived(small_in.at[pl.ds(0, 3)], small_sem.at[2])
+    arrived(vec_in.at[pl.ds(0, 3)], small_sem.at[3])
+    total = small_in[0].astype(f32)
+    sums = vec_in[0]
+    for i in range(1, 4):
+        total = total + small_in[i].astype(f32)
+        sums = sums + vec_in[i]
+    small_sum[...] = total.astype(bf16)
+    vec_sum[...] = sums
+    for j in range(1, 4):
+        put(small_sum, small_all.at[c], small_sem.at[4], (f, c ^ j, t))
+        put(vec_sum, vec_all.at[c], small_sem.at[5], (f, c ^ j, t))
+    own_small = [
+        fetch(small_sum, small_all.at[c], local_sem.at[6]),
+        fetch(vec_sum, vec_all.at[c], local_sem.at[7]),
+    ]
+    rows_hop(1, 1, 1)
     grad_z(2)
     grad_z(1)
     grad_last(3)
-    rows_hop(0, 3)
-    rows_hop(1, 2)
-    arrived(small_in.at[pl.ds(0, 15)], small_sem.at[1])
-    total = jnp.zeros(small_in.shape[1:], f32)
-    for i in range(16):
-        total = total + small_in[i].astype(f32)
-    small_sum[...] = total
-    for k in range(1, 16):
-        put(small_sum, small_out.at[n], small_sem.at[2], peers[k])
-    fetch(small_sum, small_out.at[n], local_sem.at[6]).wait()
+    rows_hop(1, 0, 2)
+    for copy in own_small:
+        copy.wait()
+    arrived(small_all.at[pl.ds(0, 3)], small_sem.at[4])
+    arrived(vec_all.at[pl.ds(0, 3)], small_sem.at[5])
+    total = small_all[0].astype(f32)
+    sums = vec_all[0]
+    for i in range(1, 4):
+        total = total + small_all[i].astype(f32)
+        sums = sums + vec_all[i]
+    norms_out[...] = sums
+    odd_slot = lax.rem(t, 2) == 1
+    for side in range(2):
+        near, far = total[2 * side], total[2 * side + 1]
+        near_high, far_high = pltpu.roll(near, 64, 1), pltpu.roll(far, 64, 1)
+        for j, (high, low) in enumerate(((near_high, near), (far, near_high), (far_high, far))):
+            maps_out[side][j] = jnp.where(odd_slot, high, low)[:, :64]
     grad_last(2)
     grad_last(1)
+    rows_hop(1, 1, 2)
     grad_z(0)
+    rows_hop(0, 0, 3)
+    rows_hop(0, 1, 3)
     grad_last(0)
     for m in range(4):
         for j in range(1, 4):
             arrived(last[m], last_sem.at[m, j])
-    arrived(small_out.at[pl.ds(0, 15)], small_sem.at[2])
-    rows_hop(1, 3)
+    rows_hop(1, 0, 3)
+    rows_hop(1, 1, 3)
     for copy in own_rows:
         copy.wait()
     for copy in started:
@@ -1210,7 +1291,8 @@
     low = [(3, d, d), (d, d), (d, ff), (d, ff), (2, heads, head, 128)]
     state_rows = heads // 2 * 128
     pieces = (16, micro, state_rows // 16, 128)
-    small = (16, 64, 128)
+    tiny = [(2 * (heads // 2), head, 128), (2 * (heads // 2), head // 2, 128), (4, 4, head // 2, 128)]
+    maps_shape = (heads // 4, head // 2, head)
     scratch = [pltpu.VMEM(s, bf16) for s in low]
     scratch += [pltpu.VMEM((8, d), f32)]
     scratch += [pltpu.VMEM((rows, d), bf16)] * 3
@@ -1227,27 +1309,25 @@
     scratch += [pltpu.VMEM(s, bf16) for s in sums]
     scratch += [pltpu.VMEM((3,) + s, bf16) for s in last]
     scratch += [pltpu.VMEM(s, bf16) for s in last]
-    scratch += [pltpu.VMEM(small, f32)] * 2 + [pltpu.VMEM(small, bf16)] * 2 + [pltpu.VMEM(small[1:], f32)]
+    scratch += [pltpu.VMEM(s, f32) for s in tiny[:2]] + [pltpu.VMEM(tiny[2], bf16)] * 2
+    scratch += [pltpu.VMEM(tiny[2][1:], bf16), pltpu.VMEM(tiny[2], bf16)]
+    scratch += [pltpu.VMEM(s, f32) for s in ((8, d), (8, d // 2), (8, d // 2), (4, 8, d // 2), (8, d // 2), (4, 8, d // 2))]
     scratch += [dma((14,)), dma(()), dma((8,)), dma((4, 4)), dma((4, 4, 4)), dma((4,))]
-    scratch += [dma((8,)), dma((2, 2, 3, 2)), dma((4,)), dma((4, 4)), dma((4, 4)), dma((4, 4)), dma((3,))]
+    scratch += [dma((8,)), dma((2, 2, 3, 2, 2)), dma((4,)), dma((4, 4)), dma((4, 4)), dma((4, 4)), dma((6,))]
     spread_rows = (micro, 4, span, d)
     anywhere = pl.BlockSpec(memory_space=pl.ANY)
-    all_out, all_in, share_0, share_1, share_2, share_3, small = pl.pallas_call(
+    all_out, all_in, share_0, share_1, share_2, share_3, map_0, map_1, norm_grads = pl.pallas_call(
         layer_kernel,
         out_shape=[jax.ShapeDtypeStruct(spread_rows, bf16)] * 2
         + [jax.ShapeDtypeStruct(s, bf16) for s in outs]
-        + [jax.ShapeDtypeStruct(small, f32)],
+        + [jax.ShapeDtypeStruct(maps_shape, f32)] * 2
+        + [jax.ShapeDtypeStruct((8, d // 2), f32)],
         in_specs=[anywhere] * 2 + [pl.BlockSpec(memory_space=pltpu.VMEM)] + [anywhere] * 6,
-        out_specs=[anywhere] * 7,
+        out_specs=[anywhere] * 6 + [pl.BlockSpec(memory_space=pltpu.VMEM)] * 3,
         scratch_shapes=scratch,
         compiler_params=pltpu.CompilerParams(collective_id=0, has_side_effects=True, vmem_limit_bytes=67043328),
         name="layer",
     )(inputs, cotangent, flags, maps, norms, qkv_weight.transpose(0, 2, 1), out_weight, up_weight, down_weight.T)
-    small = small.reshape(-1, 128)
-    pairs = small[: heads * head].reshape(heads, head, 2, head)
-    pairs = pairs.transpose(0, 2, 1, 3).reshape(2, heads, head, head)
-    norm_grads = small[heads * head :].reshape(-1)[: 4 * d].reshape(4, d)
-    norm_grads = lax.dynamic_slice_in_dim(norm_grads, lax.axis_index("fsdp") * (d // 2), d // 2, 1)
     return (
         all_out.reshape(inputs.shape),
         all_in.reshape(inputs.shape).astype(f32),
@@ -1255,8 +1335,8 @@
         share_1.astype(f32),
         share_2.astype(f32),
         share_3.astype(f32).T,
-        own_maps(pairs[0]),
-        own_maps(pairs[1]),
+        map_0,
+        map_1,
         norm_grads[0],
         norm_grads[1],
         norm_grads[2],

time: 323 us -> 296 us (0.916)
  Pallas kernels: 298 us -> 272 us
    pallas_call x1, Pallas kernels: 298 us -> 272 us  [mesh_device(): pl.pallas_call(layer_kernel, out_shape=[jax.ShapeDtypeStruct(spread_rows,...]
where the time goes in v4:
time: 296 us; the launch traced here: 295 us
  Pallas kernels  272 us (92%)
  other arithmetic  11.7 us (4%)
  local copies, waits for them, and re-layouts  11.3 us (4%)
    pallas_call x1, Pallas kernels, mesh_device(): pl.pallas_call(layer_kernel, out_shape=[jax.ShapeDtypeStruct(spread_rows,...  272 us
    unnamed x19, local copies, waits for them, and re-layouts  6.43 us

profile of v4, /device:TPU:0, one launch (start us, length us, event | category | flops | bytes accessed | tf_op | source)
XLA Modules:
  0.0 295.3 jit_solution(14372528096720711938)
XLA Ops:
  0.6 0.8 maximum_negate_fusion
  1.4 1.5 pad_maximum_fusion.refs_3_
  2.9 0.8 compare_reduce_fusion
  3.7 0.7 broadcast_in_dim.2.refs_2_
  4.4 2.1 copy.25
  6.5 0.7 stack.27
  7.2 0.7 stack.28
  7.9 0.7 stack.29
  8.5 0.7 stack.30
  9.2 0.6 fusion.7.refs_4_
  9.8 271.6 %layer.1 = (bf16[2,4,256,768]{3,2,1,0:T(8,128)(2,1)}, bf16[2,4,256,768]{3,2,1,0:T(8,128)(2,1)}, bf16[3,192,384]{2,1,0:T(8,128)(2,1)}, bf16[192,384]{1,0:T(8,128)...) custom-call(bf16[2,1,1024,768]{3,2,1,0:T(8,128)(2,1)} %refs_0_.1, ...), custom_call_target="tpu_custom_call" | custom-call | tf_op jit(solution)/shard_map/layer/pallas_call | solution.py:1319
  281.5 1.5 slice_reduce_fusion
  282.9 0.0 copy-start.2
  282.9 5.1 %bitcast_convert_fusion = f32[2,1,1024,768]{3,2,1,0:T(8,128)} fusion(bf16[2,1,1024,768]{3,2,1,0:T(8,128)(2,1)} %bitcast.20), kind=kLoop, calls=%fused_computation | loop fusion | flops 1572864 | bytes 9437184
  288.1 0.0 copy-start.1
  288.1 0.0 copy-start.3
  288.1 0.0 copy-done.2
  288.1 0.1 convert_bitcast_fusion
  288.2 0.0 copy-start.4
  288.2 1.4 copy.28
  289.6 0.0 copy-start
  289.6 0.0 copy-done.1
  289.6 1.1 convert_element_type.34
  290.7 0.0 copy-done.3
  290.7 1.0 convert_bitcast_fusion.1
  291.6 0.0 copy-done.4
  291.6 0.7 convert_element_type.33
  292.4 0.0 copy-done
  292.4 0.0 copy-start.6
  292.4 0.0 copy-start.5
  292.4 1.7 copy.32
  294.1 0.0 copy-done.6
  294.1 0.6 copy.33
  294.7 0.0 copy-done.5
  294.7 0.6 copy.34
  (1 shorter events, 0.0 us)
Async XLA Ops:
  282.9 5.2 %copy-start.2 = (bf16[384,768]{1,0:T(8,128)(2,1)S(1)}, bf16[384,768]{1,0:T(8,128)(2,1)}, u32[]{:S(2)}) copy-start(bf16[384,768]{1,0:T(8,128)(2,1)} %get-tuple-element.26) | copy-start | bytes 1769476
  288.1 1.5 copy-start.1
  288.1 2.6 copy-start.3
  288.2 3.5 %copy-start.4 = (bf16[192,384]{1,0:T(8,128)(2,1)S(1)}, bf16[192,384]{1,0:T(8,128)(2,1)}, u32[]{:S(2)}) copy-start(bf16[192,384]{1,0:T(8,128)(2,1)} %get-tuple-element.24) | copy-start | bytes 442372
  289.6 2.8 copy-start
  292.4 1.7 copy-start.6
  292.4 2.3 copy-start.5

commit v5 on v4

--- a/solution.py
+++ b/solution.py
@@ -453,6 +453,15 @@
     return ref.at[at(c * h, h, 16), :]
 
 
+def two_of(ref, m, side):
+    if m == 0:
+        return ref.at[:, pl.ds(2 * side, 2)]
+    if m == 1:
+        return ref.at[pl.ds(2 * side, 2)]
+    w = ref.shape[1] // 2
+    return ref.at[:, pl.ds(side * w, w)]
+
+
 def tensor_part(ref, m, t):
     if m == 0:
         return ref.at[:, t]
@@ -901,12 +910,38 @@
                 rows = at(i * 32, 32, 16)
                 mine = w[m][at(f * (d // 2) + i * 32, 32, 16), :].astype(f32)
                 pair_in[m][rows, :] = (mine + pair_in[m][rows, :].astype(f32)).astype(bf16)
-        for j in range(1, 4):
-            put(context_part(pair_in[m], m, c ^ j), xy_in[m].at[j - 1], gxy_sem.at[m, j], (f, c ^ j, t))
+        for side in range(2):
+            way = 1 + side
+            for i, owner in ((1, 3), (0, way)):
+                put(
+                    two_of(context_part(pair_in[m], m, c ^ owner), m, side), two_of(xy_in[m].at[i], m, side),
+                    gxy_sem.at[m, side, i], (f, c ^ way, t),
+                )
+
+    def grad_mid(m):
+        for side in range(2):
+            way = 1 + side
+            rest = two_of(xy_in[m].at[1], m, side)
+            mine = two_of(context_part(pair_in[m], m, c ^ 3 ^ way), m, side)
+            arrived(rest, gxy_sem.at[m, side, 1])
+            if m == 0:
+                @pl.loop(0, 6)
+                def _(i):
+                    kind, tt = i // 2, lax.rem(i, 2)
+                    rest[kind, tt] = (mine[kind, tt].astype(f32) + rest[kind, tt].astype(f32)).astype(bf16)
+            elif m == 1:
+                rest[...] = (mine[...].astype(f32) + rest[...].astype(f32)).astype(bf16)
+            else:
+                @pl.loop(0, d // 8 // 16)
+                def _(i):
+                    rows = at(i * 16, 16, 16)
+                    rest[rows, :] = (mine[rows, :].astype(f32) + rest[rows, :].astype(f32)).astype(bf16)
+            put(rest, two_of(xy_in[m].at[2], m, side), gxy_sem.at[m, side, 2], (f, c ^ 3 ^ way, t))
 
     def grad_z(m):
-        for j in range(1, 4):
-            arrived(xy_in[m].at[j - 1], gxy_sem.at[m, j])
+        for side in range(2):
+            for i in (0, 2):
+                arrived(two_of(xy_in[m].at[i], m, side), gxy_sem.at[m, side, i])
         if m == 0:
             h = d // 16
 
@@ -914,7 +949,7 @@
             def _(i):
                 kind, tt = i // 4, lax.rem(i, 4)
                 total = pair_in[0][kind, tt, at(c * h, h, 16), :].astype(f32)
-                for j in range(3):
+                for j in (0, 2):
                     total = total + xy_in[0][j, kind, tt].astype(f32)
                 part[0][kind, tt] = total.astype(bf16)
         elif m == 1:
@@ -923,7 +958,7 @@
             @pl.loop(0, 4)
             def _(tt):
                 total = pair_in[1][tt, at(c * h, h, 16), :].astype(f32)
-                for j in range(3):
+                for j in (0, 2):
                     total = total + xy_in[1][j, tt].astype(f32)
                 part[1][tt] = total.astype(bf16)
         else:
@@ -931,37 +966,76 @@
             def _(i):
                 rows = at(i * 16, 16, 16)
                 total = pair_in[m][at(c * (d // 8) + i * 16, 16, 16), :].astype(f32)
-                for j in range(3):
+                for j in (0, 2):
                     total = total + xy_in[m][j, rows, :].astype(f32)
                 part[m][rows, :] = total.astype(bf16)
-        for k in range(1, 4):
-            other = lax.rem(t + k, 4)
-            put(tensor_part(part[m], m, other), tz_in[m].at[k - 1], gz_sem.at[m, k], (f, c, other))
-
-    def grad_last(m):
-        for k in range(1, 4):
-            arrived(tz_in[m].at[k - 1], gz_sem.at[m, k])
+        for way, first_ in ((0, 0), (1, 3)):
+            @pl.when(t == first_)
+            def _():
+                for owner in (3, 2, 1) if way == 0 else (0, 1, 2):
+                    step_on(m, way, owner, True).start()
+
+    def came(m, way, owner):
+        return tz_in[m].at[owner - 1 if way == 0 else 3 + owner], gz_sem.at[m, owner - 1 if way == 0 else 3 + owner]
+
+    def step_on(m, way, owner, from_end=False):
+        dst, sem = came(m, way, owner)
+        return pltpu.make_async_remote_copy(
+            src_ref=tensor_part(part[m], m, owner) if from_end else dst, dst_ref=dst, send_sem=send_sem,
+            recv_sem=sem, device_id=(f, c, t + 1 if way == 0 else t - 1), device_id_type=MESH,
+        )
+
+    def add_up(m, dst, own_part, others):
         if m == 0:
             for kind in range(3):
-                total = part[0][kind, t].astype(f32)
-                for k in range(3):
-                    total = total + tz_in[0][k, kind].astype(f32)
-                last[0][kind] = total.astype(bf16)
+                total = own_part[kind].astype(f32)
+                for other in others:
+                    total = total + other[kind].astype(f32)
+                dst[kind] = total.astype(bf16)
         elif m == 1:
-            total = part[1][t].astype(f32)
-            for k in range(3):
-                total = total + tz_in[1][k].astype(f32)
-            last[1][...] = total.astype(bf16)
+            total = own_part[...].astype(f32)
+            for other in others:
+                total = total + other[...].astype(f32)
+            dst[...] = total.astype(bf16)
         else:
-            cols = at(t * (ff // 4), ff // 4, 128)
-
             @pl.loop(0, d // 8 // 16)
             def _(i):
                 rows = at(i * 16, 16, 16)
-                total = part[m][rows, cols].astype(f32)
-                for k in range(3):
-                    total = total + tz_in[m][k, rows, :].astype(f32)
-                last[m][rows, :] = total.astype(bf16)
+                total = own_part[rows, :].astype(f32)
+                for other in others:
+                    total = total + other[rows, :].astype(f32)
+                dst[rows, :] = total.astype(bf16)
+
+    def grad_chain(m, hop):
+        for way, here in ((0, hop), (1, 3 - hop)):
+            @pl.when(t == here)
+            def _():
+                for owner in range(3, here, -1) if way == 0 else range(here):
+                    buf, sem = came(m, way, owner)
+                    arrived(buf, sem)
+                    add_up(m, buf, tensor_part(part[m], m, owner), [buf])
+                    step_on(m, way, owner).start()
+
+    def chains_sent():
+        for m in range(4):
+            for way in range(2):
+                for owner in (1, 2, 3) if way == 0 else (0, 1, 2):
+                    @pl.when(t < owner if way == 0 else t > owner)
+                    def _():
+                        step_on(m, way, owner).wait_send()
+
+    def grad_last(m):
+        for tt in range(4):
+            @pl.when(t == tt)
+            def _():
+                others = []
+                for way in range(2):
+                    if (tt > 0, tt < 3)[way]:
+                        buf, sem = came(m, way, tt)
+                        arrived(buf, sem)
+                        others.append(buf)
+                add_up(m, last[m], tensor_part(part[m], m, tt), others)
+
         for j in range(1, 4):
             put(last[m], quarter(outs[m], m, c), last_sem.at[m, j], (f, c ^ j, t))
         fetch(last[m], quarter(outs[m], m, c), local_sem.at[10 + m]).wait()
@@ -1055,6 +1129,7 @@
         wo[cols, :] = mm(o[:, cols].astype(f32).T.astype(bf16), gm[...]).astype(bf16)
 
     grad_pair(1)
+    grad_mid(3)
 
     lane = lanes_of((1, 128))
 
@@ -1111,6 +1186,7 @@
     grad_xy(2)
     scan_end(4)
     rows_hop(0, 0, 2)
+    grad_z(3)
 
     def key_side(b, p):
         rows = pl.ds(b * half_rows, half_rows)
@@ -1144,6 +1220,12 @@
         if b == 0:
             grad_xy(1)
             rows_hop(0, 1, 2)
+            grad_mid(2)
+            grad_chain(3, 1)
+        else:
+            grad_mid(1)
+            grad_z(2)
+            grad_chain(3, 2)
 
         @pl.loop(0, chunks)
         def _(i):
@@ -1194,9 +1276,11 @@
         fetch(small_own.at[t], small_in.at[t], local_sem.at[6]),
         fetch(vec_own, vec_in.at[t], local_sem.at[7]),
     ]
-    grad_z(3)
     rows_hop(1, 0, 1)
+    grad_last(3)
     grad_xy(0)
+    grad_chain(2, 1)
+    grad_z(1)
     for copy in own_small:
         copy.wait()
     arrived(small_in.at[pl.ds(0, 3)], small_sem.at[2])
@@ -1216,9 +1300,12 @@
         fetch(vec_sum, vec_all.at[c], local_sem.at[7]),
     ]
     rows_hop(1, 1, 1)
-    grad_z(2)
-    grad_z(1)
-    grad_last(3)
+    grad_chain(2, 2)
+    grad_chain(1, 1)
+    grad_mid(0)
+    grad_last(2)
+    grad_chain(1, 2)
+    grad_z(0)
     rows_hop(1, 0, 2)
     for copy in own_small:
         copy.wait()
@@ -1236,10 +1323,10 @@
         near_high, far_high = pltpu.roll(near, 64, 1), pltpu.roll(far, 64, 1)
         for j, (high, low) in enumerate(((near_high, near), (far, near_high), (far_high, far))):
             maps_out[side][j] = jnp.where(odd_slot, high, low)[:, :64]
-    grad_last(2)
+    grad_chain(0, 1)
     grad_last(1)
     rows_hop(1, 1, 2)
-    grad_z(0)
+    grad_chain(0, 2)
     rows_hop(0, 0, 3)
     rows_hop(0, 1, 3)
     grad_last(0)
@@ -1252,6 +1339,7 @@
         copy.wait()
     for copy in started:
         copy.wait_send()
+    chains_sent()
     rows_sent(0)
     rows_sent(1)
 
@@ -1307,13 +1395,13 @@
     scratch += [pltpu.VMEM(s, bf16) for s in own]
     scratch += [pltpu.VMEM((3,) + s, bf16) for s in sums]
     scratch += [pltpu.VMEM(s, bf16) for s in sums]
-    scratch += [pltpu.VMEM((3,) + s, bf16) for s in last]
+    scratch += [pltpu.VMEM((6,) + s, bf16) for s in last]
     scratch += [pltpu.VMEM(s, bf16) for s in last]
     scratch += [pltpu.VMEM(s, f32) for s in tiny[:2]] + [pltpu.VMEM(tiny[2], bf16)] * 2
     scratch += [pltpu.VMEM(tiny[2][1:], bf16), pltpu.VMEM(tiny[2], bf16)]
     scratch += [pltpu.VMEM(s, f32) for s in ((8, d), (8, d // 2), (8, d // 2), (4, 8, d // 2), (8, d // 2), (4, 8, d // 2))]
     scratch += [dma((14,)), dma(()), dma((8,)), dma((4, 4)), dma((4, 4, 4)), dma((4,))]
-    scratch += [dma((8,)), dma((2, 2, 3, 2, 2)), dma((4,)), dma((4, 4)), dma((4, 4)), dma((4, 4)), dma((6,))]
+    scratch += [dma((8,)), dma((2, 2, 3, 2, 2)), dma((4,)), dma((4, 2, 3)), dma((4, 6)), dma((4, 4)), dma((6,))]
     spread_rows = (micro, 4, span, d)
     anywhere = pl.BlockSpec(memory_space=pl.ANY)
     all_out, all_in, share_0, share_1, share_2, share_3, map_0, map_1, norm_grads = pl.pallas_call(

time: 296 us -> 264 us (0.89)
  Pallas kernels: 272 us -> 240 us
    pallas_call x1, Pallas kernels: 272 us -> 240 us  [mesh_device(): pl.pallas_call(layer_kernel, out_shape=[jax.ShapeDtypeStruct(spread_rows,...]
where the time goes in v5:
time: 264 us
  Pallas kernels  240 us (91%)
  other arithmetic  11.7 us (4%)
  local copies, waits for them, and re-layouts  11.3 us (4%)
    pallas_call x1, Pallas kernels, mesh_device(): pl.pallas_call(layer_kernel, out_shape=[jax.ShapeDtypeStruct(spread_rows,...  240 us
    unnamed x19, local copies, waits for them, and re-layouts  6.43 us

profile of v5, /device:TPU:0, one launch (start us, length us, event | category | flops | bytes accessed | tf_op | source)
XLA Modules:
  0.0 263.9 jit_solution(1719124486345866410)
XLA Ops:
  0.6 0.8 maximum_negate_fusion
  1.4 1.5 pad_maximum_fusion.refs_3_
  2.9 0.8 compare_reduce_fusion
  3.7 0.7 broadcast_in_dim.2.refs_2_
  4.4 2.1 copy.25
  6.5 0.7 stack.27
  7.2 0.7 stack.28
  7.9 0.7 stack.29
  8.5 0.7 stack.30
  9.2 0.6 fusion.7.refs_4_
  9.8 240.2 %layer.1 = (bf16[2,4,256,768]{3,2,1,0:T(8,128)(2,1)}, bf16[2,4,256,768]{3,2,1,0:T(8,128)(2,1)}, bf16[3,192,384]{2,1,0:T(8,128)(2,1)}, bf16[192,384]{1,0:T(8,128)...) custom-call(bf16[2,1,1024,768]{3,2,1,0:T(8,128)(2,1)} %refs_0_.1, ...), custom_call_target="tpu_custom_call" | custom-call | tf_op jit(solution)/shard_map/layer/pallas_call | solution.py:1407
  250.0 1.5 slice_reduce_fusion
  251.5 0.0 copy-start.2
  251.5 5.1 %bitcast_convert_fusion = f32[2,1,1024,768]{3,2,1,0:T(8,128)} fusion(bf16[2,1,1024,768]{3,2,1,0:T(8,128)(2,1)} %bitcast.20), kind=kLoop, calls=%fused_computation | loop fusion | flops 1572864 | bytes 9437184
  256.6 0.0 copy-start.1
  256.6 0.0 copy-start.3
  256.7 0.0 copy-done.2
  256.7 0.1 convert_bitcast_fusion
  256.7 0.0 copy-start.4
  256.7 1.4 copy.28
  258.1 0.0 copy-start
  258.1 0.0 copy-done.1
  258.1 1.1 convert_element_type.34
  259.2 0.0 copy-done.3
  259.2 1.0 convert_bitcast_fusion.1
  260.2 0.0 copy-done.4
  260.2 0.7 convert_element_type.33
  260.9 0.0 copy-done
  260.9 0.0 copy-start.6
  260.9 0.0 copy-start.5
  260.9 1.7 copy.32
  262.6 0.0 copy-done.6
  262.6 0.6 copy.33
  263.2 0.0 copy-done.5
  263.2 0.6 copy.34
  (1 shorter events, 0.0 us)
Async XLA Ops:
  251.5 5.2 %copy-start.2 = (bf16[384,768]{1,0:T(8,128)(2,1)S(1)}, bf16[384,768]{1,0:T(8,128)(2,1)}, u32[]{:S(2)}) copy-start(bf16[384,768]{1,0:T(8,128)(2,1)} %get-tuple-element.26) | copy-start | bytes 1769476
  256.6 1.5 copy-start.1
  256.6 2.6 copy-start.3
  256.7 3.5 %copy-start.4 = (bf16[192,384]{1,0:T(8,128)(2,1)S(1)}, bf16[192,384]{1,0:T(8,128)(2,1)}, u32[]{:S(2)}) copy-start(bf16[192,384]{1,0:T(8,128)(2,1)} %get-tuple-element.24) | copy-start | bytes 442372
  258.1 2.8 %copy-start = (bf16[2,4,256,768]{3,2,1,0:T(8,128)(2,1)S(1)}, bf16[2,4,256,768]{3,2,1,0:T(8,128)(2,1)}, u32[]{:S(2)}) copy-start(bf16[2,4,256,768]{3,2,1,0:T(8,128)(2,1)} %get-tuple-element.21) | copy-start | bytes 9437188
  260.9 1.7 copy-start.6
  260.9 2.3 copy-start.5

commit v6 on v5

--- a/solution.py
+++ b/solution.py
@@ -401,8 +401,24 @@
     return pl.ds(pl.multiple_of(start, unit), size)
 
 
+GROUPS = (0, 4, 1, 2, 3)
+
+
+def of(refs, m, *index):
+    ref = refs[m % 4].at[index] if index else refs[m % 4]
+    return ref.at[kinds(m)] if m % 4 == 0 else ref
+
+
+def kinds(m):
+    return pl.ds(1, 2) if m == 0 else pl.ds(0, 1)
+
+
+def kind_count(m):
+    return 2 if m == 0 else 1
+
+
 def half(ref, m, f):
-    if m == 0:
+    if m % 4 == 0:
         w = ref.shape[2] // 2
         return ref.at[:, :, at(f * w, w, 128)]
     if m == 1:
@@ -413,7 +429,7 @@
 
 
 def shard(ref, m, f, t):
-    if m == 0:
+    if m % 4 == 0:
         w, h = ref.shape[2] // 2, ref.shape[1] // 4
         return ref.at[:, at(t * h, h, 16), at(f * w, w, 128)]
     if m == 1:
@@ -424,7 +440,7 @@
 
 
 def piece(ref, m, f, c, t):
-    if m == 0:
+    if m % 4 == 0:
         w, h = ref.shape[2] // 2, ref.shape[1] // 16
         return ref.at[:, at(t * 4 * h + c * h, h, 16), at(f * w, w, 128)]
     if m == 1:
@@ -435,7 +451,7 @@
 
 
 def quarter(ref, m, c):
-    if m == 0:
+    if m % 4 == 0:
         h = ref.shape[1] // 4
         return ref.at[:, at(c * h, h, 16), :]
     h = ref.shape[0] // 4
@@ -443,7 +459,7 @@
 
 
 def context_part(ref, m, c):
-    if m == 0:
+    if m % 4 == 0:
         h = ref.shape[2] // 4
         return ref.at[:, :, at(c * h, h, 16), :]
     if m == 1:
@@ -454,7 +470,7 @@
 
 
 def two_of(ref, m, side):
-    if m == 0:
+    if m % 4 == 0:
         return ref.at[:, pl.ds(2 * side, 2)]
     if m == 1:
         return ref.at[pl.ds(2 * side, 2)]
@@ -463,7 +479,7 @@
 
 
 def tensor_part(ref, m, t):
-    if m == 0:
+    if m % 4 == 0:
         return ref.at[:, t]
     if m == 1:
         return ref.at[t]
@@ -546,6 +562,20 @@
     def put(src, dst, recv_sem, peer):
         started.append(send(src, dst, send_sem, recv_sem, peer))
 
+    started_if = []
+
+    def put_if(pred, src, dst, recv_sem, peer):
+        def copy():
+            return pltpu.make_async_remote_copy(
+                src_ref=src, dst_ref=dst, send_sem=send_sem, recv_sem=recv_sem, device_id=peer, device_id_type=MESH,
+            )
+
+        @pl.when(pred)
+        def _():
+            copy().start()
+
+        started_if.append((pred, copy))
+
     fetched = []
 
     def fetch(src, dst, sem):
@@ -570,42 +600,49 @@
 
     fetched.append(fetch(maps, map_place(f, t), local_sem.at[4]))
     fetched.append(fetch(norms, norm_place(f), local_sem.at[5]))
-    shard_copies = [fetch(shards[m], shard(w[m], m, f, t), local_sem.at[6 + m]) for m in range(4)]
+    shard_copies = [fetch(of(shards, m), shard(of(w, m), m, f, t), local_sem.at[6 + m]) for m in range(5)]
     z_buf[...] = jnp.zeros_like(z_buf)
     small[...] = jnp.zeros_like(small)
     vec[...] = jnp.zeros_like(vec)
     meet(f, c, t)
 
-    order = (0, 1, 2, 3)
     put(norms, norm_place(f), extra_sem.at[0], partner)
     put(maps, map_place(f, t), extra_sem.at[4], partner)
-    for m in order:
-        for k in range(1, 4):
-            put(quarter(shards[m], m, c), piece(w[m], m, f, c, t), z_sem.at[m, k], (f, c, lax.rem(t + k, 4)))
+    for m in GROUPS:
+        for k, pred in ((2, None), (1, t != 3), (3, t != 0)):
+            src, dst = quarter(of(shards, m), m, c), piece(of(w, m), m, f, c, t)
+            peer = (f, c, lax.rem(t + k, 4))
+            if pred is None:
+                put(src, dst, z_sem.at[m, k], peer)
+            else:
+                put_if(pred, src, dst, z_sem.at[m, k], peer)
         if m == 0:
             for k in range(1, 4):
                 put(maps, map_place(f, t), extra_sem.at[k], (f, c, lax.rem(t + k, 4)))
-    for m in order:
-        put(shards[m], shard(w[m], m, f, t), pair_sem.at[m], partner)
+    for m in GROUPS:
+        put(of(shards, m), shard(of(w, m), m, f, t), pair_sem.at[m], partner)
 
     def forward(m, k):
-        got = piece(w[m], m, f, c, lax.rem(t + 4 - k, 4))
+        got = piece(of(w, m), m, f, c, lax.rem(t + 4 - k, 4))
         arrived(got, z_sem.at[m, k])
+        if k == 2:
+            put_if(t == 2, got, got, z_sem.at[m, 3], (f, c, t + 1))
+            put_if(t == 1, got, got, z_sem.at[m, 1], (f, c, t - 1))
         for j in range(1, 3):
             put(got, got, xy_sem.at[m, k, j], (f, c ^ j, t))
         put(got, got, pair_sem.at[m], partner)
 
     def relay(m, k):
         for j in range(1, 3):
-            got = piece(w[m], m, f, c ^ j, lax.rem(t + 4 - k, 4))
+            got = piece(of(w, m), m, f, c ^ j, lax.rem(t + 4 - k, 4))
             arrived(got, xy_sem.at[m, k, j])
-            if (m + k + j) % 2:
+            if ((0, 1, 2, 3, 1)[m] + k + j) % 2:
                 put(got, got, xy_sem.at[m, k, 3], (f, c ^ 3 ^ j, t))
             put(got, got, pair_sem.at[m], partner)
 
     def across(m):
         for k in range(1, 4):
-            got = piece(w[m], m, f, c ^ 3, lax.rem(t + 4 - k, 4))
+            got = piece(of(w, m), m, f, c ^ 3, lax.rem(t + 4 - k, 4))
             arrived(got, xy_sem.at[m, k, 3])
             put(got, got, pair_sem.at[m], partner)
 
@@ -621,9 +658,9 @@
 
     def complete(m):
         shard_copies[m].wait()
-        arrived(half(w[m], m, 1 - f), pair_sem.at[m])
-
-    for k in range(1, 4):
+        arrived(half(of(w, m), m, 1 - f), pair_sem.at[m])
+
+    for k in (2, 1, 3):
         forward(0, k)
     for copy in fetched:
         copy.wait()
@@ -639,24 +676,27 @@
         n1[rows, :] = (e * nrm[0:1, :] + nrm[1:2, :]).astype(bf16)
 
     take_maps()
-    for k in range(1, 4):
+    for k in (2, 1, 3):
         relay(0, k)
+        forward(4, k)
+    for k in (2, 1, 3):
         forward(1, k)
     across(0)
-    forward(2, 1)
+    forward(2, 2)
     complete(0)
 
     chunks = d // 256
 
-    @pl.loop(0, 3 * chunks)
-    def _(i):
+    def project(i):
         kind, j = i // chunks, lax.rem(i, chunks)
         cols = at(j * 256, 256, 128)
         qkv[kind, :, cols] = mm(n1[...], wq[kind, cols, :], NT).astype(bf16)
 
-    for k in range(1, 4):
-        relay(1, k)
-    forward(2, 2)
+    pl.loop(chunks, 3 * chunks)(project)
+
+    for k in (2, 1, 3):
+        relay(4, k)
+    forward(2, 1)
     maps_here()
 
     pairs = d // 128
@@ -683,9 +723,10 @@
     def _(i):
         features_of(1, i)
 
+    across(4)
+    for k in (2, 1, 3):
+        relay(1, k)
     forward(2, 3)
-    across(1)
-    relay(2, 1)
 
     @pl.loop(0, 2 * pairs)
     def _(i):
@@ -735,14 +776,19 @@
         arrived(z_in.at[pl.ds(0, 15)], scan_sem.at[sem0 + 3])
 
     scan_out(0)
+    complete(4)
+    pl.loop(0, chunks)(project)
     relay(2, 2)
-    for k in range(1, 4):
-        forward(3, k)
+    forward(3, 2)
 
     @pl.loop(0, 2 * pairs)
     def _(i):
         features_of(0, i)
 
+    forward(3, 1)
+    forward(3, 3)
+    across(1)
+    relay(2, 1)
     relay(2, 3)
 
     def mask_of(b, turn):
@@ -770,8 +816,9 @@
         rden[rows, at(p * 128, 128, 128)] = both[:, 128:]
 
     scan_back(0, False)
-    for k in range(1, 4):
+    for k in (2, 1, 3):
         relay(3, k)
+    across(2)
     complete(1)
     scan_end(0)
 
@@ -802,8 +849,6 @@
         rows = at(i * half_rows, half_rows, 16)
         mid[rows, :] = x[rows, :].astype(f32) + mm(o[rows, :], wo[...])
 
-    across(2)
-
     @pl.loop(0, 4)
     def _(i):
         rows = at(i * step, step, 16)
@@ -827,10 +872,12 @@
     across(3)
     complete(3)
 
-    @pl.loop(0, chunks)
-    def _(i):
-        cols = at(i * 256, 256, 128)
-        rows_out[:, cols] = (mid[:, cols] + mm(a[...], wd[cols, :], NT)).astype(bf16)
+    def branch(b):
+        @pl.loop(0, chunks)
+        def _(i):
+            rows = pl.ds(b * half_rows, half_rows)
+            cols = at(i * 256, 256, 128)
+            rows_out[rows, cols] = (mid[rows, cols] + mm(a[rows, :], wd[cols, :], NT)).astype(bf16)
 
     links = []
 
@@ -873,16 +920,17 @@
 
     own_rows = []
     for b in range(2):
+        branch(b)
         own_rows.append(fetch(rows_out.at[pl.ds(b * half_rows, half_rows)], all_out.at[b, t], local_sem.at[2 + b]))
         rows_hop(0, b, 0)
 
     def grad_pair(m):
-        if m < 2:
+        if m % 4 < 2:
             h = d // 4
             for tt in range(4):
-                if m == 0:
-                    src = w[m].at[:, pl.ds(tt * h, h), at((1 - f) * (d // 2), d // 2, 128)]
-                    put(src, pair_in[m].at[:, tt], gpair_sem.at[m], partner)
+                if m % 4 == 0:
+                    src = of(w, m).at[:, pl.ds(tt * h, h), at((1 - f) * (d // 2), d // 2, 128)]
+                    put(src, of(pair_in, m).at[:, tt], gpair_sem.at[m], partner)
                 else:
                     src = w[m].at[pl.ds(tt * h, h), at((1 - f) * (d // 2), d // 2, 128)]
                     put(src, pair_in[m].at[tt], gpair_sem.at[m], partner)
@@ -890,13 +938,13 @@
             put(half(w[m], m, 1 - f), pair_in[m], gpair_sem.at[m], partner)
 
     def grad_xy(m):
-        arrived(pair_in[m], gpair_sem.at[m])
+        arrived(of(pair_in, m), gpair_sem.at[m])
         h = d // 4
         cols = at(f * (d // 2), d // 2, 128)
-        if m == 0:
-            @pl.loop(0, 12)
+        if m % 4 == 0:
+            @pl.loop(0, 4 * kind_count(m))
             def _(i):
-                kind, tt = i // 4, lax.rem(i, 4)
+                kind, tt = i // 4 + (m == 0), lax.rem(i, 4)
                 mine = wq[kind, at(tt * h, h, 16), cols].astype(f32)
                 pair_in[0][kind, tt] = (mine + pair_in[0][kind, tt].astype(f32)).astype(bf16)
         elif m == 1:
@@ -914,18 +962,18 @@
             way = 1 + side
             for i, owner in ((1, 3), (0, way)):
                 put(
-                    two_of(context_part(pair_in[m], m, c ^ owner), m, side), two_of(xy_in[m].at[i], m, side),
+                    two_of(context_part(of(pair_in, m), m, c ^ owner), m, side), two_of(of(xy_in, m, i), m, side),
                     gxy_sem.at[m, side, i], (f, c ^ way, t),
                 )
 
     def grad_mid(m):
         for side in range(2):
             way = 1 + side
-            rest = two_of(xy_in[m].at[1], m, side)
-            mine = two_of(context_part(pair_in[m], m, c ^ 3 ^ way), m, side)
+            rest = two_of(of(xy_in, m, 1), m, side)
+            mine = two_of(context_part(of(pair_in, m), m, c ^ 3 ^ way), m, side)
             arrived(rest, gxy_sem.at[m, side, 1])
-            if m == 0:
-                @pl.loop(0, 6)
+            if m % 4 == 0:
+                @pl.loop(0, 2 * kind_count(m))
                 def _(i):
                     kind, tt = i // 2, lax.rem(i, 2)
                     rest[kind, tt] = (mine[kind, tt].astype(f32) + rest[kind, tt].astype(f32)).astype(bf16)
@@ -936,18 +984,18 @@
                 def _(i):
                     rows = at(i * 16, 16, 16)
                     rest[rows, :] = (mine[rows, :].astype(f32) + rest[rows, :].astype(f32)).astype(bf16)
-            put(rest, two_of(xy_in[m].at[2], m, side), gxy_sem.at[m, side, 2], (f, c ^ 3 ^ way, t))
+            put(rest, two_of(of(xy_in, m, 2), m, side), gxy_sem.at[m, side, 2], (f, c ^ 3 ^ way, t))
 
     def grad_z(m):
         for side in range(2):
             for i in (0, 2):
-                arrived(two_of(xy_in[m].at[i], m, side), gxy_sem.at[m, side, i])
-        if m == 0:
+                arrived(two_of(of(xy_in, m, i), m, side), gxy_sem.at[m, side, i])
+        if m % 4 == 0:
             h = d // 16
 
-            @pl.loop(0, 12)
+            @pl.loop(0, 4 * kind_count(m))
             def _(i):
-                kind, tt = i // 4, lax.rem(i, 4)
+                kind, tt = i // 4 + (m == 0), lax.rem(i, 4)
                 total = pair_in[0][kind, tt, at(c * h, h, 16), :].astype(f32)
                 for j in (0, 2):
                     total = total + xy_in[0][j, kind, tt].astype(f32)
@@ -976,18 +1024,19 @@
                     step_on(m, way, owner, True).start()
 
     def came(m, way, owner):
-        return tz_in[m].at[owner - 1 if way == 0 else 3 + owner], gz_sem.at[m, owner - 1 if way == 0 else 3 + owner]
+        slot = owner - 1 if way == 0 else 3 + owner
+        return of(tz_in, m, slot), gz_sem.at[m, slot]
 
     def step_on(m, way, owner, from_end=False):
         dst, sem = came(m, way, owner)
         return pltpu.make_async_remote_copy(
-            src_ref=tensor_part(part[m], m, owner) if from_end else dst, dst_ref=dst, send_sem=send_sem,
+            src_ref=tensor_part(of(part, m), m, owner) if from_end else dst, dst_ref=dst, send_sem=send_sem,
             recv_sem=sem, device_id=(f, c, t + 1 if way == 0 else t - 1), device_id_type=MESH,
         )
 
     def add_up(m, dst, own_part, others):
-        if m == 0:
-            for kind in range(3):
+        if m % 4 == 0:
+            for kind in range(kind_count(m)):
                 total = own_part[kind].astype(f32)
                 for other in others:
                     total = total + other[kind].astype(f32)
@@ -1013,11 +1062,11 @@
                 for owner in range(3, here, -1) if way == 0 else range(here):
                     buf, sem = came(m, way, owner)
                     arrived(buf, sem)
-                    add_up(m, buf, tensor_part(part[m], m, owner), [buf])
+                    add_up(m, buf, tensor_part(of(part, m), m, owner), [buf])
                     step_on(m, way, owner).start()
 
     def chains_sent():
-        for m in range(4):
+        for m in range(5):
             for way in range(2):
                 for owner in (1, 2, 3) if way == 0 else (0, 1, 2):
                     @pl.when(t < owner if way == 0 else t > owner)
@@ -1034,15 +1083,19 @@
                         buf, sem = came(m, way, tt)
                         arrived(buf, sem)
                         others.append(buf)
-                add_up(m, last[m], tensor_part(part[m], m, tt), others)
+                add_up(m, of(last, m), tensor_part(of(part, m), m, tt), others)
 
         for j in range(1, 4):
-            put(last[m], quarter(outs[m], m, c), last_sem.at[m, j], (f, c ^ j, t))
-        fetch(last[m], quarter(outs[m], m, c), local_sem.at[10 + m]).wait()
+            put(of(last, m), quarter(of(outs, m), m, c), last_sem.at[m, j], (f, c ^ j, t))
+        fetch(of(last, m), quarter(of(outs, m), m, c), local_sem.at[11 + m]).wait()
 
     for copy in started:
         copy.wait_send()
     started.clear()
+    for pred, copy in started_if:
+        @pl.when(pred)
+        def _():
+            copy().wait_send()
 
     @pl.loop(0, ff // 256)
     def _(i):
@@ -1184,6 +1237,19 @@
         through_features(0, b, p, rows, cols, grads)
 
     grad_xy(2)
+
+    @pl.loop(0, chunks)
+    def _(i):
+        cols = at(i * 256, 256, 128)
+        num[:, cols] = mm(dproj[0], wq[0, :, cols])
+
+    def grad_of(i):
+        kind, j = i // chunks, lax.rem(i, chunks)
+        cols = at(j * 256, 256, 128)
+        wq[kind, cols, :] = mm(dproj[kind, :, cols].astype(f32).T.astype(bf16), n1[...]).astype(bf16)
+
+    pl.loop(0, chunks)(grad_of)
+    grad_pair(4)
     scan_end(4)
     rows_hop(0, 0, 2)
     grad_z(3)
@@ -1222,8 +1288,10 @@
             rows_hop(0, 1, 2)
             grad_mid(2)
             grad_chain(3, 1)
+            grad_xy(4)
         else:
             grad_mid(1)
+            grad_mid(4)
             grad_z(2)
             grad_chain(3, 2)
 
@@ -1231,7 +1299,7 @@
         def _(i):
             cols = at(i * 256, 256, 128)
             rows = pl.ds(b * half_rows, half_rows)
-            total = mm(dproj[0, rows, :], wq[0, :, cols])
+            total = num[rows, cols]
             for kind in range(1, 3):
                 total = total + mm(dproj[kind, rows, :], wq[kind, :, cols])
             num[rows, cols] = total
@@ -1252,12 +1320,7 @@
     put(small.at[:, at((1 - f) * lo_map, lo_map, 16), :], small_pair, small_sem.at[0], partner)
     put(vec.at[:, at((1 - f) * lo_norm, lo_norm, 128)], vec_pair, small_sem.at[1], partner)
 
-    @pl.loop(0, 3 * chunks)
-    def _(i):
-        kind, j = i // chunks, lax.rem(i, chunks)
-        cols = at(j * 256, 256, 128)
-        wq[kind, cols, :] = mm(dproj[kind, :, cols].astype(f32).T.astype(bf16), n1[...]).astype(bf16)
-
+    pl.loop(chunks, 3 * chunks)(grad_of)
     grad_pair(0)
     arrived(small_pair, small_sem.at[0])
     arrived(vec_pair, small_sem.at[1])
@@ -1281,6 +1344,7 @@
     grad_xy(0)
     grad_chain(2, 1)
     grad_z(1)
+    grad_z(4)
     for copy in own_small:
         copy.wait()
     arrived(small_in.at[pl.ds(0, 3)], small_sem.at[2])
@@ -1302,9 +1366,11 @@
     rows_hop(1, 1, 1)
     grad_chain(2, 2)
     grad_chain(1, 1)
+    grad_chain(4, 1)
     grad_mid(0)
     grad_last(2)
     grad_chain(1, 2)
+    grad_chain(4, 2)
     grad_z(0)
     rows_hop(1, 0, 2)
     for copy in own_small:
@@ -1325,14 +1391,15 @@
             maps_out[side][j] = jnp.where(odd_slot, high, low)[:, :64]
     grad_chain(0, 1)
     grad_last(1)
+    grad_last(4)
     rows_hop(1, 1, 2)
     grad_chain(0, 2)
     rows_hop(0, 0, 3)
     rows_hop(0, 1, 3)
     grad_last(0)
-    for m in range(4):
+    for m in range(5):
         for j in range(1, 4):
-            arrived(last[m], last_sem.at[m, j])
+            arrived(of(last, m), last_sem.at[m, j])
     rows_hop(1, 0, 3)
     rows_hop(1, 1, 3)
     for copy in own_rows:
@@ -1400,8 +1467,8 @@
     scratch += [pltpu.VMEM(s, f32) for s in tiny[:2]] + [pltpu.VMEM(tiny[2], bf16)] * 2
     scratch += [pltpu.VMEM(tiny[2][1:], bf16), pltpu.VMEM(tiny[2], bf16)]
     scratch += [pltpu.VMEM(s, f32) for s in ((8, d), (8, d // 2), (8, d // 2), (4, 8, d // 2), (8, d // 2), (4, 8, d // 2))]
-    scratch += [dma((14,)), dma(()), dma((8,)), dma((4, 4)), dma((4, 4, 4)), dma((4,))]
-    scratch += [dma((8,)), dma((2, 2, 3, 2, 2)), dma((4,)), dma((4, 2, 3)), dma((4, 6)), dma((4, 4)), dma((6,))]
+    scratch += [dma((16,)), dma(()), dma((8,)), dma((5, 4)), dma((5, 4, 4)), dma((5,))]
+    scratch += [dma((8,)), dma((2, 2, 3, 2, 2)), dma((5,)), dma((5, 2, 3)), dma((5, 6)), dma((5, 4)), dma((6,))]
     spread_rows = (micro, 4, span, d)
     anywhere = pl.BlockSpec(memory_space=pl.ANY)
     all_out, all_in, share_0, share_1, share_2, share_3, map_0, map_1, norm_grads = pl.pallas_call(

time: 264 us -> 254 us (0.962)
  Pallas kernels: 240 us -> 230 us
    pallas_call x1, Pallas kernels: 240 us -> 230 us  [mesh_device(): pl.pallas_call(layer_kernel, out_shape=[jax.ShapeDtypeStruct(spread_rows,...]
where the time goes in v6:
time: 254 us
  Pallas kernels  230 us (91%)
  other arithmetic  11.7 us (5%)
  local copies, waits for them, and re-layouts  11.3 us (4%)
    pallas_call x1, Pallas kernels, mesh_device(): pl.pallas_call(layer_kernel, out_shape=[jax.ShapeDtypeStruct(spread_rows,...  230 us
    unnamed x19, local copies, waits for them, and re-layouts  6.43 us
    unnamed x1, other arithmetic  5.14 us

profile of v6, /device:TPU:0, one launch (start us, length us, event | category | flops | bytes accessed | tf_op | source)
XLA Modules:
  0.0 253.9 jit_solution(3196199963362486468)
XLA Ops:
  0.6 0.8 maximum_negate_fusion
  1.4 1.5 pad_maximum_fusion.refs_3_
  2.9 0.8 compare_reduce_fusion
  3.7 0.7 broadcast_in_dim.2.refs_2_
  4.4 2.1 copy.25
  6.5 0.7 stack.27
  7.2 0.7 stack.28
  7.9 0.7 stack.29
  8.5 0.7 stack.30
  9.2 0.6 fusion.7.refs_4_
  9.8 230.2 %layer.1 = (bf16[2,4,256,768]{3,2,1,0:T(8,128)(2,1)}, bf16[2,4,256,768]{3,2,1,0:T(8,128)(2,1)}, bf16[3,192,384]{2,1,0:T(8,128)(2,1)}, bf16[192,384]{1,0:T(8,128)...) custom-call(bf16[2,1,1024,768]{3,2,1,0:T(8,128)(2,1)} %refs_0_.1, ...), custom_call_target="tpu_custom_call" | custom-call | tf_op jit(solution)/shard_map/layer/pallas_call | solution.py:1474
  240.1 1.5 slice_reduce_fusion
  241.5 0.0 copy-start.2
  241.5 5.1 %bitcast_convert_fusion = f32[2,1,1024,768]{3,2,1,0:T(8,128)} fusion(bf16[2,1,1024,768]{3,2,1,0:T(8,128)(2,1)} %bitcast.20), kind=kLoop, calls=%fused_computation | loop fusion | flops 1572864 | bytes 9437184
  246.7 0.0 copy-start.1
  246.7 0.0 copy-start.3
  246.7 0.0 copy-done.2
  246.7 0.1 convert_bitcast_fusion
  246.8 0.0 copy-start.4
  246.8 1.4 copy.28
  248.2 0.0 copy-start
  248.2 0.0 copy-done.1
  248.2 1.1 convert_element_type.34
  249.3 0.0 copy-done.3
  249.3 1.0 convert_bitcast_fusion.1
  250.2 0.0 copy-done.4
  250.2 0.7 convert_element_type.33
  251.0 0.0 copy-done
  251.0 0.0 copy-start.6
  251.0 0.0 copy-start.5
  251.0 1.7 copy.32
  252.6 0.0 copy-done.6
  252.6 0.6 copy.33
  253.3 0.0 copy-done.5
  253.3 0.6 copy.34
  (1 shorter events, 0.0 us)
Async XLA Ops:
  241.5 5.2 %copy-start.2 = (bf16[384,768]{1,0:T(8,128)(2,1)S(1)}, bf16[384,768]{1,0:T(8,128)(2,1)}, u32[]{:S(2)}) copy-start(bf16[384,768]{1,0:T(8,128)(2,1)} %get-tuple-element.26) | copy-start | bytes 1769476
  246.7 1.5 copy-start.1
  246.7 2.6 %copy-start.3 = (bf16[3,192,384]{2,1,0:T(8,128)(2,1)S(1)}, bf16[3,192,384]{2,1,0:T(8,128)(2,1)}, u32[]{:S(2)}) copy-start(bf16[3,192,384]{2,1,0:T(8,128)(2,1)} %get-tuple-element.23) | copy-start | bytes 1327108
  246.8 3.5 %copy-start.4 = (bf16[192,384]{1,0:T(8,128)(2,1)S(1)}, bf16[192,384]{1,0:T(8,128)(2,1)}, u32[]{:S(2)}) copy-start(bf16[192,384]{1,0:T(8,128)(2,1)} %get-tuple-element.24) | copy-start | bytes 442372
  248.2 2.8 %copy-start = (bf16[2,4,256,768]{3,2,1,0:T(8,128)(2,1)S(1)}, bf16[2,4,256,768]{3,2,1,0:T(8,128)(2,1)}, u32[]{:S(2)}) copy-start(bf16[2,4,256,768]{3,2,1,0:T(8,128)(2,1)} %get-tuple-element.21) | copy-start | bytes 9437188
  251.0 1.7 copy-start.6
  251.0 2.3 copy-start.5

commit v7 on v6

--- a/solution.py
+++ b/solution.py
@@ -536,8 +536,10 @@
 
 
 def layer_kernel(*refs):
-    inputs, cotangent, flags, maps, norms = refs[:5]
-    shards = refs[5:9]
+    inputs, cotangent, starts, own_maps_in = *refs[:3], refs[3:5]
+    norms_in, shards, down = refs[5:9], refs[9:12], refs[12]
+    flags, maps, norms = refs[-3:]
+    refs = refs[4:-3]
     all_out, all_in = refs[9:11]
     outs, maps_out, norms_out = refs[11:15], refs[15:17], refs[17]
     w, mx, nrm, x, g, n1, qkv, feat = refs[18:22], *refs[22:29]
@@ -553,6 +555,7 @@
     d = x.shape[1]
     ff = a.shape[1]
     half_rows = x.shape[0] // 2
+    shards = (*shards, gm.at[pl.ds(0, d // 2)])
     f, c, t = whereabouts()
     n = c * 4 + t
     peers = neighbours(f, c, t)
@@ -598,10 +601,21 @@
     def norm_place(ff_):
         return nrm.at[:, at(ff_ * lo_norm, lo_norm, 128)]
 
+    for side in range(2):
+        own_map = own_maps_in[side][...]
+        maps[side] = jnp.concatenate([own_map, -own_map], -1)
+    norms[...] = jnp.zeros_like(norms)
+    for i in range(4):
+        norms[i : i + 1, :] = norms_in[i][...].astype(f32).reshape(1, -1)
     fetched.append(fetch(maps, map_place(f, t), local_sem.at[4]))
     fetched.append(fetch(norms, norm_place(f), local_sem.at[5]))
-    shard_copies = [fetch(of(shards, m), shard(of(w, m), m, f, t), local_sem.at[6 + m]) for m in range(5)]
+    shard_copies = {m: fetch(of(shards, m), shard(of(w, m), m, f, t), local_sem.at[6 + m]) for m in (0, 4, 1, 2)}
+    down_rows = turned.at[:, pl.ds(0, d // 2)]
+    down_copy = fetch(down, down_rows, local_sem.at[11])
     z_buf[...] = jnp.zeros_like(z_buf)
+    for b in range(2):
+        hits = jnp.where(starts[b] == n * BLK, 1.0, 0.0)
+        flags[b] = jnp.broadcast_to(jnp.max(hits, -1, keepdims=True), flags.shape[1:])
     small[...] = jnp.zeros_like(small)
     vec[...] = jnp.zeros_like(vec)
     meet(f, c, t)
@@ -609,6 +623,11 @@
     put(norms, norm_place(f), extra_sem.at[0], partner)
     put(maps, map_place(f, t), extra_sem.at[4], partner)
     for m in GROUPS:
+        if m == 3:
+            down_copy.wait()
+            for i in range(0, ff // 4, 256):
+                gm[0 : d // 2, i : i + 256] = turned[i : i + 256, 0 : d // 2].astype(f32).T.astype(bf16)
+            shard_copies[3] = fetch(shards[3], shard(w[3], 3, f, t), local_sem.at[9])
         for k, pred in ((2, None), (1, t != 3), (3, t != 0)):
             src, dst = quarter(of(shards, m), m, c), piece(of(w, m), m, f, c, t)
             peer = (f, c, lax.rem(t + k, 4))
@@ -1431,13 +1450,6 @@
     ff = up_weight.shape[1] * 4
     heads = query_map.shape[0] * 4
     head = query_map.shape[2]
-    own_block = lax.axis_index("context") * 4 + lax.axis_index("tensor")
-    flags = jnp.any(picture_starts.reshape(micro, -1) // BLK == own_block, 1).astype(f32)
-    flags = jnp.broadcast_to(flags[:, None, None], (micro, 8, span))
-    maps = jnp.stack([query_map, key_map])
-    maps = jnp.concatenate([maps, -maps], -1)
-    norms = jnp.stack([first_gain, first_bias, second_gain, second_bias]).astype(f32)
-    norms = jnp.concatenate([norms, jnp.zeros_like(norms)])
     dma = pltpu.SemaphoreType.DMA
     own = [(3, 4, d // 4, d // 2), (4, d // 4, d // 2), (d // 2, ff), (d // 2, ff)]
     sums = [(3, 4, d // 16, d // 2), (4, d // 16, d // 2), (d // 8, ff), (d // 8, ff)]
@@ -1469,6 +1481,9 @@
     scratch += [pltpu.VMEM(s, f32) for s in ((8, d), (8, d // 2), (8, d // 2), (4, 8, d // 2), (8, d // 2), (4, 8, d // 2))]
     scratch += [dma((16,)), dma(()), dma((8,)), dma((5, 4)), dma((5, 4, 4)), dma((5,))]
     scratch += [dma((8,)), dma((2, 2, 3, 2, 2)), dma((5,)), dma((5, 2, 3)), dma((5, 6)), dma((5, 4)), dma((6,))]
+    scratch += [pltpu.VMEM((micro, 8, span), f32), pltpu.VMEM((2, heads // 4, head // 2, 128), bf16)]
+    scratch += [pltpu.VMEM((8, d // 2), f32)]
+    vmem = pl.BlockSpec(memory_space=pltpu.VMEM)
     spread_rows = (micro, 4, span, d)
     anywhere = pl.BlockSpec(memory_space=pl.ANY)
     all_out, all_in, share_0, share_1, share_2, share_3, map_0, map_1, norm_grads = pl.pallas_call(
@@ -1477,12 +1492,15 @@
         + [jax.ShapeDtypeStruct(s, bf16) for s in outs]
         + [jax.ShapeDtypeStruct(maps_shape, f32)] * 2
         + [jax.ShapeDtypeStruct((8, d // 2), f32)],
-        in_specs=[anywhere] * 2 + [pl.BlockSpec(memory_space=pltpu.VMEM)] + [anywhere] * 6,
-        out_specs=[anywhere] * 6 + [pl.BlockSpec(memory_space=pltpu.VMEM)] * 3,
+        in_specs=[anywhere] * 2 + [vmem] * 7 + [anywhere] * 4,
+        out_specs=[anywhere] * 6 + [vmem] * 3,
         scratch_shapes=scratch,
         compiler_params=pltpu.CompilerParams(collective_id=0, has_side_effects=True, vmem_limit_bytes=67043328),
         name="layer",
-    )(inputs, cotangent, flags, maps, norms, qkv_weight.transpose(0, 2, 1), out_weight, up_weight, down_weight.T)
+    )(
+        inputs, cotangent, picture_starts, query_map, key_map, first_gain, first_bias, second_gain, second_bias,
+        qkv_weight.transpose(0, 2, 1), out_weight, up_weight, down_weight,
+    )
     return (
         all_out.reshape(inputs.shape),
         all_in.reshape(inputs.shape).astype(f32),

time: 254 us -> 245 us (0.965)
  local copies, waits for them, and re-layouts: 11.3 us -> 5.78 us
  other arithmetic: 11.7 us -> 8.01 us
    another operation x4 -> x0, local copies, waits for them, and re-layouts: 2.73 us -> none  [mesh_device(): jnp.stack([first_gain, first_bias, second_gain, second_bias]).astype(f32)]
    unnamed x19 -> x18, local copies, waits for them, and re-layouts: 6.43 us -> 4.31 us
where the time goes in v7:
time: 245 us
  Pallas kernels  231 us (94%)
  other arithmetic  8.01 us (3%)
  local copies, waits for them, and re-layouts  5.78 us (2%)
    pallas_call x1, Pallas kernels, mesh_device(): pl.pallas_call(layer_kernel, out_shape=[jax.ShapeDtypeStruct(spread_rows,...  231 us
    unnamed x1, other arithmetic  5.14 us

profile of v7, /device:TPU:0, one launch (start us, length us, event | category | flops | bytes accessed | tf_op | source)
XLA Modules:
  0.0 245.0 jit_solution(2290739069099038756)
XLA Ops:
  0.6 230.5 %layer.1 = (bf16[2,4,256,768]{3,2,1,0:T(8,128)(2,1)}, bf16[2,4,256,768]{3,2,1,0:T(8,128)(2,1)}, bf16[3,192,384]{2,1,0:T(8,128)(2,1)}, bf16[192,384]{1,0:T(8,128)...) custom-call(bf16[2,1,1024,768]{3,2,1,0:T(8,128)(2,1)} %refs_0_.1, ...), custom_call_target="tpu_custom_call" | custom-call | tf_op jit(solution)/shard_map/layer/pallas_call | solution.py:1489
  231.2 1.5 slice_reduce_fusion
  232.7 0.0 copy-start.2
  232.7 5.1 %bitcast_convert_fusion = f32[2,1,1024,768]{3,2,1,0:T(8,128)} fusion(bf16[2,1,1024,768]{3,2,1,0:T(8,128)(2,1)} %bitcast.16), kind=kLoop, calls=%fused_computation | loop fusion | flops 1572864 | bytes 9437184
  237.8 0.0 copy-start.1
  237.8 0.0 copy-start.3
  237.8 0.0 copy-done.2
  237.8 0.1 convert_bitcast_fusion
  237.9 0.0 copy-start.4
  237.9 1.4 copy.27
  239.3 0.0 copy-start
  239.3 0.0 copy-done.1
  239.3 1.1 convert_element_type.25
  240.4 0.0 copy-done.3
  240.4 1.0 convert_bitcast_fusion.1
  241.4 0.0 copy-done.4
  241.4 0.7 convert_element_type.24
  242.1 0.0 copy-done
  242.1 0.0 copy-start.6
  242.1 0.0 copy-start.5
  242.1 1.7 copy.31
  243.8 0.0 copy-done.6
  243.8 0.6 copy.32
  244.4 0.0 copy-done.5
  244.4 0.6 copy.33
Async XLA Ops:
  232.7 5.2 %copy-start.2 = (bf16[384,768]{1,0:T(8,128)(2,1)S(1)}, bf16[384,768]{1,0:T(8,128)(2,1)}, u32[]{:S(2)}) copy-start(bf16[384,768]{1,0:T(8,128)(2,1)} %get-tuple-element.26) | copy-start | bytes 1769476
  237.8 1.5 copy-start.1
  237.8 2.6 %copy-start.3 = (bf16[3,192,384]{2,1,0:T(8,128)(2,1)S(1)}, bf16[3,192,384]{2,1,0:T(8,128)(2,1)}, u32[]{:S(2)}) copy-start(bf16[3,192,384]{2,1,0:T(8,128)(2,1)} %get-tuple-element.23) | copy-start | bytes 1327108
  237.9 3.5 %copy-start.4 = (bf16[192,384]{1,0:T(8,128)(2,1)S(1)}, bf16[192,384]{1,0:T(8,128)(2,1)}, u32[]{:S(2)}) copy-start(bf16[192,384]{1,0:T(8,128)(2,1)} %get-tuple-element.24) | copy-start | bytes 442372
  239.3 2.8 %copy-start = (bf16[2,4,256,768]{3,2,1,0:T(8,128)(2,1)S(1)}, bf16[2,4,256,768]{3,2,1,0:T(8,128)(2,1)}, u32[]{:S(2)}) copy-start(bf16[2,4,256,768]{3,2,1,0:T(8,128)(2,1)} %get-tuple-element.21) | copy-start | bytes 9437188
  242.1 1.7 copy-start.6
  242.1 2.3 copy-start.5

commit v8 on v7

--- a/solution.py
+++ b/solution.py
@@ -694,6 +694,13 @@
         e, _unused = statistics(x[rows, :].astype(f32))
         n1[rows, :] = (e * nrm[0:1, :] + nrm[1:2, :]).astype(bf16)
 
+    def turn(src):
+        @pl.loop(0, d // 256)
+        def _(i):
+            cols = at(i * 256, 256, 128)
+            turned[at(i * 256, 256, 16), :] = src[:, cols].astype(f32).T.astype(bf16)
+
+    turn(g)
     take_maps()
     for k in (2, 1, 3):
         relay(0, k)
@@ -1121,14 +1128,6 @@
         cols = at(i * 256, 256, 128)
         gp[:, cols] = (mm(g[...], wd[:, cols]) * gp[:, cols].astype(f32)).astype(bf16)
 
-    def turn(src):
-        @pl.loop(0, chunks)
-        def _(i):
-            cols = at(i * 256, 256, 128)
-            turned[at(i * 256, 256, 16), :] = src[:, cols].astype(f32).T.astype(bf16)
-
-    turn(g)
-
     @pl.loop(0, ff // 256)
     def _(i):
         cols = at(i * 256, 256, 128)
@@ -1361,6 +1360,7 @@
     rows_hop(1, 0, 1)
     grad_last(3)
     grad_xy(0)
+    rows_hop(1, 1, 1)
     grad_chain(2, 1)
     grad_z(1)
     grad_z(4)
@@ -1382,16 +1382,15 @@
         fetch(small_sum, small_all.at[c], local_sem.at[6]),
         fetch(vec_sum, vec_all.at[c], local_sem.at[7]),
     ]
-    rows_hop(1, 1, 1)
     grad_chain(2, 2)
     grad_chain(1, 1)
     grad_chain(4, 1)
     grad_mid(0)
+    rows_hop(1, 0, 2)
     grad_last(2)
     grad_chain(1, 2)
     grad_chain(4, 2)
     grad_z(0)
-    rows_hop(1, 0, 2)
     for copy in own_small:
         copy.wait()
     arrived(small_all.at[pl.ds(0, 3)], small_sem.at[4])

time: 245 us -> 245 us (level)
  no operation moved by 1% of the time
where the time goes in v8:
time: 245 us
  Pallas kernels  231 us (94%)
  other arithmetic  8.01 us (3%)
  local copies, waits for them, and re-layouts  5.78 us (2%)
    pallas_call x1, Pallas kernels, mesh_device(): pl.pallas_call(layer_kernel, out_shape=[jax.ShapeDtypeStruct(spread_rows,...  231 us
    unnamed x1, other arithmetic  5.14 us

profile of v8, /device:TPU:0, one launch (start us, length us, event | category | flops | bytes accessed | tf_op | source)
XLA Modules:
  0.0 245.0 jit_solution(18202616718830525453)
XLA Ops:
  0.6 230.5 %layer.1 = (bf16[2,4,256,768]{3,2,1,0:T(8,128)(2,1)}, bf16[2,4,256,768]{3,2,1,0:T(8,128)(2,1)}, bf16[3,192,384]{2,1,0:T(8,128)(2,1)}, bf16[192,384]{1,0:T(8,128)...) custom-call(bf16[2,1,1024,768]{3,2,1,0:T(8,128)(2,1)} %refs_0_.1, ...), custom_call_target="tpu_custom_call" | custom-call | tf_op jit(solution)/shard_map/layer/pallas_call | solution.py:1488
  231.2 1.5 slice_reduce_fusion
  232.7 0.0 copy-start.2
  232.7 5.1 %bitcast_convert_fusion = f32[2,1,1024,768]{3,2,1,0:T(8,128)} fusion(bf16[2,1,1024,768]{3,2,1,0:T(8,128)(2,1)} %bitcast.16), kind=kLoop, calls=%fused_computation | loop fusion | flops 1572864 | bytes 9437184
  237.8 0.0 copy-start.1
  237.8 0.0 copy-start.3
  237.8 0.0 copy-done.2
  237.8 0.1 convert_bitcast_fusion
  237.9 0.0 copy-start.4
  237.9 1.4 copy.27
  239.3 0.0 copy-start
  239.3 0.0 copy-done.1
  239.3 1.1 convert_element_type.25
  240.4 0.0 copy-done.3
  240.4 1.0 convert_bitcast_fusion.1
  241.4 0.0 copy-done.4
  241.4 0.7 convert_element_type.24
  242.1 0.0 copy-done
  242.1 0.0 copy-start.6
  242.1 0.0 copy-start.5
  242.1 1.7 copy.31
  243.8 0.0 copy-done.6
  243.8 0.6 copy.32
  244.4 0.0 copy-done.5
  244.4 0.6 copy.33
Async XLA Ops:
  232.7 5.2 %copy-start.2 = (bf16[384,768]{1,0:T(8,128)(2,1)S(1)}, bf16[384,768]{1,0:T(8,128)(2,1)}, u32[]{:S(2)}) copy-start(bf16[384,768]{1,0:T(8,128)(2,1)} %get-tuple-element.26) | copy-start | bytes 1769476
  237.8 1.5 copy-start.1
  237.8 2.6 %copy-start.3 = (bf16[3,192,384]{2,1,0:T(8,128)(2,1)S(1)}, bf16[3,192,384]{2,1,0:T(8,128)(2,1)}, u32[]{:S(2)}) copy-start(bf16[3,192,384]{2,1,0:T(8,128)(2,1)} %get-tuple-element.23) | copy-start | bytes 1327108
  237.9 3.5 %copy-start.4 = (bf16[192,384]{1,0:T(8,128)(2,1)S(1)}, bf16[192,384]{1,0:T(8,128)(2,1)}, u32[]{:S(2)}) copy-start(bf16[192,384]{1,0:T(8,128)(2,1)} %get-tuple-element.24) | copy-start | bytes 442372
  239.3 2.8 %copy-start = (bf16[2,4,256,768]{3,2,1,0:T(8,128)(2,1)S(1)}, bf16[2,4,256,768]{3,2,1,0:T(8,128)(2,1)}, u32[]{:S(2)}) copy-start(bf16[2,4,256,768]{3,2,1,0:T(8,128)(2,1)} %get-tuple-element.21) | copy-start | bytes 9437188
  242.1 1.7 copy-start.6
  242.1 2.3 copy-start.5
